TPU v7x, 32 devices: a whole 2x2x4 slice. The times are simulated.
32 devices in a mesh: seq: 16 (over z, x, core), fsdp: 2 (over y).
Axes of the slice: x: 2, y: 2, z: 4, core: 2. Of those that a mesh axis runs over, the one named last changes fastest.
Arguments:
- activations: bfloat16 [65536, 2048], P('seq', 'fsdp'), may hold values from -3 to 3
- mix_first: bfloat16 [256, 256], replicated, may hold values from -0.375 to 0.375
- twiddle: float32 [256, 256], P('seq'), may hold values from 0.4 to 2
- mix_second: bfloat16 [256, 256], replicated, may hold values from -0.375 to 0.375
- up_first: bfloat16 [8, 256, 256], P('fsdp'), may hold values from -0.375 to 0.375
- up_second: bfloat16 [8, 256, 1024], P('fsdp'), may hold values from -0.375 to 0.375
- down_first: bfloat16 [8, 1024, 256], P('fsdp'), may hold values from -0.1875 to 0.1875
- down_second: bfloat16 [8, 256, 256], P('fsdp'), may hold values from -0.375 to 0.375
- grad_out: bfloat16 [65536, 2048], P('seq', 'fsdp'), may hold values from -3 to 3
Outputs:
- output: bfloat16 [65536, 2048], P('seq', 'fsdp')
- grad_inputs: bfloat16 [65536, 2048], P('seq', 'fsdp')
- grad_up_first: float32 [8, 256, 256], P('fsdp')
- grad_up_second: float32 [8, 256, 1024], P('fsdp')
- grad_down_first: float32 [8, 1024, 256], P('fsdp')
- grad_down_second: float32 [8, 256, 256], P('fsdp')
All inputs are finite; a program needn't handle non-finite values.
Results may differ from a plain program's by a relative error of at most 0.01.
Values may be sent and summed in bfloat16 or wider, within the bound.
No kernel may reach another device: no remote copies, remote signals or barrier semaphores. Data moves between devices by JAX's collectives and lax.ppermute only.
A program may use at most 320 MiB of HBM per device.

v0:
```python
import jax
import jax.numpy as jnp
from jax import lax
from jax.sharding import PartitionSpec as P

NBLK = 8


root_two_pi = 0.7978845608028654
cubic_term = 0.044715


def gelu_value(values):
    inner = root_two_pi * (values + cubic_term * values * values * values)
    return 0.5 * values * (1.0 + jnp.tanh(inner))


def gelu_slope(values):
    inner = root_two_pi * (values + cubic_term * values * values * values)
    hyper = jnp.tanh(inner)
    return 0.5 * (1.0 + hyper) + 0.5 * values * (1.0 - hyper * hyper) * root_two_pi * (
        1.0 + 3.0 * cubic_term * values * values
    )


def product(form, left, right):
    return jnp.einsum(form, left, right, preferred_element_type=jnp.float32)


def column_pass(field, factor):
    result = product(
        "ajc,ai->ijc", lax.all_to_all(field, "seq", split_axis=1, concat_axis=0, tiled=True), factor
    ).astype(jnp.bfloat16)
    return lax.all_to_all(result, "seq", split_axis=0, concat_axis=1, tiled=True)


def shuffle_blocks(values):
    return lax.all_to_all(values, "fsdp", split_axis=2, concat_axis=1, tiled=True)


def spread_blocks(values):
    count, local_blocks, width = values.shape
    stride = width // NBLK
    received = shuffle_blocks(values)
    shaped = received.reshape(count, NBLK, local_blocks, stride)
    return jnp.transpose(shaped, (0, 2, 3, 1)).reshape(count, local_blocks, width)


def return_blocks(values):
    count, local_blocks, width = values.shape
    stride = width // NBLK
    parts = NBLK // local_blocks
    shaped = values.reshape(count, local_blocks, stride, parts, local_blocks)
    sending = jnp.transpose(shaped, (0, 1, 3, 4, 2)).reshape(count, local_blocks, width)
    received = shuffle_blocks(sending).reshape(count, NBLK, local_blocks, stride)
    return jnp.transpose(received, (0, 2, 1, 3)).reshape(count, local_blocks, width)


def blocks_layer(hidden, grad_out, up_first, up_second, down_first, down_second):
    count, channels = hidden.shape
    local_blocks, width = (up_first.shape[0], up_first.shape[1])
    hidden_three = hidden.reshape(count, local_blocks, width)
    up_mid = product("tkp,kpq->tkq", hidden_three, up_first).astype(jnp.bfloat16)
    up_perm = spread_blocks(up_mid)
    pre_act = product("tge,geo->tgo", up_perm, up_second)
    activated = gelu_value(pre_act).astype(jnp.bfloat16)
    down_mid = product("tgo,goq->tgq", activated, down_first).astype(jnp.bfloat16)
    down_perm = spread_blocks(down_mid)
    down_out = product("tge,geq->tgq", down_perm, down_second).reshape(count, channels)
    output = (hidden.astype(jnp.float32) + down_out).astype(jnp.bfloat16)
    grad_three = grad_out.reshape(count, local_blocks, width)
    sum_down_second = product("tge,tgq->geq", down_perm, grad_three)
    back_perm = product("tgq,geq->tge", grad_three, down_second).astype(jnp.bfloat16)
    back_mid = return_blocks(back_perm)
    sum_down_first = product("tgo,tgq->goq", activated, back_mid)
    grad_act = product("tgq,goq->tgo", back_mid, down_first)
    grad_pre = (grad_act * gelu_slope(pre_act)).astype(jnp.bfloat16)
    sum_up_second = product("tge,tgo->geo", up_perm, grad_pre)
    grad_perm = product("tgo,geo->tge", grad_pre, up_second).astype(jnp.bfloat16)
    grad_mid = return_blocks(grad_perm)
    sum_up_first = product("tkp,tkq->kpq", hidden_three, grad_mid)
    grad_inner = product("tkq,kpq->tkp", grad_mid, up_first).reshape(count, channels)
    grad_hidden = (grad_out.astype(jnp.float32) + grad_inner).astype(jnp.bfloat16)
    return (output, grad_hidden, (sum_up_first, sum_up_second, sum_down_first, sum_down_second))


def shards(
    activations,
    mix_first,
    twiddle,
    mix_second,
    up_first,
    up_second,
    down_first,
    down_second,
    grad_out,
):
    local_rows, local_channels = activations.shape
    block_rows = twiddle.shape[0]
    length = mix_first.shape[0]
    inputs_three = activations.reshape(block_rows, length, local_channels)
    first_pass = (product("abc,bj->ajc", inputs_three, mix_first) * twiddle[:, :, None]).astype(
        jnp.bfloat16
    )
    mixed = column_pass(first_pass, mix_second).reshape(local_rows, local_channels)
    inputs_float = activations.astype(jnp.float32)
    gating = jax.nn.sigmoid(inputs_float)
    mixed_float = mixed.astype(jnp.float32)
    hidden = (inputs_float + gating * mixed_float).astype(jnp.bfloat16)
    output, grad_hidden, grads = blocks_layer(
        hidden, grad_out, up_first, up_second, down_first, down_second
    )
    totals = lax.psum((grads[0], grads[1], grads[2], grads[3]), "seq")
    grad_float = grad_hidden.astype(jnp.float32)
    grad_mixed = (grad_float * gating).astype(jnp.bfloat16)
    back_rows = column_pass(grad_mixed.reshape(block_rows, length, local_channels), mix_second.T)
    twisted = (back_rows.astype(jnp.float32) * twiddle[:, :, None]).astype(jnp.bfloat16)
    mix_grad = product("ajc,bj->abc", twisted, mix_first).reshape(local_rows, local_channels)
    grad_inputs = (grad_float * (1.0 + gating * (1.0 - gating) * mixed_float) + mix_grad).astype(
        jnp.bfloat16
    )
    scale = 1.0 / length
    return (
        output,
        grad_inputs,
        totals[0] * scale,
        totals[1] * scale,
        totals[2] * scale,
        totals[3] * scale,
    )


def solution(mesh):
    in_specs = (
        P("seq", "fsdp"),
        P(),
        P("seq", None),
        P(),
        P("fsdp", None, None),
        P("fsdp", None, None),
        P("fsdp", None, None),
        P("fsdp", None, None),
        P("seq", "fsdp"),
    )
    out_specs = (
        P("seq", "fsdp"),
        P("seq", "fsdp"),
        P("fsdp", None, None),
        P("fsdp", None, None),
        P("fsdp", None, None),
        P("fsdp", None, None),
    )
    return jax.shard_map(shards, mesh=mesh, in_specs=in_specs, out_specs=out_specs, check_vma=False)
```

profile of v0, /device:TPU:0, one launch (start us, length us, event | category | flops | bytes accessed | tf_op | source)
XLA Modules:
  0.0 1738.0 jit_solution(1957139552533190147)
XLA Ops:
  28.0 189.5 %all_to_all.114 = bf16[16,256,1024]{2,0,1:T(8,128)(2,1)} all-to-all(bf16[16,256,1024]{2,0,1:T(8,128)(2,1)} %copy.130), channel_id=1, replica_groups=mesh['seq'=16,'fsdp'=2] {'seq'}, dimensions={1} | all-to-all | bytes 16777216 | tf_op jit(solution)/shard_map/all_to_all | solution.py:32
  230.3 17.0 convert_bitcast_fusion.7
  311.6 104.5 %all-to-all-done.1 = bf16[256,16,1024]{2,1,0:T(8,128)(2,1)} async-done(((bf16[256,16,1024]{2,1,0:T(8,128)(2,1)}), bf16[256,16,1024]{2,1,0:T(8,128)(2,1)}, u32[]{:S(2)}, u32[]{:S(2)}) %all-to-all-start.1) | async-done | bytes 8388640 | tf_op jit(solution)/shard_map/all_to_all | solution.py:34
  492.7 24.1 %all-to-all-done.4 = bf16[4096,4,256]{0,1,2:T(4,128)(2,1)} async-done(((bf16[4096,4,256]{0,1,2:T(4,128)(2,1)}), bf16[4096,4,256]{0,1,2:T(4,128)(2,1)}, u32[]{:S(2)}, u32[]{:S(2)}) %all-to-all-start.4) | async-done | bytes 8388640 | tf_op jit(solution)/shard_map/all_to_all | solution.py:38
  550.8 66.1 %all-to-all-done.2 = bf16[4096,4,256]{0,1,2:T(4,128)(2,1)} async-done(((bf16[4096,4,256]{0,1,2:T(4,128)(2,1)}), bf16[4096,4,256]{0,1,2:T(4,128)(2,1)}, u32[]{:S(2)}, u32[]{:S(2)}) %all-to-all-start.2) | async-done | bytes 8388640 | tf_op jit(solution)/shard_map/all_to_all | solution.py:38
  635.9 48.6 %multiply_convert_fusion = (bf16[4096,4,1024]{2,0,1:T(8,128)(2,1)}, f32[4,4096,1024]{2,1,0:T(8,128)}) fusion(bf16[4,256,1024]{2,1,0:T(8,128)(2,1)S(1)} %copy-done, bf16[4096,4,32,8]{0,2,1,3:T(8,128)(2,1)} %bitcast.185), kind=kOutput, calls=%fused_computation.10 | convolution fusion | flops 8740929536 | bytes 111149056 | tf_op jit(solution)/shard_map/tge,geo->tgo/dot_general | solution.py:27
  684.5 53.2 %fusion.6 = bf16[4096,4,1024]{2,0,1:T(8,128)(2,1)} fusion(f32[4,4096,1024]{2,1,0:T(8,128)} %get-tuple-element.11, bf16[4096,4,256]{0,2,1:T(8,128)(2,1)} %bitcast.183, bf16[4,1024,256]{2,1,0:T(8,128)(2,1)} %param.15), kind=kOutput, calls=%fused_computation.8 | convolution fusion | flops 8908701696 | bytes 111149056 | tf_op jit(solution)/shard_map/tgq,goq->tgo/dot_general | solution.py:27
  737.7 19.0 %convert_bitcast_fusion.3 = bf16[4096,4,256]{0,2,1:T(8,128)(2,1)} fusion(bf16[4096,4,1024]{2,0,1:T(8,128)(2,1)} %fusion.6, bf16[4,256,1024]{2,1,0:T(8,128)(2,1)S(1)} %copy-done), kind=kOutput, calls=%fused_computation.50 | convolution fusion | flops 8594128896 | bytes 44040192 | tf_op jit(solution)/shard_map/tgo,geo->tge/dot_general | solution.py:27
  791.4 96.6 %all_to_all.115 = bf16[4096,4,256]{0,1,2:T(4,128)(2,1)} all-to-all(bf16[4096,4,256]{0,1,2:T(4,128)(2,1)S(1)} %copy.157), channel_id=1, replica_groups=mesh['seq'=16,'fsdp'=2] {'fsdp'}, dimensions={2} | all-to-all | bytes 16777216 | tf_op jit(solution)/shard_map/all_to_all | solution.py:38
  926.3 17.4 %copy.162 = f32[4096,1024]{1,0:T(8,128)} copy(f32[4096,1024]{0,1:T(8,128)} %bitcast.164) | data formatting | bytes 33554432 | tf_op jit(solution)/shard_map/reshape | solution.py:82
  943.8 15.4 fusion.13
  970.5 35.0 %all-to-all-start.6 = ((bf16[16,256,1024]{2,0,1:T(8,128)(2,1)}), bf16[16,256,1024]{2,0,1:T(8,128)(2,1)}, u32[]{:S(2)}, u32[]{:S(2)}) async-start(bf16[16,256,1024]{2,0,1:T(8,128)(2,1)} %copy.163), calls=%async_computation.6 | async-start | bytes 16777216 | tf_op jit(solution)/shard_map/all_to_all | solution.py:32
  1005.5 17.1 convert_bitcast_fusion.5
  1022.6 14.6 copy.142
  1037.2 118.8 %all-to-all-done.6 = bf16[16,256,1024]{2,0,1:T(8,128)(2,1)} async-done(((bf16[16,256,1024]{2,0,1:T(8,128)(2,1)}), bf16[16,256,1024]{2,0,1:T(8,128)(2,1)}, u32[]{:S(2)}, u32[]{:S(2)}) %all-to-all-start.6) | async-done | bytes 8388640 | tf_op jit(solution)/shard_map/all_to_all | solution.py:32
  1176.0 23.3 %convert_bitcast_fusion.2 = bf16[256,16,1024]{0,2,1:T(8,128)(2,1)} fusion(bf16[256,16,1024]{2,1,0:T(8,128)(2,1)} %bitcast.162, bf16[256,256]{1,0:T(8,128)(2,1)S(1)} %copy-done.10), kind=kOutput, calls=%fused_computation.49 | convolution fusion | flops 2151677952 | bytes 16908288 | tf_op jit(solution)/shard_map/ajc,ai->ijc/dot_general | solution.py:27
  1211.7 45.2 %all-to-all-done.3 = bf16[4096,4,256]{0,1,2:T(4,128)(2,1)} async-done(((bf16[4096,4,256]{0,1,2:T(4,128)(2,1)}), bf16[4096,4,256]{0,1,2:T(4,128)(2,1)}, u32[]{:S(2)}, u32[]{:S(2)}) %all-to-all-start.3) | async-done | bytes 8388640 | tf_op jit(solution)/shard_map/all_to_all | solution.py:38
  1256.9 36.0 %all-to-all-start.7 = ((bf16[256,16,1024]{2,1,0:T(8,128)(2,1)}), bf16[256,16,1024]{2,1,0:T(8,128)(2,1)}, u32[]{:S(2)}, u32[]{:S(2)}) async-start(bf16[256,16,1024]{2,1,0:T(8,128)(2,1)} %copy.167), calls=%async_computation.7 | async-start | bytes 16777216 | tf_op jit(solution)/shard_map/all_to_all | solution.py:34
  1293.3 20.5 %fusion.51 = f32[4,1024,256]{2,1,0:T(8,128)} fusion(bf16[4096,4,1024]{2,0,1:T(8,128)(2,1)} %get-tuple-element.10, bf16[4096,4,256]{0,2,1:T(8,128)(2,1)} %bitcast.184), kind=kOutput, calls=%fused_computation.71 | convolution fusion | flops 8589934592 | bytes 46137344 | tf_op jit(solution)/shard_map/tgo,tgq->goq/dot_general | solution.py:27
  1313.9 26.3 %fusion.25 = f32[4,256,1024]{2,1,0:T(8,128)} fusion(bf16[4096,4,1024]{2,0,1:T(8,128)(2,1)} %fusion.6, bf16[4096,4,32,8]{0,2,1,3:T(8,128)(2,1)} %bitcast.186), kind=kOutput, calls=%fused_computation.41 | convolution fusion | flops 8589934592 | bytes 46137344 | tf_op jit(solution)/shard_map/tge,tgo->geo/dot_general | solution.py:27
  1379.6 15.1 fusion.23
  1394.7 17.5 %copy.148 = f32[4096,1024]{1,0:T(8,128)} copy(f32[4096,1024]{0,1:T(8,128)} %bitcast.163) | data formatting | bytes 33554432 | tf_op jit(solution)/shard_map/reshape | solution.py:69
  1424.3 243.4 %all-reduce.3.cloned.1.call-done = (f32[4,256,256]{2,1,0:T(8,128)}, f32[4,256,1024]{2,1,0:T(8,128)}, f32[4,1024,256]{2,1,0:T(8,128)}, f32[4,256,256]{2,1,0:T(8,128)}) async-done(((f32[4,256,256]{2,1,0:T(8,128)}, f32[4,256,1024]{2,1,0:T(8,128)}, f32[4,1024,256]{2,1,0:T(8,128)}, f32[4,256,256]{2,1,0:T(8,128)}), (f32[4,256,256]{2,1,0:T(8,128)}, f32[4,256,1024]{2,1,0:T(8,128)}, f32[4,1024,256]{2,1,0:T(8,128)}, ...) | async-done | bytes 10485776 | tf_op jit(solution)/shard_map/psum | solution.py:113
  1707.0 23.6 %fusion.12 = bf16[4096,1024]{1,0:T(8,128)(2,1)} fusion(f32[16,1024,256]{1,2,0:T(8,128)} %fusion.47, f32[16,16,16,1024]{3,2,1,0:T(8,128)} %copy-done.2, bf16[4096,1024]{1,0:T(8,128)(2,1)S(1)} %bitcast.159, f32[4096,1024]{1,0:T(8,128)} %copy.162, bf16[4096,1024]{1,0:T(8,128)(2,1)} %param.17), kind=kLoop, calls=%fused_computation.21 | loop fusion | flops 62914560 | bytes 75497472 | tf_op jit(solution)/shard_map/convert_element_type | solution.py:119
  (89 shorter events, 435.3 us)
Async XLA Ops:
  7.2 628.7 %copy-start = (bf16[4,256,1024]{2,1,0:T(8,128)(2,1)S(1)}, bf16[4,256,1024]{2,1,0:T(8,128)(2,1)}, u32[]{:S(2)}) copy-start(bf16[4,256,1024]{2,1,0:T(8,128)(2,1)} %param.14) | copy-start | bytes 6291460
  217.4 12.9 copy-start.9
  259.6 5.9 copy-start.6
  259.6 156.5 %all-to-all-start.1 = ((bf16[256,16,1024]{2,1,0:T(8,128)(2,1)}), bf16[256,16,1024]{2,1,0:T(8,128)(2,1)}, u32[]{:S(2)}, u32[]{:S(2)}) async-start(bf16[256,16,1024]{2,1,0:T(8,128)(2,1)} %copy.134), calls=%async_computation.1 | async-start | bytes 16777216 | tf_op jit(solution)/shard_map/all_to_all | solution.py:34
  416.1 100.7 %all-to-all-start.4 = ((bf16[4096,4,256]{0,1,2:T(4,128)(2,1)}), bf16[4096,4,256]{0,1,2:T(4,128)(2,1)}, u32[]{:S(2)}, u32[]{:S(2)}) async-start(bf16[4096,4,256]{0,1,2:T(4,128)(2,1)} %copy.151), calls=%async_computation.4 | async-start | bytes 16777216 | tf_op jit(solution)/shard_map/all_to_all | solution.py:38
  423.0 24.6 %slice-start = ((s8[8388608]{0:T(1024)(128)(4,1)}), s8[4194304]{0:T(1024)(128)(4,1)S(1)}, s32[]{:S(2)}) async-start(s8[8388608]{0:T(1024)(128)(4,1)} %bitcast.156), calls=%async_computation.9 | async-start | bytes 8388608
  434.6 13.0 slice-start.1
  441.9 5.8 copy-start.2
  456.3 12.0 copy-start.4
  516.8 100.1 %all-to-all-start.2 = ((bf16[4096,4,256]{0,1,2:T(4,128)(2,1)}), bf16[4096,4,256]{0,1,2:T(4,128)(2,1)}, u32[]{:S(2)}, u32[]{:S(2)}) async-start(bf16[4096,4,256]{0,1,2:T(4,128)(2,1)} %copy.137), calls=%async_computation.2 | async-start | bytes 16777216 | tf_op jit(solution)/shard_map/all_to_all | solution.py:38
  907.0 7.8 copy-start.5
  970.5 35.0 %copy-start.12 = (bf16[4,1024,256]{2,1,0:T(8,128)(2,1)S(1)}, bf16[4,1024,256]{2,1,0:T(8,128)(2,1)}, u32[]{:S(2)}) copy-start(bf16[4,1024,256]{2,1,0:T(8,128)(2,1)} %param.15) | copy-start | bytes 6291460
  970.5 185.5 %all-to-all-start.6 = ((bf16[16,256,1024]{2,0,1:T(8,128)(2,1)}), bf16[16,256,1024]{2,0,1:T(8,128)(2,1)}, u32[]{:S(2)}, u32[]{:S(2)}) async-start(bf16[16,256,1024]{2,0,1:T(8,128)(2,1)} %copy.163), calls=%async_computation.6 | async-start | bytes 16777216 | tf_op jit(solution)/shard_map/all_to_all | solution.py:32
  1156.0 100.9 %all-to-all-start.3 = ((bf16[4096,4,256]{0,1,2:T(4,128)(2,1)}), bf16[4096,4,256]{0,1,2:T(4,128)(2,1)}, u32[]{:S(2)}, u32[]{:S(2)}) async-start(bf16[4096,4,256]{0,1,2:T(4,128)(2,1)} %copy.142), calls=%async_computation.3 | async-start | bytes 16777216 | tf_op jit(solution)/shard_map/all_to_all | solution.py:38
  1163.2 12.8 copy-start.10
  1256.9 421.4 %all-to-all-start.7 = ((bf16[256,16,1024]{2,1,0:T(8,128)(2,1)}), bf16[256,16,1024]{2,1,0:T(8,128)(2,1)}, u32[]{:S(2)}, u32[]{:S(2)}) async-start(bf16[256,16,1024]{2,1,0:T(8,128)(2,1)} %copy.167), calls=%async_computation.7 | async-start | bytes 16777216 | tf_op jit(solution)/shard_map/all_to_all | solution.py:34
  1292.9 374.7 %all-reduce.3.cloned.1.call-start = ((), (), s32[]{:S(2)}) async-start(), calls=%async_computation.8 | async-start | bytes 20971520 | tf_op jit(solution)/shard_map/psum | solution.py:113
  1351.5 20.1 %slice-start.4 = ((s8[8388608]{0:T(1024)(128)(4,1)}), s8[4194304]{0:T(1024)(128)(4,1)S(1)}, s32[]{:S(2)}) async-start(s8[8388608]{0:T(1024)(128)(4,1)} %bitcast.166), calls=%async_computation.13 | async-start | bytes 8388608
  1359.3 12.3 slice-start.5
  1667.6 8.3 copy-start.3
  1689.7 6.6 copy-start.11
  1696.3 10.7 slice-start.2
  1698.9 8.1 slice-start.3
  1707.0 23.6 %copy-start.1 = (bf16[4,256,1024]{2,1,0:T(8,128)(2,1)S(1)}, bf16[4,256,1024]{2,1,0:T(8,128)(2,1)}, u32[]{:S(2)}) copy-start(bf16[4,256,1024]{2,1,0:T(8,128)(2,1)} %param.14) | copy-start | bytes 6291460
  (2 other events, 3.7 us)
Sparse Core Ops, SparseCore 0:
  1378.7 288.8 all-reduce.2
where the time goes:
time: 1750 us; the launch traced here: 1740 us
  waiting for transfers between devices  602 us (34%)
  local copies, waits for them, and re-layouts  333 us (19%)
  matrix products  307 us (18%)
  blocking collectives  286 us (16%)
  starting transfers between devices  98.6 us (6%)
  other arithmetic  95.9 us (5%)
    dot_general x16, matrix products, product(): return jnp.einsum(form, left, right, preferred_element_type=jnp.float32)  307 us
    psum x1, waiting for transfers between devices, shards(): totals = lax.psum((grads[0], grads[1], grads[2], grads[3]), 'seq')  243 us
    all_to_all x1, blocking collectives, column_pass(): lax.all_to_all(field, 'seq', split_axis=1, concat_axis=0, tiled=True)  189 us
    all_to_all x3, waiting for transfers between devices, shuffle_blocks(): lax.all_to_all(values, 'fsdp', split_axis=2, concat_axis=1, tiled=True)  135 us
    all_to_all x1, waiting for transfers between devices, column_pass(): lax.all_to_all(field, 'seq', split_axis=1, concat_axis=0, tiled=True)  119 us
    all_to_all x2, waiting for transfers between devices, column_pass(): lax.all_to_all(result, 'seq', split_axis=0, concat_axis=1, tiled=True)  104 us
    all_to_all x1, blocking collectives, shuffle_blocks(): lax.all_to_all(values, 'fsdp', split_axis=2, concat_axis=1, tiled=True)  96.6 us
    all_to_all x8, local copies, waits for them, and re-layouts, shuffle_blocks(): lax.all_to_all(values, 'fsdp', split_axis=2, concat_axis=1, tiled=True)  76.1 us
  transfers between devices with their start and end apart: 7, of which 6 were waited for; matrix products, arithmetic and copies ran while one was open for 21% of the time, Pallas kernels for 0%

commit v1 on v0

--- a/solution.py
+++ b/solution.py
@@ -1,13 +1,23 @@
+import functools
+
 import jax
 import jax.numpy as jnp
 from jax import lax
+from jax.experimental import pallas as pl
+from jax.experimental.pallas import tpu as pltpu
 from jax.sharding import PartitionSpec as P
 
+
 NBLK = 8
+LANES = 128
+CHUNKS = 4
 
 
 root_two_pi = 0.7978845608028654
 cubic_term = 0.044715
+
+BF = jnp.bfloat16
+F32 = jnp.float32
 
 
 def gelu_value(values):
@@ -84,7 +94,7 @@
     return (output, grad_hidden, (sum_up_first, sum_up_second, sum_down_first, sum_down_second))
 
 
-def shards(
+def general_shards(
     activations,
     mix_first,
     twiddle,
@@ -130,6 +140,599 @@
     )
 
 
+def dot(left, right):
+    return jnp.dot(left, right, preferred_element_type=F32)
+
+
+def dot_nt(left, right):
+    return lax.dot_general(left, right, (((1,), (1,)), ((), ())), preferred_element_type=F32)
+
+
+def dot_tn(left, right):
+    return lax.dot_general(left, right, (((0,), (0,)), ((), ())), preferred_element_type=F32)
+
+
+def swap_rows(rows):
+    size = rows * rows
+    out = lax.broadcasted_iota(jnp.int32, (size, size), 0)
+    inp = lax.broadcasted_iota(jnp.int32, (size, size), 1)
+    same = (out // rows == inp % rows) & (out % rows == inp // rows)
+    return jnp.where(same, 1.0, 0.0).astype(BF)
+
+
+def swap_lanes(parts):
+    lane = lax.broadcasted_iota(jnp.int32, parts[0].shape, 1)
+    low = lane < 64
+    even = (lane & 32) == 0
+    x0, x1, x2, x3 = parts
+    a0 = jnp.where(low, x0, pltpu.roll(x2, 64, 1))
+    a2 = jnp.where(low, pltpu.roll(x0, 64, 1), x2)
+    a1 = jnp.where(low, x1, pltpu.roll(x3, 64, 1))
+    a3 = jnp.where(low, pltpu.roll(x1, 64, 1), x3)
+    b0 = jnp.where(even, a0, pltpu.roll(a1, 32, 1))
+    b1 = jnp.where(even, pltpu.roll(a0, 96, 1), a1)
+    b2 = jnp.where(even, a2, pltpu.roll(a3, 32, 1))
+    b3 = jnp.where(even, pltpu.roll(a2, 96, 1), a3)
+    return b0, b1, b2, b3
+
+
+def params(*semantics):
+    return pltpu.CompilerParams(
+        dimension_semantics=("arbitrary",) * len(semantics), vmem_limit_bytes=58 * 1024 * 1024
+    )
+
+
+def full(shape):
+    zeros = (0,) * len(shape)
+    return pl.BlockSpec(shape, lambda *_: zeros)
+
+
+def first_kernel(chunks, span, rows, x_ref, w_ref, tw_ref, *rest):
+    outs, scratch = rest[: len(chunks)], rest[len(chunks)]
+    swap = swap_rows(rows)
+    low, high = chunks[0] * span, (chunks[-1] + 1) * span
+    weight = w_ref[...].T[low:high, :]
+    scales = tw_ref[...].T[low:high, :]
+    for a in range(rows):
+        value = dot(weight, x_ref[a]) * scales[:, a : a + 1]
+        scratch[a] = value.astype(BF)
+    size = rows * rows
+    for n, out in enumerate(outs):
+        for group in range(span // rows):
+            start = n * span + group * rows
+            piece = scratch[:, start : start + rows, :].reshape(size, scratch.shape[2])
+            out[group * size : (group + 1) * size, :] = dot(swap, piece).astype(BF)
+
+
+def first_stage(chunks, x3, w1t, twt, cols=256):
+    rows, length, channels = x3.shape
+    span = length // CHUNKS
+    shape = jax.ShapeDtypeStruct((span * rows, channels), BF)
+    return pl.pallas_call(
+        functools.partial(first_kernel, chunks, span, rows),
+        grid=(channels // cols,),
+        in_specs=[
+            pl.BlockSpec((rows, length, cols), lambda c: (0, 0, c)),
+            full(w1t.shape),
+            full(twt.shape),
+        ],
+        out_specs=[pl.BlockSpec((span * rows, cols), lambda c: (0, c))] * len(chunks),
+        out_shape=[shape] * len(chunks),
+        scratch_shapes=[pltpu.VMEM((rows, span * len(chunks), cols), BF)],
+        compiler_params=params(0),
+        name="first",
+    )(x3, w1t, twt)
+
+
+def second_kernel(w_ref, x_ref, o_ref):
+    seq, own, rows, cols = x_ref.shape
+    weight = w_ref[...]
+    for j in range(own):
+        value = dot(weight, x_ref[:, j].reshape(seq * rows, cols))
+        o_ref[:, j] = value.astype(BF).reshape(seq, rows, cols)
+
+
+def second_stage(weight, field, seq, rows, cols=256):
+    total, channels = field.shape
+    own = total // (seq * rows)
+    four = field.reshape(seq, own, rows, channels)
+    spec = pl.BlockSpec((seq, own, rows, cols), lambda c: (0, 0, 0, c))
+    out = pl.pallas_call(
+        second_kernel,
+        grid=(channels // cols,),
+        in_specs=[full(weight.shape), spec],
+        out_specs=spec,
+        out_shape=jax.ShapeDtypeStruct(four.shape, BF),
+        compiler_params=params(0),
+        name="second",
+    )(weight, four)
+    return out.reshape(total, channels)
+
+
+def spread_store(values, own_ref, send_ref):
+    for half, ref in ((0, own_ref), (1, send_ref)):
+        parts = [v[:, half * LANES : (half + 1) * LANES] for v in values]
+        for g, part in enumerate(swap_lanes(parts)):
+            ref[g] = part.astype(BF)
+
+
+def gather_load(own_ref, recv_ref):
+    own = swap_lanes([own_ref[g].astype(F32) for g in range(own_ref.shape[0])])
+    recv = swap_lanes([recv_ref[g].astype(F32) for g in range(recv_ref.shape[0])])
+    return [jnp.concatenate([a, b], axis=1).astype(BF) for a, b in zip(own, recv)]
+
+
+def back_kernel(g_ref, w_ref, own_ref, send_ref):
+    rows, cols, channels = g_ref.shape
+    grad = g_ref[...].reshape(rows * cols, channels)
+    blocks, width = w_ref.shape[0], w_ref.shape[2]
+    values = [dot_nt(grad[:, h * width : (h + 1) * width], w_ref[h]) for h in range(blocks)]
+    spread_store(values, own_ref, send_ref)
+
+
+def back_stage(chunk, g3, down_second):
+    rows, length, channels = g3.shape
+    size = rows * rows
+    steps = length // CHUNKS // rows
+    blocks = down_second.shape[0]
+    shape = jax.ShapeDtypeStruct((blocks, steps * size, LANES), BF)
+    spec = pl.BlockSpec((blocks, size, LANES), lambda s: (0, s, 0))
+    return pl.pallas_call(
+        back_kernel,
+        grid=(steps,),
+        in_specs=[
+            pl.BlockSpec((rows, rows, channels), lambda s: (0, chunk * steps + s, 0)),
+            full(down_second.shape),
+        ],
+        out_specs=[spec, spec],
+        out_shape=[shape, shape],
+        compiler_params=params(0),
+        name="back",
+    )(g3, down_second)
+
+
+def hidden_kernel(x_ref, m_ref, w_ref, h_ref, own_ref, send_ref):
+    rows, cols, channels = x_ref.shape
+    mixed = dot(swap_rows(rows), m_ref[...])
+    inputs = x_ref[...].reshape(rows * cols, channels).astype(F32)
+    hidden = (inputs + jax.nn.sigmoid(inputs) * mixed).astype(BF)
+    h_ref[...] = hidden
+    blocks, width = w_ref.shape[0], w_ref.shape[1]
+    values = [dot(hidden[:, k * width : (k + 1) * width], w_ref[k]) for k in range(blocks)]
+    spread_store(values, own_ref, send_ref)
+
+
+def hidden_stage(chunk, x3, mixed, up_first):
+    rows, length, channels = x3.shape
+    size = rows * rows
+    steps = length // CHUNKS // rows
+    blocks = up_first.shape[0]
+    flat = pl.BlockSpec((size, channels), lambda s: (s, 0))
+    part = pl.BlockSpec((blocks, size, LANES), lambda s: (0, s, 0))
+    return pl.pallas_call(
+        hidden_kernel,
+        grid=(steps,),
+        in_specs=[
+            pl.BlockSpec((rows, rows, channels), lambda s: (0, chunk * steps + s, 0)),
+            flat,
+            full(up_first.shape),
+        ],
+        out_specs=[flat, part, part],
+        out_shape=[
+            jax.ShapeDtypeStruct(mixed.shape, BF),
+            jax.ShapeDtypeStruct((blocks, mixed.shape[0], LANES), BF),
+            jax.ShapeDtypeStruct((blocks, mixed.shape[0], LANES), BF),
+        ],
+        compiler_params=params(0),
+        name="hidden",
+    )(x3, mixed, up_first)
+
+
+def middle_kernel(fresh, cols, *refs):
+    uo, ur, bo, br, us, df = refs[:6]
+    refs = refs[6:]
+    if not fresh:
+        sus_in, sdf_in = refs[:2]
+        refs = refs[2:]
+    down_own, down_send, grad_own, grad_send, sus, sdf = refs
+    start = pl.program_id(1) == 0
+
+    @pl.when(start)
+    def _():
+        if fresh:
+            sus[...] = jnp.zeros(sus.shape, F32)
+            sdf[...] = jnp.zeros(sdf.shape, F32)
+        else:
+            sus[...] = sus_in[...]
+            sdf[...] = sdf_in[...]
+
+    up = jnp.concatenate([uo[0], ur[0]], axis=1)
+    back = jnp.concatenate([bo[0], br[0]], axis=1)
+    hidden_units = us.shape[2]
+    down = None
+    grad = None
+    for low in range(0, hidden_units, cols):
+        part = slice(low, low + cols)
+        z = dot(up, us[0, :, part])
+        z2 = z * z
+        h = 0.5 + 0.5 * jnp.tanh(z * (root_two_pi + (root_two_pi * cubic_term) * z2))
+        act = (z * h).astype(BF)
+        slope = h + (h - h * h) * (
+            z * (2.0 * root_two_pi + (6.0 * root_two_pi * cubic_term) * z2)
+        )
+        pre = (dot_nt(back, df[0, part, :]) * slope).astype(BF)
+        step = dot(act, df[0, part, :])
+        down = step if down is None else down + step
+        step = dot_nt(pre, us[0, :, part])
+        grad = step if grad is None else grad + step
+        sdf[0, part, :] += dot_tn(act, back)
+        sus[0, :, part] += dot_tn(up, pre)
+    down_own[0] = down[:, :LANES].astype(BF)
+    down_send[0] = down[:, LANES:].astype(BF)
+    grad_own[0] = grad[:, :LANES].astype(BF)
+    grad_send[0] = grad[:, LANES:].astype(BF)
+
+
+def middle_stage(up_own, up_recv, back_own, back_recv, up_second, down_first, sums, tile=512, cols=256):
+    blocks, count, _ = up_own.shape
+    steps = count // tile
+    part = pl.BlockSpec((1, tile, LANES), lambda g, t: (g, t, 0))
+    us_spec = pl.BlockSpec((1,) + up_second.shape[1:], lambda g, t: (g, 0, 0))
+    df_spec = pl.BlockSpec((1,) + down_first.shape[1:], lambda g, t: (g, 0, 0))
+    fresh = sums is None
+    shape = jax.ShapeDtypeStruct(up_own.shape, BF)
+    return pl.pallas_call(
+        functools.partial(middle_kernel, fresh, cols),
+        grid=(blocks, steps),
+        in_specs=[part, part, part, part, us_spec, df_spec] + ([] if fresh else [us_spec, df_spec]),
+        out_specs=[part] * 4 + [us_spec, df_spec],
+        out_shape=[shape] * 4
+        + [jax.ShapeDtypeStruct(up_second.shape, F32), jax.ShapeDtypeStruct(down_first.shape, F32)],
+        input_output_aliases={} if fresh else {6: 4, 7: 5},
+        compiler_params=params(0, 0),
+        name="middle",
+    )(up_own, up_recv, back_own, back_recv, up_second, down_first, *(() if fresh else sums))
+
+
+def input_kernel(fresh, *refs):
+    x_ref, g_ref, m_ref, h_ref, go, gr, w_ref = refs[:7]
+    refs = refs[7:]
+    if not fresh:
+        suf_in = refs[0]
+        refs = refs[1:]
+    send_ref, base_ref, suf = refs
+
+    @pl.when(pl.program_id(0) == 0)
+    def _():
+        suf[...] = jnp.zeros(suf.shape, F32) if fresh else suf_in[...]
+
+    rows, cols, channels = x_ref.shape
+    size = rows * cols
+    swap = swap_rows(rows)
+    width = w_ref.shape[1]
+    mids = gather_load(go, gr)
+    x3, g3 = x_ref[...].reshape(size, channels), g_ref[...].reshape(size, channels)
+    for k, mid in enumerate(mids):
+        part = slice(k * width, (k + 1) * width)
+        inner = dot_nt(mid, w_ref[k])
+        suf[k] += dot_tn(h_ref[:, part], mid)
+        grad = (g3[:, part].astype(F32) + inner).astype(BF).astype(F32)
+        gating = jax.nn.sigmoid(x3[:, part].astype(F32))
+        mixed = dot(swap, m_ref[:, part])
+        send_ref[:, part] = dot(swap, (grad * gating).astype(BF)).astype(BF)
+        base_ref[:, part] = (grad * (1.0 + gating * (1.0 - gating) * mixed)).astype(BF)
+
+
+def input_stage(chunk, x3, g3, mixed, hidden, grad_own, grad_recv, up_first, sums):
+    rows, length, channels = x3.shape
+    size = rows * rows
+    steps = length // CHUNKS // rows
+    blocks = up_first.shape[0]
+    natural = pl.BlockSpec((rows, rows, channels), lambda s: (0, chunk * steps + s, 0))
+    flat = pl.BlockSpec((size, channels), lambda s: (s, 0))
+    part = pl.BlockSpec((blocks, size, LANES), lambda s: (0, s, 0))
+    fresh = sums is None
+    wspec = full(up_first.shape)
+    return pl.pallas_call(
+        functools.partial(input_kernel, fresh),
+        grid=(steps,),
+        in_specs=[natural, natural, flat, flat, part, part, wspec] + ([] if fresh else [wspec]),
+        out_specs=[flat, flat, wspec],
+        out_shape=[
+            jax.ShapeDtypeStruct(mixed.shape, BF),
+            jax.ShapeDtypeStruct(mixed.shape, BF),
+            jax.ShapeDtypeStruct(up_first.shape, F32),
+        ],
+        input_output_aliases={} if fresh else {7: 2},
+        compiler_params=params(0),
+        name="inputs",
+    )(x3, g3, mixed, hidden, grad_own, grad_recv, up_first, *(() if fresh else (sums,)))
+
+
+def output_kernel(fresh, *refs):
+    g_ref, h_ref, do, dr, w_ref = refs[:5]
+    refs = refs[5:]
+    if not fresh:
+        sds_in = refs[0]
+        refs = refs[2:]
+    o_ref, sds = refs
+
+    @pl.when(pl.program_id(0) == 0)
+    def _():
+        sds[...] = jnp.zeros(sds.shape, F32) if fresh else sds_in[...]
+
+    rows, cols, channels = g_ref.shape
+    size = rows * cols
+    width = w_ref.shape[2]
+    g3 = g_ref[...].reshape(size, channels)
+    for h, perm in enumerate(gather_load(do, dr)):
+        part = slice(h * width, (h + 1) * width)
+        value = h_ref[:, part].astype(F32) + dot(perm, w_ref[h])
+        o_ref[:, :, part] = value.astype(BF).reshape(rows, cols, width)
+        sds[h] += dot_tn(perm, g3[:, part])
+
+
+def output_stage(chunk, g3, hidden, down_own, down_recv, down_second, sums, output):
+    rows, length, channels = g3.shape
+    size = rows * rows
+    steps = length // CHUNKS // rows
+    blocks = down_second.shape[0]
+    natural = pl.BlockSpec((rows, rows, channels), lambda s: (0, chunk * steps + s, 0))
+    flat = pl.BlockSpec((size, channels), lambda s: (s, 0))
+    part = pl.BlockSpec((blocks, size, LANES), lambda s: (0, s, 0))
+    fresh = sums is None
+    wspec = full(down_second.shape)
+    return pl.pallas_call(
+        functools.partial(output_kernel, fresh),
+        grid=(steps,),
+        in_specs=[natural, flat, part, part, wspec]
+        + ([] if fresh else [wspec, pl.BlockSpec(memory_space=pl.ANY)]),
+        out_specs=[natural, wspec],
+        out_shape=[
+            jax.ShapeDtypeStruct(g3.shape, BF),
+            jax.ShapeDtypeStruct(down_second.shape, F32),
+        ],
+        input_output_aliases={} if fresh else {5: 1, 6: 0},
+        compiler_params=params(0),
+        name="outputs",
+    )(g3, hidden, down_own, down_recv, down_second, *(() if fresh else (sums, output)))
+
+
+def last_kernel(rows, w_ref, tw_ref, *refs):
+    chunk_refs, base_refs = refs[:CHUNKS], refs[CHUNKS : 2 * CHUNKS]
+    o_ref, scratch = refs[2 * CHUNKS :]
+    size = rows * rows
+    swap = swap_rows(rows)
+    cols = o_ref.shape[2]
+    groups = chunk_refs[0].shape[0] // size
+    for n, ref in enumerate(chunk_refs):
+        for g in range(groups):
+            index = n * groups + g
+            value = dot(swap, ref[g * size : (g + 1) * size, :]) * tw_ref[:, index : index + 1]
+            scratch[:, index * rows : (index + 1) * rows, :] = value.astype(BF).reshape(rows, rows, cols)
+    weight = w_ref[...]
+    for a in range(rows):
+        base = jnp.concatenate(
+            [ref[g * size + a * rows : g * size + (a + 1) * rows, :] for ref in base_refs for g in range(groups)],
+            axis=0,
+        )
+        o_ref[a] = (dot(weight, scratch[a]) + base.astype(F32)).astype(BF)
+
+
+def last_stage(rows, length, mix_first, tw_cols, fields, bases, cols=256):
+    channels = fields[0].shape[1]
+    spec = pl.BlockSpec((fields[0].shape[0], cols), lambda c: (0, c))
+    return pl.pallas_call(
+        functools.partial(last_kernel, rows),
+        grid=(channels // cols,),
+        in_specs=[full(mix_first.shape), full(tw_cols.shape)] + [spec] * (2 * CHUNKS),
+        out_specs=pl.BlockSpec((rows, length, cols), lambda c: (0, 0, c)),
+        out_shape=jax.ShapeDtypeStruct((rows, length, channels), BF),
+        scratch_shapes=[pltpu.VMEM((rows, length, cols), BF)],
+        compiler_params=params(0),
+        name="last",
+    )(mix_first, tw_cols, *fields, *bases)
+
+
+def exchange(field):
+    return lax.all_to_all(field, "seq", split_axis=0, concat_axis=0, tiled=True)
+
+
+def partner(values):
+    return lax.ppermute(values, "fsdp", [(0, 1), (1, 0)])
+
+
+PLAN = (
+    (1, 0, (("first", 1), ("back", 0), ("back", 1), ("back", 2), ("back", 3))),
+    (1, 1, (("second", 0),)),
+    (2, 0, (("second", 1),)),
+    (1, 2, (("hidden", 0),)),
+    (2, 1, (("second", 2), ("middle", 0))),
+    (1, 3, (("hidden", 1), ("inputs", 0))),
+    (2, 2, (("second", 3), ("middle", 1))),
+    (2, 3, (("hidden", 2), ("inputs", 1), ("outputs", 0))),
+    (3, 0, (("hidden", 3), ("middle", 2))),
+    (3, 1, (("fourth", 0), ("middle", 3), ("inputs", 2))),
+    (4, 0, (("fourth", 1), ("outputs", 1), ("inputs", 3))),
+    (3, 2, (("outputs", 2), ("outputs", 3), ("scatter", 0))),
+    (4, 1, (("fourth", 2),)),
+    (3, 3, (("across", 0),)),
+    (4, 2, (("fourth", 3), ("gather", 0))),
+    (4, 3, (("finish", 0),)),
+)
+
+
+def tie(value, others):
+    return lax.optimization_barrier((value, others))[0]
+
+
+def chunked_shards(
+    seq,
+    activations,
+    mix_first,
+    twiddle,
+    mix_second,
+    up_first,
+    up_second,
+    down_first,
+    down_second,
+    grad_out,
+):
+    local_rows, channels = activations.shape
+    rows, length = twiddle.shape
+    blocks, width = up_first.shape[0], up_first.shape[1]
+    stride = width // NBLK
+    mine = lax.axis_index("fsdp")
+
+    def own_first(values, axis):
+        return jnp.where(mine == 0, values, jnp.roll(values, LANES, axis))
+
+    def group_rows(weight):
+        shaped = weight.reshape(blocks, stride, NBLK, weight.shape[2])
+        return own_first(jnp.transpose(shaped, (0, 2, 1, 3)).reshape(weight.shape), 1)
+
+    def ungroup_rows(weight):
+        shaped = own_first(weight, 1).reshape(blocks, NBLK, stride, weight.shape[2])
+        return jnp.transpose(shaped, (0, 2, 1, 3)).reshape(weight.shape)
+
+    x3 = activations.reshape(rows, length, channels)
+    g3 = grad_out.reshape(rows, length, channels)
+    w2, w2t = mix_second, mix_second.T
+    ups_first, downs_first = own_first(up_first, 2), own_first(down_first, 2)
+    ups_second, downs_second = group_rows(up_second), group_rows(down_second)
+    tw_cols = jnp.transpose(twiddle.reshape(rows, length // rows, rows), (0, 2, 1)).reshape(
+        rows * rows, length // rows
+    )
+
+    sends = first_stage((0,), x3, mix_first, twiddle)
+    going = {(1, 0): sends[0]}
+    arrived, kept = {}, {}
+    sums, sum_first, sum_last, output = None, None, None, None
+    last = sends[0]
+    done = sends[0]
+
+    half = seq // 2
+    halves = [list(range(half)), list(range(half, seq))]
+    across = [(d, (d + half) % seq) for d in range(seq)]
+
+    for step, chunk_of_step, tasks in PLAN:
+        previous = done
+        done = exchange(tie(going[step, chunk_of_step], (last, previous)))
+        arrived[step, chunk_of_step] = done
+        last = previous
+        for name, n in tasks:
+            if name == "first":
+                results = first_stage(tuple(range(1, CHUNKS)), tie(x3, last), mix_first, twiddle)
+                for m, sent in enumerate(results):
+                    going[1, m + 1] = sent
+                last = results[0]
+            elif name == "back":
+                own, send = back_stage(n, tie(g3, last), downs_second)
+                kept["back", n] = (own, partner(send))
+                last = own
+            elif name == "second":
+                last = going[2, n] = second_stage(w2t, tie(arrived[1, n], last), seq, rows)
+            elif name == "hidden":
+                hidden, own, send = hidden_stage(n, x3, tie(arrived[2, n], last), ups_first)
+                kept["hidden", n] = hidden
+                kept["up", n] = (own, partner(send))
+                last = own
+            elif name == "middle":
+                up_own, up_recv = kept["up", n]
+                back_own, back_recv = kept["back", n]
+                down_own, down_send, grad_own, grad_send, *sums = middle_stage(
+                    tie(up_own, last), up_recv, back_own, back_recv, ups_second, downs_first, sums
+                )
+                kept["grad", n] = (grad_own, partner(grad_send))
+                kept["down", n] = (down_own, partner(down_send))
+                last = down_own
+            elif name == "inputs":
+                going[3, n], kept["base", n], sum_first = input_stage(
+                    n,
+                    x3,
+                    g3,
+                    arrived[2, n],
+                    kept["hidden", n],
+                    tie(kept["grad", n][0], last),
+                    kept["grad", n][1],
+                    ups_first,
+                    sum_first,
+                )
+                last = going[3, n]
+            elif name == "outputs":
+                output, sum_last = output_stage(
+                    n,
+                    g3,
+                    kept["hidden", n],
+                    tie(kept["down", n][0], last),
+                    kept["down", n][1],
+                    downs_second,
+                    sum_last,
+                    output,
+                )
+                last = sum_last
+            elif name == "scatter":
+                count = sums[0].shape[0] * sums[0].shape[1]
+                parts = (
+                    sums[0].reshape(count, -1),
+                    jnp.concatenate([v.reshape(-1, width) for v in (sums[1], sum_first, sum_last)], axis=0),
+                )
+                parts = [
+                    lax.psum_scatter(v, "seq", scatter_dimension=0, axis_index_groups=halves, tiled=True)
+                    for v in parts
+                ]
+            elif name == "across":
+                parts = [(tie(v, last) * (1.0 / length)).astype(BF) for v in parts]
+                others = [lax.ppermute(v, "seq", across) for v in parts]
+                last = parts
+            elif name == "gather":
+                parts = [
+                    (v.astype(F32) + tie(w, last).astype(F32)).astype(BF) for v, w in zip(parts, others)
+                ]
+                wholes = [
+                    lax.all_gather(v, "seq", axis=0, axis_index_groups=halves, tiled=True) for v in parts
+                ]
+                last = parts
+            elif name == "finish":
+                one, two = tie(wholes, last)
+                rest = two.reshape(-1, width, width)
+                cut = down_first.shape[0] * down_first.shape[1] // width
+                grads = (
+                    own_first(rest[cut : cut + blocks].astype(F32), 2),
+                    ungroup_rows(one.astype(F32).reshape(up_second.shape)),
+                    own_first(rest[:cut].astype(F32).reshape(down_first.shape), 2),
+                    ungroup_rows(rest[cut + blocks :].astype(F32)),
+                )
+            else:
+                last = going[4, n] = second_stage(w2, tie(arrived[3, n], last), seq, rows)
+
+    fields = [arrived[4, n] for n in range(CHUNKS)]
+    bases = [kept["base", n] for n in range(CHUNKS)]
+    grad_inputs = last_stage(rows, length, mix_first, tw_cols, fields, bases)
+    return (
+        output.reshape(local_rows, channels),
+        grad_inputs.reshape(local_rows, channels),
+        *grads,
+    )
+
+
+def shards(*args):
+    _, _, twiddle, _, up_first = args[:5]
+    rows, length = twiddle.shape
+    blocks, width = up_first.shape[0], up_first.shape[1]
+    seq = length // rows
+    fits = (
+        blocks * (width // NBLK) == LANES
+        and 2 * blocks == NBLK
+        and rows == 16
+        and seq == 16
+        and length % (CHUNKS * seq) == 0
+    )
+    if fits:
+        return chunked_shards(seq, *args)
+    return general_shards(*args)
+
+
 def solution(mesh):
     in_specs = (
         P("seq", "fsdp"),

time: 1750 us -> 1110 us (0.63)
  matrix products: 307 us -> 0 us
  local copies, waits for them, and re-layouts: 333 us -> 38.6 us
  Pallas kernels: 0 us -> 272 us
  blocking collectives: 286 us -> 115 us
  waiting for transfers between devices: 602 us -> 511 us
  other arithmetic: 95.9 us -> 23.1 us
  starting transfers between devices: 98.6 us -> 127 us
    dot_general x16 -> x0, matrix products: 307 us -> none  [product(): return jnp.einsum(form, left, right, preferred_element_type=jnp.float32)]
    ppermute x0 -> x18, waiting for transfers between devices: none -> 276 us  [the longest x16 249 us: partner(): return lax.ppermute(values, 'fsdp', [(0, 1), (1, 0)])]
    pallas_call x0 -> x31, Pallas kernels: none -> 272 us  [the longest x4 96.4 us: middle_stage(): pl.pallas_call(functools.partial(middle_kernel, fresh, cols), grid=(block...]
    psum x1 -> x0, waiting for transfers between devices: 243 us -> none  [shards(): totals = lax.psum((grads[0], grads[1], grads[2], grads[3]), 'seq')]
    all_to_all x2, blocking collectives: 286 us -> 115 us  [exchange(): return lax.all_to_all(field, 'seq', split_axis=0, concat_axis=0, tiled=True)]
    reshape x10 -> x4, local copies, waits for them, and re-layouts: 130 us -> 3.71 us  [the longest x2 2.86 us: group_rows(): shaped = weight.reshape(blocks, stride, NBLK, weight.shape[2])]
    all_to_all x6 -> x14, waiting for transfers between devices: 359 us -> 235 us  [exchange(): return lax.all_to_all(field, 'seq', split_axis=0, concat_axis=0, tiled=True)]
    all_to_all x10 -> x0, local copies, waits for them, and re-layouts: 102 us -> none  [the longest x8 76.1 us: shuffle_blocks(): lax.all_to_all(values, 'fsdp', split_axis=2, concat_axis=1, tiled=True)]
  transfers between devices with their start and end apart: 7 -> 36, of which waited for: 6 -> 25; matrix products, arithmetic and copies ran while one was open for 21% -> 3% of each run, Pallas kernels for 0% -> 23%
where the time goes in v1:
time: 1110 us; the launch traced here: 1100 us
  waiting for transfers between devices  511 us (46%)
  Pallas kernels  272 us (25%)
  starting transfers between devices  127 us (11%)
  blocking collectives  115 us (10%)
  local copies, waits for them, and re-layouts  38.6 us (3%)
  other arithmetic  23.1 us (2%)
  between operations  14.5 us (1%)
    ppermute x16, waiting for transfers between devices, partner(): return lax.ppermute(values, 'fsdp', [(0, 1), (1, 0)])  249 us
    all_to_all x14, waiting for transfers between devices, exchange(): return lax.all_to_all(field, 'seq', split_axis=0, concat_axis=0, tiled=True)  235 us
    all_to_all x2, blocking collectives, exchange(): return lax.all_to_all(field, 'seq', split_axis=0, concat_axis=0, tiled=True)  115 us
    all_to_all x14, starting transfers between devices, exchange(): return lax.all_to_all(field, 'seq', split_axis=0, concat_axis=0, tiled=True)  105 us
    pallas_call x4, Pallas kernels, middle_stage(): pl.pallas_call(functools.partial(middle_kernel, fresh, cols), grid=(block...  96.4 us
    pallas_call x4, Pallas kernels, input_stage(): pl.pallas_call(functools.partial(input_kernel, fresh), grid=(steps,), in_...  37.3 us
    pallas_call x8, Pallas kernels, second_stage(): pl.pallas_call(second_kernel, grid=(channels // cols,), in_specs=[full(we...  35.4 us
    pallas_call x4, Pallas kernels, output_stage(): pl.pallas_call(functools.partial(output_kernel, fresh), grid=(steps,), in...  31.8 us
  transfers between devices with their start and end apart: 36, of which 25 were waited for; matrix products, arithmetic and copies ran while one was open for 3% of the time, Pallas kernels for 23%

profile of v1, /device:TPU:0, one launch (start us, length us, event | category | flops | bytes accessed | tf_op | source)
XLA Modules:
  0.0 1100.6 jit_solution(9166108676824827963)
XLA Ops:
  80.2 35.8 %all-to-all-done.1 = bf16[16,64,1024]{2,1,0:T(8,128)(2,1)} async-done(((bf16[16,64,1024]{2,1,0:T(8,128)(2,1)}), bf16[16,64,1024]{2,1,0:T(8,128)(2,1)}, u32[]{:S(2)}, u32[]{:S(2)}) %all-to-all-start.1) | async-done | bytes 2097184 | tf_op jit(solution)/shard_map/all_to_all | solution.py:538
  131.7 36.5 %all-to-all-done.2 = bf16[16,64,1024]{2,1,0:T(8,128)(2,1)S(1)} async-done(((bf16[16,64,1024]{2,1,0:T(8,128)(2,1)}), bf16[16,64,1024]{2,1,0:T(8,128)(2,1)S(1)}, u32[]{:S(2)}, u32[]{:S(2)}) %all-to-all-start.2) | async-done | bytes 2097184 | tf_op jit(solution)/shard_map/all_to_all | solution.py:538
  187.9 34.0 %all-to-all-done.3 = bf16[16,64,1024]{2,1,0:T(8,128)(2,1)} async-done(((bf16[16,64,1024]{2,1,0:T(8,128)(2,1)}), bf16[16,64,1024]{2,1,0:T(8,128)(2,1)}, u32[]{:S(2)}, u32[]{:S(2)}) %all-to-all-start.3) | async-done | bytes 2097184 | tf_op jit(solution)/shard_map/all_to_all | solution.py:538
  259.5 22.0 %collective-permute-done.refs_1_ = bf16[4,1024,128]{2,1,0:T(8,128)(2,1)S(1)} collective-permute-done((bf16[4,1024,128]{2,1,0:T(8,128)(2,1)}, bf16[4,1024,128]{2,1,0:T(8,128)(2,1)S(1)}, u32[]{:S(2)}, u32[]{:S(2)}) %collective-permute-start) | collective-permute-done | bytes 1048608 | tf_op jit(solution)/shard_map/ppermute | solution.py:542
  282.5 23.6 %middle.4 = (bf16[4,1024,128]{2,1,0:T(8,128)(2,1)}, bf16[4,1024,128]{2,1,0:T(8,128)(2,1)}, bf16[4,1024,128]{2,1,0:T(8,128)(2,1)}, bf16[4,1024,128]{2,1,0:T(8,128...) custom-call(bf16[4,1024,128]{2,1,0:T(8,128)(2,1)} %get-tuple-element.145.refs_0_, ...), custom_call_target="tpu_custom_call" | custom-call | tf_op jit(solution)/shard_map/middle/pallas_call | solution.py:384
  320.8 17.9 %collective-permute-done.4.refs_5_ = bf16[4,1024,128]{2,1,0:T(8,128)(2,1)S(1)} collective-permute-done((bf16[4,1024,128]{2,1,0:T(8,128)(2,1)S(1)}, bf16[4,1024,128]{2,1,0:T(8,128)(2,1)S(1)}, u32[]{:S(2)}, u32[]{:S(2)}) %collective-permute-start.4) | collective-permute-done | bytes 1048608 | tf_op jit(solution)/shard_map/ppermute | solution.py:542
  372.3 19.7 %collective-permute-done.3.refs_3_ = bf16[4,1024,128]{2,1,0:T(8,128)(2,1)S(1)} collective-permute-done((bf16[4,1024,128]{2,1,0:T(8,128)(2,1)S(1)}, bf16[4,1024,128]{2,1,0:T(8,128)(2,1)S(1)}, u32[]{:S(2)}, u32[]{:S(2)}) %collective-permute-start.3) | collective-permute-done | bytes 1048608 | tf_op jit(solution)/shard_map/ppermute | solution.py:542
  391.9 22.0 %collective-permute-done.2.refs_1_ = bf16[4,1024,128]{2,1,0:T(8,128)(2,1)S(1)} collective-permute-done((bf16[4,1024,128]{2,1,0:T(8,128)(2,1)}, bf16[4,1024,128]{2,1,0:T(8,128)(2,1)S(1)}, u32[]{:S(2)}, u32[]{:S(2)}) %collective-permute-start.2) | collective-permute-done | bytes 1048608 | tf_op jit(solution)/shard_map/ppermute | solution.py:542
  414.9 24.3 %middle.5 = (bf16[4,1024,128]{2,1,0:T(8,128)(2,1)}, bf16[4,1024,128]{2,1,0:T(8,128)(2,1)}, bf16[4,1024,128]{2,1,0:T(8,128)(2,1)}, bf16[4,1024,128]{2,1,0:T(8,128...) custom-call(bf16[4,1024,128]{2,1,0:T(8,128)(2,1)} %get-tuple-element.154.r, ...), custom_call_target="tpu_custom_call", output_to_operand_aliasing={{4}: (6, {}), {5}: (7, {})} | custom-call | tf_op jit(solution)/shard_map/middle/pallas_call | solution.py:384
  454.3 18.2 %collective-permute-done.5.refs_5_ = bf16[4,1024,128]{2,1,0:T(8,128)(2,1)S(1)} collective-permute-done((bf16[4,1024,128]{2,1,0:T(8,128)(2,1)}, bf16[4,1024,128]{2,1,0:T(8,128)(2,1)S(1)}, u32[]{:S(2)}, u32[]{:S(2)}) %collective-permute-start.5) | collective-permute-done | bytes 1048608 | tf_op jit(solution)/shard_map/ppermute | solution.py:542
  520.3 16.2 %collective-permute-done.10.refs_3_ = bf16[4,1024,128]{2,1,0:T(8,128)(2,1)S(1)} collective-permute-done((bf16[4,1024,128]{2,1,0:T(8,128)(2,1)}, bf16[4,1024,128]{2,1,0:T(8,128)(2,1)S(1)}, u32[]{:S(2)}, u32[]{:S(2)}) %collective-permute-start.10) | collective-permute-done | bytes 1048608 | tf_op jit(solution)/shard_map/ppermute | solution.py:542
  536.5 22.5 %collective-permute-done.9.refs_1_ = bf16[4,1024,128]{2,1,0:T(8,128)(2,1)S(1)} collective-permute-done((bf16[4,1024,128]{2,1,0:T(8,128)(2,1)}, bf16[4,1024,128]{2,1,0:T(8,128)(2,1)S(1)}, u32[]{:S(2)}, u32[]{:S(2)}) %collective-permute-start.9) | collective-permute-done | bytes 1048608 | tf_op jit(solution)/shard_map/ppermute | solution.py:542
  560.0 24.3 %middle.6 = (bf16[4,1024,128]{2,1,0:T(8,128)(2,1)}, bf16[4,1024,128]{2,1,0:T(8,128)(2,1)}, bf16[4,1024,128]{2,1,0:T(8,128)(2,1)}, bf16[4,1024,128]{2,1,0:T(8,128...) custom-call(bf16[4,1024,128]{2,1,0:T(8,128)(2,1)} %get-tuple-element.186.r, ...), custom_call_target="tpu_custom_call", output_to_operand_aliasing={{4}: (6, {}), {5}: (7, {})} | custom-call | tf_op jit(solution)/shard_map/middle/pallas_call | solution.py:384
  603.3 24.3 %middle.7 = (bf16[4,1024,128]{2,1,0:T(8,128)(2,1)}, bf16[4,1024,128]{2,1,0:T(8,128)(2,1)}, bf16[4,1024,128]{2,1,0:T(8,128)(2,1)}, bf16[4,1024,128]{2,1,0:T(8,128...) custom-call(bf16[4,1024,128]{2,1,0:T(8,128)(2,1)} %get-tuple-element.183.r, ...), custom_call_target="tpu_custom_call", output_to_operand_aliasing={{4}: (6, {}), {5}: (7, {})} | custom-call | tf_op jit(solution)/shard_map/middle/pallas_call | solution.py:384
  630.3 23.0 %collective-permute-done.11.refs_5_ = bf16[4,1024,128]{2,1,0:T(8,128)(2,1)S(1)} collective-permute-done((bf16[4,1024,128]{2,1,0:T(8,128)(2,1)S(1)}, bf16[4,1024,128]{2,1,0:T(8,128)(2,1)S(1)}, u32[]{:S(2)}, u32[]{:S(2)}) %collective-permute-start.11) | collective-permute-done | bytes 1048608 | tf_op jit(solution)/shard_map/ppermute | solution.py:542
  679.3 17.7 %collective-permute-done.13.refs_3_ = bf16[4,1024,128]{2,1,0:T(8,128)(2,1)S(1)} collective-permute-done((bf16[4,1024,128]{2,1,0:T(8,128)(2,1)}, bf16[4,1024,128]{2,1,0:T(8,128)(2,1)S(1)}, u32[]{:S(2)}, u32[]{:S(2)}) %collective-permute-start.13) | collective-permute-done | bytes 1048608 | tf_op jit(solution)/shard_map/ppermute | solution.py:542
  706.0 13.5 %collective-permute-done.15.refs_5_ = bf16[4,1024,128]{2,1,0:T(8,128)(2,1)S(1)} collective-permute-done((bf16[4,1024,128]{2,1,0:T(8,128)(2,1)}, bf16[4,1024,128]{2,1,0:T(8,128)(2,1)S(1)}, u32[]{:S(2)}, u32[]{:S(2)}) %collective-permute-start.15) | collective-permute-done | bytes 1048608 | tf_op jit(solution)/shard_map/ppermute | solution.py:542
  750.1 13.8 %collective-permute-done.14.refs_3_ = bf16[4,1024,128]{2,1,0:T(8,128)(2,1)S(1)} collective-permute-done((bf16[4,1024,128]{2,1,0:T(8,128)(2,1)}, bf16[4,1024,128]{2,1,0:T(8,128)(2,1)S(1)}, u32[]{:S(2)}, u32[]{:S(2)}) %collective-permute-start.14) | collective-permute-done | bytes 1048608 | tf_op jit(solution)/shard_map/ppermute | solution.py:542
  779.0 57.9 %all_to_all.184 = bf16[16,64,1024]{2,1,0:T(8,128)(2,1)} all-to-all(bf16[16,64,1024]{2,1,0:T(8,128)(2,1)S(1)} %bitcast.163), channel_id=1, replica_groups=mesh['seq'=16,'fsdp'=2] {'seq'}, dimensions={0} | all-to-all | bytes 4194304 | tf_op jit(solution)/shard_map/all_to_all | solution.py:538
  845.0 45.2 %all-to-all-done.12 = bf16[16,64,1024]{2,1,0:T(8,128)(2,1)S(1)} async-done(((bf16[16,64,1024]{2,1,0:T(8,128)(2,1)}), bf16[16,64,1024]{2,1,0:T(8,128)(2,1)S(1)}, u32[]{:S(2)}, u32[]{:S(2)}) %all-to-all-start.12) | async-done | bytes 2097184 | tf_op jit(solution)/shard_map/all_to_all | solution.py:538
  899.8 42.7 %all-to-all-done.13 = bf16[16,64,1024]{2,1,0:T(8,128)(2,1)} async-done(((bf16[16,64,1024]{2,1,0:T(8,128)(2,1)}), bf16[16,64,1024]{2,1,0:T(8,128)(2,1)}, u32[]{:S(2)}, u32[]{:S(2)}) %all-to-all-start.13) | async-done | bytes 2097184 | tf_op jit(solution)/shard_map/all_to_all | solution.py:538
  959.1 17.7 %collective-permute-done.17 = bf16[768,256]{1,0:T(8,128)(2,1)S(1)} collective-permute-done((bf16[768,256]{1,0:T(8,128)(2,1)S(1)}, bf16[768,256]{1,0:T(8,128)(2,1)S(1)}, u32[]{:S(2)}, u32[]{:S(2)}) %collective-permute-start.17) | collective-permute-done | bytes 393248 | tf_op jit(solution)/shard_map/ppermute | solution.py:686
  978.9 56.8 %all_to_all.185 = bf16[16,64,1024]{2,1,0:T(8,128)(2,1)} all-to-all(bf16[16,64,1024]{2,1,0:T(8,128)(2,1)S(1)} %bitcast.144), channel_id=1, replica_groups=mesh['seq'=16,'fsdp'=2] {'seq'}, dimensions={0} | all-to-all | bytes 4194304 | tf_op jit(solution)/shard_map/all_to_all | solution.py:538
  1056.7 23.7 %all-to-all-done.15 = bf16[16,64,1024]{2,1,0:T(8,128)(2,1)S(1)} async-done(((bf16[16,64,1024]{2,1,0:T(8,128)(2,1)}), bf16[16,64,1024]{2,1,0:T(8,128)(2,1)S(1)}, u32[]{:S(2)}, u32[]{:S(2)}) %all-to-all-start.15) | async-done | bytes 2097184 | tf_op jit(solution)/shard_map/all_to_all | solution.py:538
  (196 shorter events, 432.9 us)
Async XLA Ops:
  13.9 48.5 %all-to-all-start = ((bf16[16,64,1024]{2,1,0:T(8,128)(2,1)}), bf16[16,64,1024]{2,1,0:T(8,128)(2,1)S(1)}, u32[]{:S(2)}, u32[]{:S(2)}) async-start(bf16[16,64,1024]{2,1,0:T(8,128)(2,1)} %bitcast.151), calls=%async_computation | async-start | bytes 4194304 | tf_op jit(solution)/shard_map/all_to_all | solution.py:538
  63.7 52.3 %all-to-all-start.1 = ((bf16[16,64,1024]{2,1,0:T(8,128)(2,1)}), bf16[16,64,1024]{2,1,0:T(8,128)(2,1)}, u32[]{:S(2)}, u32[]{:S(2)}) async-start(bf16[16,64,1024]{2,1,0:T(8,128)(2,1)} %bitcast.166), calls=%async_computation.1 | async-start | bytes 4194304 | tf_op jit(solution)/shard_map/all_to_all | solution.py:538
  116.0 52.2 %all-to-all-start.2 = ((bf16[16,64,1024]{2,1,0:T(8,128)(2,1)}), bf16[16,64,1024]{2,1,0:T(8,128)(2,1)S(1)}, u32[]{:S(2)}, u32[]{:S(2)}) async-start(bf16[16,64,1024]{2,1,0:T(8,128)(2,1)} %bitcast.147), calls=%async_computation.2 | async-start | bytes 4194304 | tf_op jit(solution)/shard_map/all_to_all | solution.py:538
  169.6 52.3 %all-to-all-start.3 = ((bf16[16,64,1024]{2,1,0:T(8,128)(2,1)}), bf16[16,64,1024]{2,1,0:T(8,128)(2,1)}, u32[]{:S(2)}, u32[]{:S(2)}) async-start(bf16[16,64,1024]{2,1,0:T(8,128)(2,1)} %bitcast.165), calls=%async_computation.3 | async-start | bytes 4194304 | tf_op jit(solution)/shard_map/all_to_all | solution.py:538
  221.9 84.2 %all-to-all-start.4 = ((bf16[16,64,1024]{2,1,0:T(8,128)(2,1)}), bf16[16,64,1024]{2,1,0:T(8,128)(2,1)S(1)}, u32[]{:S(2)}, u32[]{:S(2)}) async-start(bf16[16,64,1024]{2,1,0:T(8,128)(2,1)} %bitcast.143), calls=%async_computation.4 | async-start | bytes 4194304 | tf_op jit(solution)/shard_map/all_to_all | solution.py:538
  307.4 46.8 %all-to-all-start.5 = ((bf16[16,64,1024]{2,1,0:T(8,128)(2,1)}), bf16[16,64,1024]{2,1,0:T(8,128)(2,1)}, u32[]{:S(2)}, u32[]{:S(2)}) async-start(bf16[16,64,1024]{2,1,0:T(8,128)(2,1)} %bitcast.160), calls=%async_computation.5 | async-start | bytes 4194304 | tf_op jit(solution)/shard_map/all_to_all | solution.py:538
  354.3 84.9 %all-to-all-start.6 = ((bf16[16,64,1024]{2,1,0:T(8,128)(2,1)}), bf16[16,64,1024]{2,1,0:T(8,128)(2,1)S(1)}, u32[]{:S(2)}, u32[]{:S(2)}) async-start(bf16[16,64,1024]{2,1,0:T(8,128)(2,1)} %bitcast.140), calls=%async_computation.6 | async-start | bytes 4194304 | tf_op jit(solution)/shard_map/all_to_all | solution.py:538
  440.6 62.5 %all-to-all-start.7 = ((bf16[16,64,1024]{2,1,0:T(8,128)(2,1)}), bf16[16,64,1024]{2,1,0:T(8,128)(2,1)S(1)}, u32[]{:S(2)}, u32[]{:S(2)}) async-start(bf16[16,64,1024]{2,1,0:T(8,128)(2,1)} %bitcast.145), calls=%async_computation.7 | async-start | bytes 4194304 | tf_op jit(solution)/shard_map/all_to_all | solution.py:538
  504.4 79.9 %all-to-all-start.8 = ((bf16[16,64,1024]{2,1,0:T(8,128)(2,1)}), bf16[16,64,1024]{2,1,0:T(8,128)(2,1)}, u32[]{:S(2)}, u32[]{:S(2)}) async-start(bf16[16,64,1024]{2,1,0:T(8,128)(2,1)} %bitcast.161), calls=%async_computation.8 | async-start | bytes 4194304 | tf_op jit(solution)/shard_map/all_to_all | solution.py:538
  511.7 47.2 %collective-permute-start.9 = (bf16[4,1024,128]{2,1,0:T(8,128)(2,1)}, bf16[4,1024,128]{2,1,0:T(8,128)(2,1)S(1)}, u32[]{:S(2)}, u32[]{:S(2)}) collective-permute-start(bf16[4,1024,128]{2,1,0:T(8,128)(2,1)} %get-tuple-element.187), channel_id=1, source_target_pairs={{0,1},{1,0},{2,3},{3,2},{4,5},{5,4},{6,7},{7,6},{8,9},{9,8},{10,11... | collective-permute-start | bytes 3145736 | tf_op jit(solution)/shard_map/ppermute | solution.py:542
  512.2 82.8 %collective-permute-start.8 = (bf16[4,1024,128]{2,1,0:T(8,128)(2,1)}, bf16[4,1024,128]{2,1,0:T(8,128)(2,1)S(1)}, u32[]{:S(2)}, u32[]{:S(2)}) collective-permute-start(bf16[4,1024,128]{2,1,0:T(8,128)(2,1)} %get-tuple-element.185), channel_id=1, source_target_pairs={{0,1},{1,0},{2,3},{3,2},{4,5},{5,4},{6,7},{7,6},{8,9},{9,8},{10,11... | collective-permute-start | bytes 3145736 | tf_op jit(solution)/shard_map/ppermute | solution.py:542
  519.8 83.5 %collective-permute-start.7 = (bf16[4,1024,128]{2,1,0:T(8,128)(2,1)}, bf16[4,1024,128]{2,1,0:T(8,128)(2,1)}, u32[]{:S(2)}, u32[]{:S(2)}) collective-permute-start(bf16[4,1024,128]{2,1,0:T(8,128)(2,1)} %get-tuple-element.184), channel_id=1, source_target_pairs={{0,1},{1,0},{2,3},{3,2},{4,5},{5,4},{6,7},{7,6},{8,9},{9,8},{10,11... | collective-permute-start | bytes 3145736 | tf_op jit(solution)/shard_map/ppermute | solution.py:542
  584.3 79.5 %all-to-all-start.9 = ((bf16[16,64,1024]{2,1,0:T(8,128)(2,1)}), bf16[16,64,1024]{2,1,0:T(8,128)(2,1)S(1)}, u32[]{:S(2)}, u32[]{:S(2)}) async-start(bf16[16,64,1024]{2,1,0:T(8,128)(2,1)} %bitcast.162), calls=%async_computation.9 | async-start | bytes 4194304 | tf_op jit(solution)/shard_map/all_to_all | solution.py:538
  590.2 305.8 %reduce-scatter.3.cloned.1.call-start = ((), (), s32[]{:S(2)}) async-start(), calls=%async_computation.18 | async-start | bytes 4718592 | tf_op jit(solution)/shard_map/reduce_scatter | solution.py:681
  665.2 64.6 %all-to-all-start.10 = ((bf16[16,64,1024]{2,1,0:T(8,128)(2,1)}), bf16[16,64,1024]{2,1,0:T(8,128)(2,1)S(1)}, u32[]{:S(2)}, u32[]{:S(2)}) async-start(bf16[16,64,1024]{2,1,0:T(8,128)(2,1)} %bitcast.139), calls=%async_computation.10 | async-start | bytes 4194304 | tf_op jit(solution)/shard_map/all_to_all | solution.py:538
  670.7 286.2 %reduce-scatter.5.cloned.1.call-start = ((), (), s32[]{:S(2)}) async-start(), calls=%async_computation.19 | async-start | bytes 7077888 | tf_op jit(solution)/shard_map/reduce_scatter | solution.py:681
  672.3 47.2 %collective-permute-start.15 = (bf16[4,1024,128]{2,1,0:T(8,128)(2,1)}, bf16[4,1024,128]{2,1,0:T(8,128)(2,1)S(1)}, u32[]{:S(2)}, u32[]{:S(2)}) collective-permute-start(bf16[4,1024,128]{2,1,0:T(8,128)(2,1)} %get-tuple-element.219), channel_id=1, source_target_pairs={{0,1},{1,0},{2,3},{3,2},{4,5},{5,4},{6,7},{7,6},{8,9},{9,8},{10,11... | collective-permute-start | bytes 3145736 | tf_op jit(solution)/shard_map/ppermute | solution.py:542
  672.9 69.3 %collective-permute-start.12 = (bf16[4,1024,128]{2,1,0:T(8,128)(2,1)}, bf16[4,1024,128]{2,1,0:T(8,128)(2,1)}, u32[]{:S(2)}, u32[]{:S(2)}) collective-permute-start(bf16[4,1024,128]{2,1,0:T(8,128)(2,1)} %get-tuple-element.204), channel_id=1, source_target_pairs={{0,1},{1,0},{2,3},{3,2},{4,5},{5,4},{6,7},{7,6},{8,9},{9,8},{10,11... | collective-permute-start | bytes 3145736 | tf_op jit(solution)/shard_map/ppermute | solution.py:542
  674.4 89.5 %collective-permute-start.14 = (bf16[4,1024,128]{2,1,0:T(8,128)(2,1)}, bf16[4,1024,128]{2,1,0:T(8,128)(2,1)S(1)}, u32[]{:S(2)}, u32[]{:S(2)}) collective-permute-start(bf16[4,1024,128]{2,1,0:T(8,128)(2,1)} %get-tuple-element.213), channel_id=1, source_target_pairs={{0,1},{1,0},{2,3},{3,2},{4,5},{5,4},{6,7},{7,6},{8,9},{9,8},{10,11... | collective-permute-start | bytes 3145736 | tf_op jit(solution)/shard_map/ppermute | solution.py:542
  836.9 53.2 %all-to-all-start.12 = ((bf16[16,64,1024]{2,1,0:T(8,128)(2,1)}), bf16[16,64,1024]{2,1,0:T(8,128)(2,1)S(1)}, u32[]{:S(2)}, u32[]{:S(2)}) async-start(bf16[16,64,1024]{2,1,0:T(8,128)(2,1)} %bitcast.142), calls=%async_computation.12 | async-start | bytes 4194304 | tf_op jit(solution)/shard_map/all_to_all | solution.py:538
  891.4 51.0 %all-to-all-start.13 = ((bf16[16,64,1024]{2,1,0:T(8,128)(2,1)}), bf16[16,64,1024]{2,1,0:T(8,128)(2,1)}, u32[]{:S(2)}, u32[]{:S(2)}) async-start(bf16[16,64,1024]{2,1,0:T(8,128)(2,1)} %bitcast.164), calls=%async_computation.15 | async-start | bytes 4194304 | tf_op jit(solution)/shard_map/all_to_all | solution.py:538
  895.9 144.5 %all-gather.3.cloned.1.call-start = ((), (), s32[]{:S(2)}) async-start(), calls=%async_computation.20 | async-start | bytes 2359296 | tf_op jit(solution)/shard_map/all_gather | solution.py:693
  897.1 59.0 %collective-permute-start.16 = (bf16[128,1024]{1,0:T(8,128)(2,1)S(1)}, bf16[128,1024]{1,0:T(8,128)(2,1)S(1)}, u32[]{:S(2)}, u32[]{:S(2)}) collective-permute-start(bf16[128,1024]{1,0:T(8,128)(2,1)S(1)} %multiply_convert_fusion.1), channel_id=1, source_target_pairs={{0,16},{2,18},{4,20},{6,22},{8,24},{10,26},{12,28},{14,30},{16,0},... | collective-permute-start | bytes 786440 | tf_op jit(solution)/shard_map/ppermute | solution.py:686
  956.8 83.6 %all-gather.5.cloned.1.call-start = ((), (), s32[]{:S(2)}) async-start(), calls=%async_computation.21 | async-start | bytes 3538944 | tf_op jit(solution)/shard_map/all_gather | solution.py:693
  (51 other events, 631.4 us)
Sparse Core Ops, SparseCore 0:
  627.8 49.7 reduce-scatter.2
  777.6 113.6 reduce-scatter.4
  956.9 28.8 all-gather.2
  988.0 46.4 all-gather.4

commit v2 on v1

--- a/solution.py
+++ b/solution.py
@@ -182,6 +182,10 @@
     )
 
 
+def in_hbm(shape, kind=BF):
+    return jax.ShapeDtypeStruct(shape, kind)
+
+
 def full(shape):
     zeros = (0,) * len(shape)
     return pl.BlockSpec(shape, lambda *_: zeros)
@@ -198,33 +202,39 @@
         scratch[a] = value.astype(BF)
     size = rows * rows
     for n, out in enumerate(outs):
+        _, _, height, cols = out.shape
+        count = size // height
         for group in range(span // rows):
             start = n * span + group * rows
-            piece = scratch[:, start : start + rows, :].reshape(size, scratch.shape[2])
-            out[group * size : (group + 1) * size, :] = dot(swap, piece).astype(BF)
-
-
-def first_stage(chunks, x3, w1t, twt, cols=256):
+            piece = scratch[:, start : start + rows, :].reshape(size, cols)
+            value = dot(swap, piece).astype(BF)
+            out[group * count : (group + 1) * count, 0] = value.reshape(count, height, cols)
+
+
+def first_stage(chunks, places, seq, x3, mix_first, twiddle, cols=256):
     rows, length, channels = x3.shape
     span = length // CHUNKS
-    shape = jax.ShapeDtypeStruct((span * rows, channels), BF)
+    height = span * rows // seq
     return pl.pallas_call(
         functools.partial(first_kernel, chunks, span, rows),
         grid=(channels // cols,),
         in_specs=[
             pl.BlockSpec((rows, length, cols), lambda c: (0, 0, c)),
-            full(w1t.shape),
-            full(twt.shape),
+            full(mix_first.shape),
+            full(twiddle.shape),
         ],
-        out_specs=[pl.BlockSpec((span * rows, cols), lambda c: (0, c))] * len(chunks),
-        out_shape=[shape] * len(chunks),
+        out_specs=[
+            pl.BlockSpec((seq, 1, height, cols), lambda c, part=part: (0, part, 0, c)) for part, _ in places
+        ],
+        out_shape=[in_hbm((seq, parts, height, channels)) for _, parts in places],
         scratch_shapes=[pltpu.VMEM((rows, span * len(chunks), cols), BF)],
         compiler_params=params(0),
         name="first",
-    )(x3, w1t, twt)
-
-
-def second_kernel(w_ref, x_ref, o_ref):
+    )(x3, mix_first, twiddle)
+
+
+def second_kernel(w_ref, x_ref, *refs):
+    o_ref = refs[-1]
     seq, own, rows, cols = x_ref.shape
     weight = w_ref[...]
     for j in range(own):
@@ -232,21 +242,27 @@
         o_ref[:, j] = value.astype(BF).reshape(seq, rows, cols)
 
 
-def second_stage(weight, field, seq, rows, cols=256):
-    total, channels = field.shape
-    own = total // (seq * rows)
-    four = field.reshape(seq, own, rows, channels)
-    spec = pl.BlockSpec((seq, own, rows, cols), lambda c: (0, 0, 0, c))
+def second_stage(weight, field, place, buffer, rows, cols=256):
+    source, part_in = field
+    part, parts = place
+    seq, parts_in, height, channels = source.shape
+    own = height // rows
+    five = source.reshape(seq, parts_in, own, rows, channels)
     out = pl.pallas_call(
         second_kernel,
         grid=(channels // cols,),
-        in_specs=[full(weight.shape), spec],
-        out_specs=spec,
-        out_shape=jax.ShapeDtypeStruct(four.shape, BF),
+        in_specs=[
+            full(weight.shape),
+            pl.BlockSpec((seq, None, own, rows, cols), lambda c: (0, part_in, 0, 0, c)),
+        ]
+        + ([] if buffer is None else [pl.BlockSpec(memory_space=pl.ANY)]),
+        out_specs=pl.BlockSpec((seq, None, own, rows, cols), lambda c: (0, part, 0, 0, c)),
+        out_shape=in_hbm((seq, parts, own, rows, channels)),
+        input_output_aliases={} if buffer is None else {2: 0},
         compiler_params=params(0),
         name="second",
-    )(weight, four)
-    return out.reshape(total, channels)
+    )(weight, five, *(() if buffer is None else (buffer.reshape(seq, parts, own, rows, channels),)))
+    return out.reshape(seq, parts, height, channels)
 
 
 def spread_store(values, own_ref, send_ref):
@@ -293,7 +309,7 @@
 
 def hidden_kernel(x_ref, m_ref, w_ref, h_ref, own_ref, send_ref):
     rows, cols, channels = x_ref.shape
-    mixed = dot(swap_rows(rows), m_ref[...])
+    mixed = dot(swap_rows(rows), m_ref[...].reshape(rows * cols, channels))
     inputs = x_ref[...].reshape(rows * cols, channels).astype(F32)
     hidden = (inputs + jax.nn.sigmoid(inputs) * mixed).astype(BF)
     h_ref[...] = hidden
@@ -302,30 +318,35 @@
     spread_store(values, own_ref, send_ref)
 
 
+def arriving(field, size):
+    source, part = field
+    height, channels = source.shape[2:]
+    return pl.BlockSpec((size // height, None, height, channels), lambda s: (s, part, 0, 0))
+
+
 def hidden_stage(chunk, x3, mixed, up_first):
     rows, length, channels = x3.shape
     size = rows * rows
     steps = length // CHUNKS // rows
     blocks = up_first.shape[0]
-    flat = pl.BlockSpec((size, channels), lambda s: (s, 0))
     part = pl.BlockSpec((blocks, size, LANES), lambda s: (0, s, 0))
     return pl.pallas_call(
         hidden_kernel,
         grid=(steps,),
         in_specs=[
             pl.BlockSpec((rows, rows, channels), lambda s: (0, chunk * steps + s, 0)),
-            flat,
+            arriving(mixed, size),
             full(up_first.shape),
         ],
-        out_specs=[flat, part, part],
+        out_specs=[pl.BlockSpec((size, channels), lambda s: (s, 0)), part, part],
         out_shape=[
-            jax.ShapeDtypeStruct(mixed.shape, BF),
-            jax.ShapeDtypeStruct((blocks, mixed.shape[0], LANES), BF),
-            jax.ShapeDtypeStruct((blocks, mixed.shape[0], LANES), BF),
+            jax.ShapeDtypeStruct((steps * size, channels), BF),
+            jax.ShapeDtypeStruct((blocks, steps * size, LANES), BF),
+            in_hbm((blocks, steps * size, LANES)),
         ],
         compiler_params=params(0),
         name="hidden",
-    )(x3, mixed, up_first)
+    )(x3, mixed[0], up_first)
 
 
 def middle_kernel(fresh, cols, *refs):
@@ -396,15 +417,11 @@
 
 def input_kernel(fresh, *refs):
     x_ref, g_ref, m_ref, h_ref, go, gr, w_ref = refs[:7]
-    refs = refs[7:]
-    if not fresh:
-        suf_in = refs[0]
-        refs = refs[1:]
-    send_ref, base_ref, suf = refs
+    send_ref, base_ref, suf = refs[-3:]
 
     @pl.when(pl.program_id(0) == 0)
     def _():
-        suf[...] = jnp.zeros(suf.shape, F32) if fresh else suf_in[...]
+        suf[...] = jnp.zeros(suf.shape, F32) if fresh else refs[7][...]
 
     rows, cols, channels = x_ref.shape
     size = rows * cols
@@ -418,35 +435,45 @@
         suf[k] += dot_tn(h_ref[:, part], mid)
         grad = (g3[:, part].astype(F32) + inner).astype(BF).astype(F32)
         gating = jax.nn.sigmoid(x3[:, part].astype(F32))
-        mixed = dot(swap, m_ref[:, part])
-        send_ref[:, part] = dot(swap, (grad * gating).astype(BF)).astype(BF)
+        mixed = dot(swap, m_ref[:, :, part].reshape(size, width))
+        send = dot(swap, (grad * gating).astype(BF)).astype(BF)
+        send_ref[:, :, part] = send.reshape(send_ref.shape[0], send_ref.shape[1], width)
         base_ref[:, part] = (grad * (1.0 + gating * (1.0 - gating) * mixed)).astype(BF)
 
 
-def input_stage(chunk, x3, g3, mixed, hidden, grad_own, grad_recv, up_first, sums):
+def input_stage(chunk, x3, g3, mixed, hidden, grad_own, grad_recv, up_first, sums, place, buffer):
     rows, length, channels = x3.shape
     size = rows * rows
     steps = length // CHUNKS // rows
     blocks = up_first.shape[0]
     natural = pl.BlockSpec((rows, rows, channels), lambda s: (0, chunk * steps + s, 0))
     flat = pl.BlockSpec((size, channels), lambda s: (s, 0))
-    part = pl.BlockSpec((blocks, size, LANES), lambda s: (0, s, 0))
+    half = pl.BlockSpec((blocks, size, LANES), lambda s: (0, s, 0))
     fresh = sums is None
     wspec = full(up_first.shape)
+    seq, _, height, _ = mixed[0].shape
+    part, parts = place
+    extra = [] if fresh else [(sums, wspec, 2)]
+    if buffer is not None:
+        extra.append((buffer, pl.BlockSpec(memory_space=pl.ANY), 0))
     return pl.pallas_call(
         functools.partial(input_kernel, fresh),
         grid=(steps,),
-        in_specs=[natural, natural, flat, flat, part, part, wspec] + ([] if fresh else [wspec]),
-        out_specs=[flat, flat, wspec],
+        in_specs=[natural, natural, arriving(mixed, size), flat, half, half, wspec] + [e[1] for e in extra],
+        out_specs=[
+            pl.BlockSpec((size // height, None, height, channels), lambda s: (s, part, 0, 0)),
+            flat,
+            wspec,
+        ],
         out_shape=[
-            jax.ShapeDtypeStruct(mixed.shape, BF),
-            jax.ShapeDtypeStruct(mixed.shape, BF),
+            in_hbm((seq, parts, height, channels)),
+            jax.ShapeDtypeStruct((steps * size, channels), BF),
             jax.ShapeDtypeStruct(up_first.shape, F32),
         ],
-        input_output_aliases={} if fresh else {7: 2},
+        input_output_aliases={7 + i: e[2] for i, e in enumerate(extra)},
         compiler_params=params(0),
         name="inputs",
-    )(x3, g3, mixed, hidden, grad_own, grad_recv, up_first, *(() if fresh else (sums,)))
+    )(x3, g3, mixed[0], hidden, grad_own, grad_recv, up_first, *[e[0] for e in extra])
 
 
 def output_kernel(fresh, *refs):
@@ -504,11 +531,14 @@
     size = rows * rows
     swap = swap_rows(rows)
     cols = o_ref.shape[2]
-    groups = chunk_refs[0].shape[0] // size
+    height = chunk_refs[0].shape[1]
+    count = size // height
+    groups = chunk_refs[0].shape[0] // count
     for n, ref in enumerate(chunk_refs):
         for g in range(groups):
             index = n * groups + g
-            value = dot(swap, ref[g * size : (g + 1) * size, :]) * tw_ref[:, index : index + 1]
+            piece = ref[g * count : (g + 1) * count].reshape(size, cols)
+            value = dot(swap, piece) * tw_ref[:, index : index + 1]
             scratch[:, index * rows : (index + 1) * rows, :] = value.astype(BF).reshape(rows, rows, cols)
     weight = w_ref[...]
     for a in range(rows):
@@ -520,18 +550,21 @@
 
 
 def last_stage(rows, length, mix_first, tw_cols, fields, bases, cols=256):
-    channels = fields[0].shape[1]
-    spec = pl.BlockSpec((fields[0].shape[0], cols), lambda c: (0, c))
+    seq, _, height, channels = fields[0][0].shape
+    spec = pl.BlockSpec((bases[0].shape[0], cols), lambda c: (0, c))
+    field_specs = [
+        pl.BlockSpec((seq, None, height, cols), lambda c, part=part: (0, part, 0, c)) for _, part in fields
+    ]
     return pl.pallas_call(
         functools.partial(last_kernel, rows),
         grid=(channels // cols,),
-        in_specs=[full(mix_first.shape), full(tw_cols.shape)] + [spec] * (2 * CHUNKS),
+        in_specs=[full(mix_first.shape), full(tw_cols.shape)] + field_specs + [spec] * CHUNKS,
         out_specs=pl.BlockSpec((rows, length, cols), lambda c: (0, 0, c)),
         out_shape=jax.ShapeDtypeStruct((rows, length, channels), BF),
         scratch_shapes=[pltpu.VMEM((rows, length, cols), BF)],
         compiler_params=params(0),
         name="last",
-    )(mix_first, tw_cols, *fields, *bases)
+    )(mix_first, tw_cols, *[f for f, _ in fields], *bases)
 
 
 def exchange(field):
@@ -543,27 +576,17 @@
 
 
 PLAN = (
-    (1, 0, (("first", 1), ("back", 0), ("back", 1), ("back", 2), ("back", 3))),
-    (1, 1, (("second", 0),)),
-    (2, 0, (("second", 1),)),
-    (1, 2, (("hidden", 0),)),
-    (2, 1, (("second", 2), ("middle", 0))),
-    (1, 3, (("hidden", 1), ("inputs", 0))),
-    (2, 2, (("second", 3), ("middle", 1))),
-    (2, 3, (("hidden", 2), ("inputs", 1), ("outputs", 0))),
-    (3, 0, (("hidden", 3), ("middle", 2))),
-    (3, 1, (("fourth", 0), ("middle", 3), ("inputs", 2))),
-    (4, 0, (("fourth", 1), ("outputs", 1), ("inputs", 3))),
-    (3, 2, (("outputs", 2), ("outputs", 3), ("scatter", 0))),
-    (4, 1, (("fourth", 2),)),
-    (3, 3, (("across", 0),)),
-    (4, 2, (("fourth", 3), ("gather", 0))),
-    (4, 3, (("finish", 0),)),
+    (((1, 0),), (("first", 1), ("back", 0), ("back", 1), ("back", 2), ("back", 3))),
+    (((1, 1),), (("second", 0),)),
+    (((2, 0), (1, 2)), (("second", 1),)),
+    (((2, 1), (1, 3)), (("hidden", 0), ("second", 2), ("middle", 0), ("inputs", 0))),
+    (((2, 2), (3, 0)), (("hidden", 1), ("second", 3), ("middle", 1), ("outputs", 0), ("inputs", 1))),
+    (((2, 3), (3, 1)), (("hidden", 2), ("fourth", 0), ("middle", 2), ("outputs", 1), ("inputs", 2))),
+    (((3, 2), (4, 0)), (("hidden", 3), ("fourth", 1), ("middle", 3), ("outputs", 2), ("inputs", 3))),
+    (((3, 3), (4, 1)), (("fourth", 2), ("outputs", 3))),
+    (((4, 2),), (("fourth", 3),)),
+    (((4, 3),), ()),
 )
-
-
-def tie(value, others):
-    return lax.optimization_barrier((value, others))[0]
 
 
 def chunked_shards(
@@ -604,108 +627,85 @@
         rows * rows, length // rows
     )
 
-    sends = first_stage((0,), x3, mix_first, twiddle)
-    going = {(1, 0): sends[0]}
-    arrived, kept = {}, {}
+    place = {}
+    for slot, (travels, _) in enumerate(PLAN):
+        for part, key in enumerate(travels):
+            place[key] = (slot, part, len(travels))
+    buffers, arrived, kept = {}, {}, {}
     sums, sum_first, sum_last, output = None, None, None, None
-    last = sends[0]
-    done = sends[0]
-
-    half = seq // 2
-    halves = [list(range(half)), list(range(half, seq))]
-    across = [(d, (d + half) % seq) for d in range(seq)]
-
-    for step, chunk_of_step, tasks in PLAN:
-        previous = done
-        done = exchange(tie(going[step, chunk_of_step], (last, previous)))
-        arrived[step, chunk_of_step] = done
-        last = previous
+
+    def spot(key):
+        slot, part, parts = place[key]
+        return (part, parts), buffers.get(slot)
+
+    def first(chunks):
+        results = first_stage(chunks, [place[1, m][1:] for m in chunks], seq, x3, mix_first, twiddle)
+        for m, sent in zip(chunks, results):
+            buffers[place[1, m][0]] = sent
+
+    def reduced(values):
+        return lax.psum_scatter(
+            (values * (1.0 / length)).astype(BF), "seq", scatter_dimension=0, tiled=True
+        )
+
+    def gathered(values):
+        return lax.all_gather(values, "seq", axis=0, tiled=True)
+
+    first((0,))
+    for slot, (travels, tasks) in enumerate(PLAN):
+        done = exchange(buffers[slot])
+        for part, key in enumerate(travels):
+            arrived[key] = (done, part)
         for name, n in tasks:
             if name == "first":
-                results = first_stage(tuple(range(1, CHUNKS)), tie(x3, last), mix_first, twiddle)
-                for m, sent in enumerate(results):
-                    going[1, m + 1] = sent
-                last = results[0]
+                first(tuple(range(1, CHUNKS)))
             elif name == "back":
-                own, send = back_stage(n, tie(g3, last), downs_second)
+                own, send = back_stage(n, g3, downs_second)
                 kept["back", n] = (own, partner(send))
-                last = own
             elif name == "second":
-                last = going[2, n] = second_stage(w2t, tie(arrived[1, n], last), seq, rows)
+                buffers[place[2, n][0]] = second_stage(w2t, arrived[1, n], *spot((2, n)), rows)
             elif name == "hidden":
-                hidden, own, send = hidden_stage(n, x3, tie(arrived[2, n], last), ups_first)
+                hidden, own, send = hidden_stage(n, x3, arrived[2, n], ups_first)
                 kept["hidden", n] = hidden
                 kept["up", n] = (own, partner(send))
-                last = own
             elif name == "middle":
-                up_own, up_recv = kept["up", n]
-                back_own, back_recv = kept["back", n]
                 down_own, down_send, grad_own, grad_send, *sums = middle_stage(
-                    tie(up_own, last), up_recv, back_own, back_recv, ups_second, downs_first, sums
+                    *kept["up", n], *kept["back", n], ups_second, downs_first, sums
                 )
                 kept["grad", n] = (grad_own, partner(grad_send))
                 kept["down", n] = (down_own, partner(down_send))
-                last = down_own
             elif name == "inputs":
-                going[3, n], kept["base", n], sum_first = input_stage(
+                buffers[place[3, n][0]], kept["base", n], sum_first = input_stage(
                     n,
                     x3,
                     g3,
                     arrived[2, n],
                     kept["hidden", n],
-                    tie(kept["grad", n][0], last),
-                    kept["grad", n][1],
+                    *kept["grad", n],
                     ups_first,
                     sum_first,
+                    *spot((3, n)),
                 )
-                last = going[3, n]
             elif name == "outputs":
                 output, sum_last = output_stage(
-                    n,
-                    g3,
-                    kept["hidden", n],
-                    tie(kept["down", n][0], last),
-                    kept["down", n][1],
-                    downs_second,
-                    sum_last,
-                    output,
-                )
-                last = sum_last
-            elif name == "scatter":
-                count = sums[0].shape[0] * sums[0].shape[1]
-                parts = (
-                    sums[0].reshape(count, -1),
-                    jnp.concatenate([v.reshape(-1, width) for v in (sums[1], sum_first, sum_last)], axis=0),
-                )
-                parts = [
-                    lax.psum_scatter(v, "seq", scatter_dimension=0, axis_index_groups=halves, tiled=True)
-                    for v in parts
-                ]
-            elif name == "across":
-                parts = [(tie(v, last) * (1.0 / length)).astype(BF) for v in parts]
-                others = [lax.ppermute(v, "seq", across) for v in parts]
-                last = parts
-            elif name == "gather":
-                parts = [
-                    (v.astype(F32) + tie(w, last).astype(F32)).astype(BF) for v, w in zip(parts, others)
-                ]
-                wholes = [
-                    lax.all_gather(v, "seq", axis=0, axis_index_groups=halves, tiled=True) for v in parts
-                ]
-                last = parts
-            elif name == "finish":
-                one, two = tie(wholes, last)
-                rest = two.reshape(-1, width, width)
-                cut = down_first.shape[0] * down_first.shape[1] // width
-                grads = (
-                    own_first(rest[cut : cut + blocks].astype(F32), 2),
-                    ungroup_rows(one.astype(F32).reshape(up_second.shape)),
-                    own_first(rest[:cut].astype(F32).reshape(down_first.shape), 2),
-                    ungroup_rows(rest[cut + blocks :].astype(F32)),
+                    n, g3, kept["hidden", n], *kept["down", n], downs_second, sum_last, output
                 )
             else:
-                last = going[4, n] = second_stage(w2, tie(arrived[3, n], last), seq, rows)
-
+                buffers[place[4, n][0]] = second_stage(w2, arrived[3, n], *spot((4, n)), rows)
+
+    parts = (
+        reduced(sums[0].reshape(-1, sums[0].shape[2])),
+        reduced(sums[1].reshape(-1, width)),
+        reduced(jnp.concatenate([sum_first, sum_last], axis=0).reshape(-1, width)),
+    )
+    one, two, rest = (gathered(v) for v in parts)
+    rest = rest.astype(F32).reshape(-1, width, width)
+    grads = (
+        own_first(rest[:blocks], 2),
+        ungroup_rows(one.astype(F32).reshape(up_second.shape)),
+        own_first(two.astype(F32).reshape(down_first.shape), 2),
+        ungroup_rows(rest[blocks:]),
+    )
     fields = [arrived[4, n] for n in range(CHUNKS)]
     bases = [kept["base", n] for n in range(CHUNKS)]
     grad_inputs = last_stage(rows, length, mix_first, tw_cols, fields, bases)

time: 1110 us -> 1170 us (1.054)
  waiting for transfers between devices: 511 us -> 728 us
  blocking collectives: 115 us -> 0 us
  starting transfers between devices: 127 us -> 100 us
    reduce_scatter x2 -> x3, waiting for transfers between devices: 0.04 us -> 216 us  [reduced(): lax.psum_scatter((values * (1.0 / length)).astype(BF), 'seq', scatter_dim...]
    all_gather x2 -> x3, waiting for transfers between devices: 0.01 us -> 119 us  [gathered(): return lax.all_gather(values, 'seq', axis=0, tiled=True)]
    all_to_all x2 -> x0, blocking collectives: 115 us -> none  [exchange(): return lax.all_to_all(field, 'seq', split_axis=0, concat_axis=0, tiled=True)]
    all_to_all x14 -> x10, waiting for transfers between devices: 235 us -> 142 us  [exchange(): return lax.all_to_all(field, 'seq', split_axis=0, concat_axis=0, tiled=True)]
    ppermute x2 -> x0, waiting for transfers between devices: 26.8 us -> none  [chunked_shards(): others = [lax.ppermute(v, 'seq', across) for v in parts]]
    all_to_all x14 -> x10, starting transfers between devices: 105 us -> 80.8 us  [exchange(): return lax.all_to_all(field, 'seq', split_axis=0, concat_axis=0, tiled=True)]
    unnamed x79 -> x55, local copies, waits for them, and re-layouts: 25.5 us -> 16.2 us
  transfers between devices with their start and end apart: 36 -> 32, of which waited for: 25 -> 24; matrix products, arithmetic and copies ran while one was open for 3% -> 3% of each run, Pallas kernels for 23% -> 22%
where the time goes in v2:
time: 1170 us
  waiting for transfers between devices  728 us (62%)
  Pallas kernels  272 us (23%)
  starting transfers between devices  100 us (9%)
  local copies, waits for them, and re-layouts  29 us (2%)
  other arithmetic  24.4 us (2%)
  between operations  14.9 us (1%)
    ppermute x16, waiting for transfers between devices, partner(): return lax.ppermute(values, 'fsdp', [(0, 1), (1, 0)])  251 us
    reduce_scatter x3, waiting for transfers between devices, reduced(): lax.psum_scatter((values * (1.0 / length)).astype(BF), 'seq', scatter_dim...  216 us
    all_to_all x10, waiting for transfers between devices, exchange(): return lax.all_to_all(field, 'seq', split_axis=0, concat_axis=0, tiled=True)  142 us
    all_gather x3, waiting for transfers between devices, gathered(): return lax.all_gather(values, 'seq', axis=0, tiled=True)  119 us
    pallas_call x4, Pallas kernels, middle_stage(): pl.pallas_call(functools.partial(middle_kernel, fresh, cols), grid=(block...  96.4 us
    all_to_all x10, starting transfers between devices, exchange(): return lax.all_to_all(field, 'seq', split_axis=0, concat_axis=0, tiled=True)  80.8 us
    pallas_call x4, Pallas kernels, input_stage(): pl.pallas_call(functools.partial(input_kernel, fresh), grid=(steps,), in_...  37.9 us
    pallas_call x8, Pallas kernels, second_stage(): pl.pallas_call(second_kernel, grid=(channels // cols,), in_specs=[full(we...  35 us
  transfers between devices with their start and end apart: 32, of which 24 were waited for; matrix products, arithmetic and copies ran while one was open for 3% of the time, Pallas kernels for 22%

profile of v2, /device:TPU:0, one launch (start us, length us, event | category | flops | bytes accessed | tf_op | source)
XLA Modules:
  0.0 1167.7 jit_solution(8171400373522471217)
XLA Ops:
  29.6 32.6 %all-to-all-done.2 = bf16[16,1,64,1024]{3,2,1,0:T(8,128)(2,1)S(1)} async-done(((bf16[16,1,64,1024]{3,2,1,0:T(8,128)(2,1)}), bf16[16,1,64,1024]{3,2,1,0:T(8,128)(2,1)S(1)}, u32[]{:S(2)}, u32[]{:S(2)}) %all-to-all-start.2) | async-done | bytes 2097184 | tf_op jit(solution)/shard_map/all_to_all | solution.py:571
  79.9 35.9 %all-to-all-done = bf16[16,1,64,1024]{3,2,1,0:T(8,128)(2,1)S(1)} async-done(((bf16[16,1,64,1024]{3,2,1,0:T(8,128)(2,1)}), bf16[16,1,64,1024]{3,2,1,0:T(8,128)(2,1)S(1)}, u32[]{:S(2)}, u32[]{:S(2)}) %all-to-all-start) | async-done | bytes 2097184 | tf_op jit(solution)/shard_map/all_to_all | solution.py:571
  132.7 73.2 %all-to-all-done.3.m_ref.refs_2_ = bf16[16,2,64,1024]{3,2,1,0:T(8,128)(2,1)} async-done(((bf16[16,2,64,1024]{3,2,1,0:T(8,128)(2,1)}), bf16[16,2,64,1024]{3,2,1,0:T(8,128)(2,1)}, u32[]{:S(2)}, u32[]{:S(2)}) %all-to-all-start.3) | async-done | bytes 4194336 | tf_op jit(solution)/shard_map/all_to_all | solution.py:571
  205.9 20.4 %all-to-all-start.1 = ((bf16[16,2,64,1024]{3,2,1,0:T(8,128)(2,1)}), bf16[16,2,64,1024]{3,2,1,0:T(8,128)(2,1)}, u32[]{:S(2)}, u32[]{:S(2)}) async-start(bf16[16,2,64,1024]{3,2,1,0:T(8,128)(2,1)} %bitcast.92), calls=%async_computation.1 | async-start | bytes 8388608 | tf_op jit(solution)/shard_map/all_to_all | solution.py:571
  258.8 22.0 %collective-permute-done.2.refs_1_ = bf16[4,1024,128]{2,1,0:T(8,128)(2,1)S(1)} collective-permute-done((bf16[4,1024,128]{2,1,0:T(8,128)(2,1)}, bf16[4,1024,128]{2,1,0:T(8,128)(2,1)S(1)}, u32[]{:S(2)}, u32[]{:S(2)}) %collective-permute-start.2) | collective-permute-done | bytes 1048608 | tf_op jit(solution)/shard_map/ppermute | solution.py:575
  281.7 23.6 %middle.4 = (bf16[4,1024,128]{2,1,0:T(8,128)(2,1)}, bf16[4,1024,128]{2,1,0:T(8,128)(2,1)}, bf16[4,1024,128]{2,1,0:T(8,128)(2,1)}, bf16[4,1024,128]{2,1,0:T(8,128...) custom-call(bf16[4,1024,128]{2,1,0:T(8,128)(2,1)} %get-tuple-element.81.refs_0_, ...), custom_call_target="tpu_custom_call" | custom-call | tf_op jit(solution)/shard_map/middle/pallas_call | solution.py:405
  311.2 19.0 %collective-permute-done.5.refs_5_ = bf16[4,1024,128]{2,1,0:T(8,128)(2,1)S(1)} collective-permute-done((bf16[4,1024,128]{2,1,0:T(8,128)(2,1)}, bf16[4,1024,128]{2,1,0:T(8,128)(2,1)S(1)}, u32[]{:S(2)}, u32[]{:S(2)}) %collective-permute-start.5) | collective-permute-done | bytes 1048608 | tf_op jit(solution)/shard_map/ppermute | solution.py:575
  359.1 18.2 %collective-permute-done.1.refs_3_ = bf16[4,1024,128]{2,1,0:T(8,128)(2,1)S(1)} collective-permute-done((bf16[4,1024,128]{2,1,0:T(8,128)(2,1)}, bf16[4,1024,128]{2,1,0:T(8,128)(2,1)S(1)}, u32[]{:S(2)}, u32[]{:S(2)}) %collective-permute-start.1) | collective-permute-done | bytes 1048608 | tf_op jit(solution)/shard_map/ppermute | solution.py:575
  377.4 22.0 %collective-permute-done.refs_1_ = bf16[4,1024,128]{2,1,0:T(8,128)(2,1)S(1)} collective-permute-done((bf16[4,1024,128]{2,1,0:T(8,128)(2,1)}, bf16[4,1024,128]{2,1,0:T(8,128)(2,1)S(1)}, u32[]{:S(2)}, u32[]{:S(2)}) %collective-permute-start) | collective-permute-done | bytes 1048608 | tf_op jit(solution)/shard_map/ppermute | solution.py:575
  400.3 24.3 %middle.5 = (bf16[4,1024,128]{2,1,0:T(8,128)(2,1)}, bf16[4,1024,128]{2,1,0:T(8,128)(2,1)}, bf16[4,1024,128]{2,1,0:T(8,128)(2,1)}, bf16[4,1024,128]{2,1,0:T(8,128...) custom-call(bf16[4,1024,128]{2,1,0:T(8,128)(2,1)} %get-tuple-element.76.re, ...), custom_call_target="tpu_custom_call", output_to_operand_aliasing={{4}: (6, {}), {5}: (7, {})} | custom-call | tf_op jit(solution)/shard_map/middle/pallas_call | solution.py:405
  430.6 19.1 %collective-permute-done.4.refs_5_ = bf16[4,1024,128]{2,1,0:T(8,128)(2,1)S(1)} collective-permute-done((bf16[4,1024,128]{2,1,0:T(8,128)(2,1)}, bf16[4,1024,128]{2,1,0:T(8,128)(2,1)S(1)}, u32[]{:S(2)}, u32[]{:S(2)}) %collective-permute-start.4) | collective-permute-done | bytes 1048608 | tf_op jit(solution)/shard_map/ppermute | solution.py:575
  478.7 18.2 %collective-permute-done.9.refs_3_ = bf16[4,1024,128]{2,1,0:T(8,128)(2,1)S(1)} collective-permute-done((bf16[4,1024,128]{2,1,0:T(8,128)(2,1)}, bf16[4,1024,128]{2,1,0:T(8,128)(2,1)S(1)}, u32[]{:S(2)}, u32[]{:S(2)}) %collective-permute-start.9) | collective-permute-done | bytes 1048608 | tf_op jit(solution)/shard_map/ppermute | solution.py:575
  496.9 21.8 %collective-permute-done.8.refs_1_ = bf16[4,1024,128]{2,1,0:T(8,128)(2,1)S(1)} collective-permute-done((bf16[4,1024,128]{2,1,0:T(8,128)(2,1)}, bf16[4,1024,128]{2,1,0:T(8,128)(2,1)S(1)}, u32[]{:S(2)}, u32[]{:S(2)}) %collective-permute-start.8) | collective-permute-done | bytes 1048608 | tf_op jit(solution)/shard_map/ppermute | solution.py:575
  519.7 24.3 %middle.6 = (bf16[4,1024,128]{2,1,0:T(8,128)(2,1)}, bf16[4,1024,128]{2,1,0:T(8,128)(2,1)}, bf16[4,1024,128]{2,1,0:T(8,128)(2,1)}, bf16[4,1024,128]{2,1,0:T(8,128...) custom-call(bf16[4,1024,128]{2,1,0:T(8,128)(2,1)} %get-tuple-element.100.r, ...), custom_call_target="tpu_custom_call", output_to_operand_aliasing={{4}: (6, {}), {5}: (7, {})} | custom-call | tf_op jit(solution)/shard_map/middle/pallas_call | solution.py:405
  550.0 18.9 %collective-permute-done.14.refs_5_ = bf16[4,1024,128]{2,1,0:T(8,128)(2,1)S(1)} collective-permute-done((bf16[4,1024,128]{2,1,0:T(8,128)(2,1)}, bf16[4,1024,128]{2,1,0:T(8,128)(2,1)S(1)}, u32[]{:S(2)}, u32[]{:S(2)}) %collective-permute-start.14) | collective-permute-done | bytes 1048608 | tf_op jit(solution)/shard_map/ppermute | solution.py:575
  601.8 14.7 %collective-permute-done.7.refs_3_ = bf16[4,1024,128]{2,1,0:T(8,128)(2,1)S(1)} collective-permute-done((bf16[4,1024,128]{2,1,0:T(8,128)(2,1)}, bf16[4,1024,128]{2,1,0:T(8,128)(2,1)S(1)}, u32[]{:S(2)}, u32[]{:S(2)}) %collective-permute-start.7) | collective-permute-done | bytes 1048608 | tf_op jit(solution)/shard_map/ppermute | solution.py:575
  616.6 22.5 %collective-permute-done.6.refs_1_ = bf16[4,1024,128]{2,1,0:T(8,128)(2,1)S(1)} collective-permute-done((bf16[4,1024,128]{2,1,0:T(8,128)(2,1)}, bf16[4,1024,128]{2,1,0:T(8,128)(2,1)S(1)}, u32[]{:S(2)}, u32[]{:S(2)}) %collective-permute-start.6) | collective-permute-done | bytes 1048608 | tf_op jit(solution)/shard_map/ppermute | solution.py:575
  640.0 24.3 %middle.7 = (bf16[4,1024,128]{2,1,0:T(8,128)(2,1)}, bf16[4,1024,128]{2,1,0:T(8,128)(2,1)}, bf16[4,1024,128]{2,1,0:T(8,128)(2,1)}, bf16[4,1024,128]{2,1,0:T(8,128...) custom-call(bf16[4,1024,128]{2,1,0:T(8,128)(2,1)} %get-tuple-element.95.re, ...), custom_call_target="tpu_custom_call", output_to_operand_aliasing={{4}: (6, {}), {5}: (7, {})} | custom-call | tf_op jit(solution)/shard_map/middle/pallas_call | solution.py:405
  777.8 77.7 %reduce-scatter.4.cloned.1.call-done = bf16[128,256]{1,0:T(8,128)(2,1)} async-done(((bf16[2048,256]{1,0:T(8,128)(2,1)}), bf16[128,256]{1,0:T(8,128)(2,1)}) %reduce-scatter.4.cloned.1.call-update) | async-done | bytes 65552 | tf_op jit(solution)/shard_map/reduce_scatter | solution.py:647
  855.9 71.5 %reduce-scatter.6.cloned.1.call-done = bf16[64,1024]{1,0:T(8,128)(2,1)} async-done(((bf16[1024,1024]{1,0:T(8,128)(2,1)}), bf16[64,1024]{1,0:T(8,128)(2,1)}) %reduce-scatter.6.cloned.1.call-update) | async-done | bytes 131088 | tf_op jit(solution)/shard_map/reduce_scatter | solution.py:647
  935.5 66.6 %reduce-scatter.8.cloned.1.call-done = bf16[256,256]{1,0:T(8,128)(2,1)} async-done(((bf16[4096,256]{1,0:T(8,128)(2,1)}), bf16[256,256]{1,0:T(8,128)(2,1)}) %reduce-scatter.8.cloned.1.call-update) | async-done | bytes 131088 | tf_op jit(solution)/shard_map/reduce_scatter | solution.py:647
  1011.8 48.9 %all-gather.4.cloned.1.call-done = bf16[2048,256]{1,0:T(8,128)(2,1)} async-done(((bf16[128,256]{1,0:T(8,128)(2,1)}), bf16[2048,256]{1,0:T(8,128)(2,1)}) %all-gather.4.cloned.1.call-update) | async-done | bytes 1048592 | tf_op jit(solution)/shard_map/all_gather | solution.py:652
  1065.2 36.8 %all-gather.6.cloned.1.call-done = bf16[1024,1024]{1,0:T(8,128)(2,1)} async-done(((bf16[64,1024]{1,0:T(8,128)(2,1)}), bf16[1024,1024]{1,0:T(8,128)(2,1)}) %all-gather.6.cloned.1.call-update) | async-done | bytes 2097168 | tf_op jit(solution)/shard_map/all_gather | solution.py:652
  1111.0 33.3 %all-gather.8.cloned.1.call-done = bf16[4096,256]{1,0:T(8,128)(2,1)} async-done(((bf16[256,256]{1,0:T(8,128)(2,1)}), bf16[4096,256]{1,0:T(8,128)(2,1)}) %all-gather.8.cloned.1.call-update) | async-done | bytes 2097168 | tf_op jit(solution)/shard_map/all_gather | solution.py:652
  (161 shorter events, 362.9 us)
Async XLA Ops:
  13.9 48.4 %all-to-all-start.2 = ((bf16[16,1,64,1024]{3,2,1,0:T(8,128)(2,1)}), bf16[16,1,64,1024]{3,2,1,0:T(8,128)(2,1)S(1)}, u32[]{:S(2)}, u32[]{:S(2)}) async-start(bf16[16,1,64,1024]{3,2,1,0:T(8,128)(2,1)} %first.3), calls=%async_computation.2 | async-start | bytes 4194304 | tf_op jit(solution)/shard_map/all_to_all | solution.py:571
  63.6 52.2 %all-to-all-start = ((bf16[16,1,64,1024]{3,2,1,0:T(8,128)(2,1)}), bf16[16,1,64,1024]{3,2,1,0:T(8,128)(2,1)S(1)}, u32[]{:S(2)}, u32[]{:S(2)}) async-start(bf16[16,1,64,1024]{3,2,1,0:T(8,128)(2,1)} %get-tuple-element.73), calls=%async_computation | async-start | bytes 4194304 | tf_op jit(solution)/shard_map/all_to_all | solution.py:571
  117.1 88.8 %all-to-all-start.3 = ((bf16[16,2,64,1024]{3,2,1,0:T(8,128)(2,1)}), bf16[16,2,64,1024]{3,2,1,0:T(8,128)(2,1)}, u32[]{:S(2)}, u32[]{:S(2)}) async-start(bf16[16,2,64,1024]{3,2,1,0:T(8,128)(2,1)} %bitcast.94), calls=%async_computation.3 | async-start | bytes 8388608 | tf_op jit(solution)/shard_map/all_to_all | solution.py:571
  205.9 134.5 %all-to-all-start.1 = ((bf16[16,2,64,1024]{3,2,1,0:T(8,128)(2,1)}), bf16[16,2,64,1024]{3,2,1,0:T(8,128)(2,1)}, u32[]{:S(2)}, u32[]{:S(2)}) async-start(bf16[16,2,64,1024]{3,2,1,0:T(8,128)(2,1)} %bitcast.92), calls=%async_computation.1 | async-start | bytes 8388608 | tf_op jit(solution)/shard_map/all_to_all | solution.py:571
  340.4 119.8 %all-to-all-start.5 = ((bf16[16,2,64,1024]{3,2,1,0:T(8,128)(2,1)}), bf16[16,2,64,1024]{3,2,1,0:T(8,128)(2,1)}, u32[]{:S(2)}, u32[]{:S(2)}) async-start(bf16[16,2,64,1024]{3,2,1,0:T(8,128)(2,1)} %get-tuple-element.99), calls=%async_computation.5 | async-start | bytes 8388608 | tf_op jit(solution)/shard_map/all_to_all | solution.py:571
  358.6 40.7 %collective-permute-start = (bf16[4,1024,128]{2,1,0:T(8,128)(2,1)}, bf16[4,1024,128]{2,1,0:T(8,128)(2,1)S(1)}, u32[]{:S(2)}, u32[]{:S(2)}) collective-permute-start(bf16[4,1024,128]{2,1,0:T(8,128)(2,1)} %get-tuple-element.77), channel_id=1, source_target_pairs={{0,1},{1,0},{2,3},{3,2},{4,5},{5,4},{6,7},{7,6},{8,9},{9,8},{10,11... | collective-permute-start | bytes 3145736 | tf_op jit(solution)/shard_map/ppermute | solution.py:575
  460.2 119.2 %all-to-all-start.4 = ((bf16[16,2,64,1024]{3,2,1,0:T(8,128)(2,1)}), bf16[16,2,64,1024]{3,2,1,0:T(8,128)(2,1)}, u32[]{:S(2)}, u32[]{:S(2)}) async-start(bf16[16,2,64,1024]{3,2,1,0:T(8,128)(2,1)} %get-tuple-element.93), calls=%async_computation.4 | async-start | bytes 8388608 | tf_op jit(solution)/shard_map/all_to_all | solution.py:571
  478.2 40.6 %collective-permute-start.8 = (bf16[4,1024,128]{2,1,0:T(8,128)(2,1)}, bf16[4,1024,128]{2,1,0:T(8,128)(2,1)S(1)}, u32[]{:S(2)}, u32[]{:S(2)}) collective-permute-start(bf16[4,1024,128]{2,1,0:T(8,128)(2,1)} %get-tuple-element.101), channel_id=1, source_target_pairs={{0,1},{1,0},{2,3},{3,2},{4,5},{5,4},{6,7},{7,6},{8,9},{9,8},{10,11... | collective-permute-start | bytes 3145736 | tf_op jit(solution)/shard_map/ppermute | solution.py:575
  579.5 188.4 %all-to-all-start.6 = ((bf16[16,2,64,1024]{3,2,1,0:T(8,128)(2,1)}), bf16[16,2,64,1024]{3,2,1,0:T(8,128)(2,1)}, u32[]{:S(2)}, u32[]{:S(2)}) async-start(bf16[16,2,64,1024]{3,2,1,0:T(8,128)(2,1)} %get-tuple-element.127), calls=%async_computation.6 | async-start | bytes 8388608 | tf_op jit(solution)/shard_map/all_to_all | solution.py:571
  585.1 270.5 %reduce-scatter.4.cloned.1.call-start = ((), (), s32[]{:S(2)}) async-start(), calls=%async_computation.13 | async-start | bytes 1114112 | tf_op jit(solution)/shard_map/reduce_scatter | solution.py:647
  597.8 41.2 %collective-permute-start.6 = (bf16[4,1024,128]{2,1,0:T(8,128)(2,1)}, bf16[4,1024,128]{2,1,0:T(8,128)(2,1)S(1)}, u32[]{:S(2)}, u32[]{:S(2)}) collective-permute-start(bf16[4,1024,128]{2,1,0:T(8,128)(2,1)} %get-tuple-element.96), channel_id=1, source_target_pairs={{0,1},{1,0},{2,3},{3,2},{4,5},{5,4},{6,7},{7,6},{8,9},{9,8},{10,11... | collective-permute-start | bytes 3145736 | tf_op jit(solution)/shard_map/ppermute | solution.py:575
  598.3 68.1 %collective-permute-start.13 = (bf16[4,1024,128]{2,1,0:T(8,128)(2,1)}, bf16[4,1024,128]{2,1,0:T(8,128)(2,1)S(1)}, u32[]{:S(2)}, u32[]{:S(2)}) collective-permute-start(bf16[4,1024,128]{2,1,0:T(8,128)(2,1)} %get-tuple-element.116), channel_id=1, source_target_pairs={{0,1},{1,0},{2,3},{3,2},{4,5},{5,4},{6,7},{7,6},{8,9},{9,8},{10,11... | collective-permute-start | bytes 3145736 | tf_op jit(solution)/shard_map/ppermute | solution.py:575
  599.8 84.2 %collective-permute-start.12 = (bf16[4,1024,128]{2,1,0:T(8,128)(2,1)}, bf16[4,1024,128]{2,1,0:T(8,128)(2,1)S(1)}, u32[]{:S(2)}, u32[]{:S(2)}) collective-permute-start(bf16[4,1024,128]{2,1,0:T(8,128)(2,1)} %get-tuple-element.114), channel_id=1, source_target_pairs={{0,1},{1,0},{2,3},{3,2},{4,5},{5,4},{6,7},{7,6},{8,9},{9,8},{10,11... | collective-permute-start | bytes 3145736 | tf_op jit(solution)/shard_map/ppermute | solution.py:575
  600.3 106.1 %collective-permute-start.11 = (bf16[4,1024,128]{2,1,0:T(8,128)(2,1)}, bf16[4,1024,128]{2,1,0:T(8,128)(2,1)S(1)}, u32[]{:S(2)}, u32[]{:S(2)}) collective-permute-start(bf16[4,1024,128]{2,1,0:T(8,128)(2,1)} %get-tuple-element.112), channel_id=1, source_target_pairs={{0,1},{1,0},{2,3},{3,2},{4,5},{5,4},{6,7},{7,6},{8,9},{9,8},{10,11... | collective-permute-start | bytes 3145736 | tf_op jit(solution)/shard_map/ppermute | solution.py:575
  664.3 64.6 %collective-permute-start.10 = (bf16[4,1024,128]{2,1,0:T(8,128)(2,1)}, bf16[4,1024,128]{2,1,0:T(8,128)(2,1)S(1)}, u32[]{:S(2)}, u32[]{:S(2)}) collective-permute-start(bf16[4,1024,128]{2,1,0:T(8,128)(2,1)} %get-tuple-element.109), channel_id=1, source_target_pairs={{0,1},{1,0},{2,3},{3,2},{4,5},{5,4},{6,7},{7,6},{8,9},{9,8},{10,11... | collective-permute-start | bytes 3145736 | tf_op jit(solution)/shard_map/ppermute | solution.py:575
  665.8 84.9 %collective-permute-start.15 = (bf16[4,1024,128]{2,1,0:T(8,128)(2,1)}, bf16[4,1024,128]{2,1,0:T(8,128)(2,1)S(1)}, u32[]{:S(2)}, u32[]{:S(2)}) collective-permute-start(bf16[4,1024,128]{2,1,0:T(8,128)(2,1)} %get-tuple-element.129), channel_id=1, source_target_pairs={{0,1},{1,0},{2,3},{3,2},{4,5},{5,4},{6,7},{7,6},{8,9},{9,8},{10,11... | collective-permute-start | bytes 3145736 | tf_op jit(solution)/shard_map/ppermute | solution.py:575
  763.8 163.6 %reduce-scatter.6.cloned.1.call-start = ((), (), s32[]{:S(2)}) async-start(), calls=%async_computation.15 | async-start | bytes 2228224 | tf_op jit(solution)/shard_map/reduce_scatter | solution.py:647
  767.9 163.8 %all-to-all-start.7 = ((bf16[16,2,64,1024]{3,2,1,0:T(8,128)(2,1)}), bf16[16,2,64,1024]{3,2,1,0:T(8,128)(2,1)}, u32[]{:S(2)}, u32[]{:S(2)}) async-start(bf16[16,2,64,1024]{3,2,1,0:T(8,128)(2,1)} %get-tuple-element.131), calls=%async_computation.7 | async-start | bytes 8388608 | tf_op jit(solution)/shard_map/all_to_all | solution.py:571
  773.7 228.4 %reduce-scatter.8.cloned.1.call-start = ((), (), s32[]{:S(2)}) async-start(), calls=%async_computation.17 | async-start | bytes 2228224 | tf_op jit(solution)/shard_map/reduce_scatter | solution.py:647
  777.7 282.9 %all-gather.4.cloned.1.call-start = ((), (), s32[]{:S(2)}) async-start(), calls=%async_computation.14 | async-start | bytes 1114112 | tf_op jit(solution)/shard_map/all_gather | solution.py:652
  855.6 246.4 %all-gather.6.cloned.1.call-start = ((), (), s32[]{:S(2)}) async-start(), calls=%async_computation.16 | async-start | bytes 2228224 | tf_op jit(solution)/shard_map/all_gather | solution.py:652
  931.8 74.7 %all-to-all-start.8 = ((bf16[16,1,64,1024]{3,2,1,0:T(8,128)(2,1)}), bf16[16,1,64,1024]{3,2,1,0:T(8,128)(2,1)S(1)}, u32[]{:S(2)}, u32[]{:S(2)}) async-start(bf16[16,1,64,1024]{3,2,1,0:T(8,128)(2,1)} %bitcast.103), calls=%async_computation.8 | async-start | bytes 4194304 | tf_op jit(solution)/shard_map/all_to_all | solution.py:571
  935.5 208.7 %all-gather.8.cloned.1.call-start = ((), (), s32[]{:S(2)}) async-start(), calls=%async_computation.18 | async-start | bytes 2228224 | tf_op jit(solution)/shard_map/all_gather | solution.py:652
  1006.5 142.4 %all-to-all-start.9 = ((bf16[16,1,64,1024]{3,2,1,0:T(8,128)(2,1)}), bf16[16,1,64,1024]{3,2,1,0:T(8,128)(2,1)}, u32[]{:S(2)}, u32[]{:S(2)}) async-start(bf16[16,1,64,1024]{3,2,1,0:T(8,128)(2,1)} %bitcast.100), calls=%async_computation.9 | async-start | bytes 4194304 | tf_op jit(solution)/shard_map/all_to_all | solution.py:571
  (35 other events, 473.8 us)
Sparse Core Ops, SparseCore 0:
  763.9 91.5 reduce-scatter.3
  859.3 68.0 reduce-scatter.5
  931.1 70.9 reduce-scatter.7
  1004.1 56.5 all-gather.3
  1062.7 39.2 all-gather.5
  1104.0 40.1 all-gather.7

commit v3 on v2

--- a/solution.py
+++ b/solution.py
@@ -204,11 +204,13 @@
     for n, out in enumerate(outs):
         _, _, height, cols = out.shape
         count = size // height
-        for group in range(span // rows):
-            start = n * span + group * rows
-            piece = scratch[:, start : start + rows, :].reshape(size, cols)
+
+        @pl.loop(0, span // rows)
+        def _(group, n=n, out=out):
+            start = pl.multiple_of(n * span + group * rows, rows)
+            piece = scratch[:, pl.ds(start, rows), :].reshape(size, cols)
             value = dot(swap, piece).astype(BF)
-            out[group * count : (group + 1) * count, 0] = value.reshape(count, height, cols)
+            out[pl.ds(group * count, count), 0] = value.reshape(count, height, cols)
 
 
 def first_stage(chunks, places, seq, x3, mix_first, twiddle, cols=256):
@@ -278,6 +280,27 @@
     return [jnp.concatenate([a, b], axis=1).astype(BF) for a, b in zip(own, recv)]
 
 
+def offset_call(kernel, chunk, steps, in_specs, out_specs, out_shape, aliases=None, scratch=()):
+    call = pl.pallas_call(
+        lambda _, *refs: kernel(*refs),
+        grid_spec=pltpu.PrefetchScalarGridSpec(
+            num_scalar_prefetch=1,
+            grid=(steps,),
+            in_specs=in_specs,
+            out_specs=out_specs,
+            scratch_shapes=scratch,
+        ),
+        out_shape=out_shape,
+        input_output_aliases={k + 1: v for k, v in (aliases or {}).items()},
+        compiler_params=params(0),
+    )
+    return functools.partial(call, jnp.stack([jnp.int32(v) for v in chunk]))
+
+
+def natural_block(rows, steps, channels):
+    return pl.BlockSpec((rows, rows, channels), lambda s, chunk: (0, chunk[0] * steps + s, 0))
+
+
 def back_kernel(g_ref, w_ref, own_ref, send_ref):
     rows, cols, channels = g_ref.shape
     grad = g_ref[...].reshape(rows * cols, channels)
@@ -286,20 +309,16 @@
     spread_store(values, own_ref, send_ref)
 
 
-def back_stage(chunk, g3, down_second):
+def back_stage(g3, down_second):
     rows, length, channels = g3.shape
     size = rows * rows
-    steps = length // CHUNKS // rows
     blocks = down_second.shape[0]
-    shape = jax.ShapeDtypeStruct((blocks, steps * size, LANES), BF)
+    shape = jax.ShapeDtypeStruct((blocks, rows * length, LANES), BF)
     spec = pl.BlockSpec((blocks, size, LANES), lambda s: (0, s, 0))
     return pl.pallas_call(
         back_kernel,
-        grid=(steps,),
-        in_specs=[
-            pl.BlockSpec((rows, rows, channels), lambda s: (0, chunk * steps + s, 0)),
-            full(down_second.shape),
-        ],
+        grid=(length // rows,),
+        in_specs=[pl.BlockSpec((rows, rows, channels), lambda s: (0, s, 0)), full(down_second.shape)],
         out_specs=[spec, spec],
         out_shape=[shape, shape],
         compiler_params=params(0),
@@ -307,21 +326,28 @@
     )(g3, down_second)
 
 
-def hidden_kernel(x_ref, m_ref, w_ref, h_ref, own_ref, send_ref):
-    rows, cols, channels = x_ref.shape
-    mixed = dot(swap_rows(rows), m_ref[...].reshape(rows * cols, channels))
-    inputs = x_ref[...].reshape(rows * cols, channels).astype(F32)
-    hidden = (inputs + jax.nn.sigmoid(inputs) * mixed).astype(BF)
-    h_ref[...] = hidden
+def hidden_kernel(x_ref, m_ref, w_ref, h_ref, own_ref, send_ref, mids):
+    rows, cols, _ = x_ref.shape
+    size = rows * cols
     blocks, width = w_ref.shape[0], w_ref.shape[1]
-    values = [dot(hidden[:, k * width : (k + 1) * width], w_ref[k]) for k in range(blocks)]
-    spread_store(values, own_ref, send_ref)
+    swap = swap_rows(rows)
+
+    @pl.loop(0, blocks)
+    def _(k):
+        part = pl.ds(pl.multiple_of(k * width, width), width)
+        mixed = dot(swap, m_ref[:, :, part].reshape(size, width))
+        inputs = x_ref[:, :, part].reshape(size, width).astype(F32)
+        hidden = (inputs + jax.nn.sigmoid(inputs) * mixed).astype(BF)
+        h_ref[:, part] = hidden
+        mids[k] = dot(hidden, w_ref[k])
+
+    spread_store([mids[k] for k in range(blocks)], own_ref, send_ref)
 
 
 def arriving(field, size):
     source, part = field
     height, channels = source.shape[2:]
-    return pl.BlockSpec((size // height, None, height, channels), lambda s: (s, part, 0, 0))
+    return pl.BlockSpec((size // height, None, height, channels), lambda s, *_: (s, part, 0, 0))
 
 
 def hidden_stage(chunk, x3, mixed, up_first):
@@ -329,112 +355,113 @@
     size = rows * rows
     steps = length // CHUNKS // rows
     blocks = up_first.shape[0]
-    part = pl.BlockSpec((blocks, size, LANES), lambda s: (0, s, 0))
-    return pl.pallas_call(
+    part = pl.BlockSpec((blocks, size, LANES), lambda s, _: (0, s, 0))
+    return offset_call(
         hidden_kernel,
-        grid=(steps,),
-        in_specs=[
-            pl.BlockSpec((rows, rows, channels), lambda s: (0, chunk * steps + s, 0)),
-            arriving(mixed, size),
-            full(up_first.shape),
-        ],
-        out_specs=[pl.BlockSpec((size, channels), lambda s: (s, 0)), part, part],
-        out_shape=[
+        (chunk,),
+        steps,
+        [natural_block(rows, steps, channels), arriving(mixed, size), full(up_first.shape)],
+        [pl.BlockSpec((size, channels), lambda s, _: (s, 0)), part, part],
+        [
             jax.ShapeDtypeStruct((steps * size, channels), BF),
             jax.ShapeDtypeStruct((blocks, steps * size, LANES), BF),
             in_hbm((blocks, steps * size, LANES)),
         ],
-        compiler_params=params(0),
-        name="hidden",
+        scratch=[pltpu.VMEM((blocks, size, 2 * LANES), F32)],
     )(x3, mixed[0], up_first)
 
 
-def middle_kernel(fresh, cols, *refs):
-    uo, ur, bo, br, us, df = refs[:6]
-    refs = refs[6:]
-    if not fresh:
-        sus_in, sdf_in = refs[:2]
-        refs = refs[2:]
-    down_own, down_send, grad_own, grad_send, sus, sdf = refs
+def middle_kernel(cols, *refs):
+    uo, ur, bo, br, us, df, sus_in, sdf_in = refs[:8]
+    down_own, down_send, grad_own, grad_send, sus, sdf, down_sum, grad_sum = refs[8:]
     start = pl.program_id(1) == 0
 
     @pl.when(start)
     def _():
-        if fresh:
-            sus[...] = jnp.zeros(sus.shape, F32)
-            sdf[...] = jnp.zeros(sdf.shape, F32)
-        else:
-            sus[...] = sus_in[...]
-            sdf[...] = sdf_in[...]
+        sus[...] = sus_in[...]
+        sdf[...] = sdf_in[...]
 
     up = jnp.concatenate([uo[0], ur[0]], axis=1)
     back = jnp.concatenate([bo[0], br[0]], axis=1)
     hidden_units = us.shape[2]
-    down = None
-    grad = None
-    for low in range(0, hidden_units, cols):
-        part = slice(low, low + cols)
-        z = dot(up, us[0, :, part])
-        z2 = z * z
-        h = 0.5 + 0.5 * jnp.tanh(z * (root_two_pi + (root_two_pi * cubic_term) * z2))
-        act = (z * h).astype(BF)
-        slope = h + (h - h * h) * (
-            z * (2.0 * root_two_pi + (6.0 * root_two_pi * cubic_term) * z2)
-        )
-        pre = (dot_nt(back, df[0, part, :]) * slope).astype(BF)
-        step = dot(act, df[0, part, :])
-        down = step if down is None else down + step
-        step = dot_nt(pre, us[0, :, part])
-        grad = step if grad is None else grad + step
-        sdf[0, part, :] += dot_tn(act, back)
-        sus[0, :, part] += dot_tn(up, pre)
+    down_sum[...] = jnp.zeros(down_sum.shape, F32)
+    grad_sum[...] = jnp.zeros(grad_sum.shape, F32)
+
+    @pl.loop(0, hidden_units // (2 * cols))
+    def _(pair):
+        down, grad = None, None
+        for side in range(2):
+            part = pl.ds(pl.multiple_of((2 * pair + side) * cols, cols), cols)
+            z = dot(up, us[0, :, part])
+            z2 = z * z
+            h = 0.5 + 0.5 * jnp.tanh(z * (root_two_pi + (root_two_pi * cubic_term) * z2))
+            act = (z * h).astype(BF)
+            slope = h + (h - h * h) * (
+                z * (2.0 * root_two_pi + (6.0 * root_two_pi * cubic_term) * z2)
+            )
+            pre = (dot_nt(back, df[0, part, :]) * slope).astype(BF)
+            step = dot(act, df[0, part, :])
+            down = step if down is None else down + step
+            step = dot_nt(pre, us[0, :, part])
+            grad = step if grad is None else grad + step
+            sdf[0, part, :] += dot_tn(act, back)
+            sus[0, :, part] += dot_tn(up, pre)
+        down_sum[...] += down
+        grad_sum[...] += grad
+
+    down, grad = down_sum[...], grad_sum[...]
     down_own[0] = down[:, :LANES].astype(BF)
     down_send[0] = down[:, LANES:].astype(BF)
     grad_own[0] = grad[:, :LANES].astype(BF)
     grad_send[0] = grad[:, LANES:].astype(BF)
 
 
-def middle_stage(up_own, up_recv, back_own, back_recv, up_second, down_first, sums, tile=512, cols=256):
+def middle_stage(chunk, up_own, up_recv, back_own, back_recv, up_second, down_first, sums, tile=512, cols=256):
     blocks, count, _ = up_own.shape
     steps = count // tile
     part = pl.BlockSpec((1, tile, LANES), lambda g, t: (g, t, 0))
+    shifted = pl.BlockSpec((1, tile, LANES), lambda g, t: (g, chunk * steps + t, 0))
     us_spec = pl.BlockSpec((1,) + up_second.shape[1:], lambda g, t: (g, 0, 0))
     df_spec = pl.BlockSpec((1,) + down_first.shape[1:], lambda g, t: (g, 0, 0))
-    fresh = sums is None
     shape = jax.ShapeDtypeStruct(up_own.shape, BF)
     return pl.pallas_call(
-        functools.partial(middle_kernel, fresh, cols),
+        functools.partial(middle_kernel, cols),
         grid=(blocks, steps),
-        in_specs=[part, part, part, part, us_spec, df_spec] + ([] if fresh else [us_spec, df_spec]),
+        in_specs=[part, part, shifted, shifted, us_spec, df_spec, us_spec, df_spec],
         out_specs=[part] * 4 + [us_spec, df_spec],
         out_shape=[shape] * 4
         + [jax.ShapeDtypeStruct(up_second.shape, F32), jax.ShapeDtypeStruct(down_first.shape, F32)],
-        input_output_aliases={} if fresh else {6: 4, 7: 5},
+        scratch_shapes=[pltpu.VMEM((tile, 2 * LANES), F32)] * 2,
+        input_output_aliases={6: 4, 7: 5},
         compiler_params=params(0, 0),
         name="middle",
-    )(up_own, up_recv, back_own, back_recv, up_second, down_first, *(() if fresh else sums))
-
-
-def input_kernel(fresh, *refs):
-    x_ref, g_ref, m_ref, h_ref, go, gr, w_ref = refs[:7]
-    send_ref, base_ref, suf = refs[-3:]
+    )(up_own, up_recv, back_own, back_recv, up_second, down_first, *sums)
+
+
+def input_kernel(*refs):
+    x_ref, g_ref, m_ref, h_ref, go, gr, w_ref, suf_in = refs[:8]
+    send_ref, base_ref, suf, mids = refs[-4:]
 
     @pl.when(pl.program_id(0) == 0)
     def _():
-        suf[...] = jnp.zeros(suf.shape, F32) if fresh else refs[7][...]
-
-    rows, cols, channels = x_ref.shape
+        suf[...] = suf_in[...]
+
+    rows, cols, _ = x_ref.shape
     size = rows * cols
     swap = swap_rows(rows)
     width = w_ref.shape[1]
-    mids = gather_load(go, gr)
-    x3, g3 = x_ref[...].reshape(size, channels), g_ref[...].reshape(size, channels)
-    for k, mid in enumerate(mids):
-        part = slice(k * width, (k + 1) * width)
+    for k, mid in enumerate(gather_load(go, gr)):
+        mids[k] = mid
+
+    @pl.loop(0, w_ref.shape[0])
+    def _(k):
+        part = pl.ds(pl.multiple_of(k * width, width), width)
+        mid = mids[k]
         inner = dot_nt(mid, w_ref[k])
         suf[k] += dot_tn(h_ref[:, part], mid)
-        grad = (g3[:, part].astype(F32) + inner).astype(BF).astype(F32)
-        gating = jax.nn.sigmoid(x3[:, part].astype(F32))
+        grad = g_ref[:, :, part].reshape(size, width).astype(F32) + inner
+        grad = grad.astype(BF).astype(F32)
+        gating = jax.nn.sigmoid(x_ref[:, :, part].reshape(size, width).astype(F32))
         mixed = dot(swap, m_ref[:, :, part].reshape(size, width))
         send = dot(swap, (grad * gating).astype(BF)).astype(BF)
         send_ref[:, :, part] = send.reshape(send_ref.shape[0], send_ref.shape[1], width)
@@ -446,34 +473,30 @@
     size = rows * rows
     steps = length // CHUNKS // rows
     blocks = up_first.shape[0]
-    natural = pl.BlockSpec((rows, rows, channels), lambda s: (0, chunk * steps + s, 0))
-    flat = pl.BlockSpec((size, channels), lambda s: (s, 0))
-    half = pl.BlockSpec((blocks, size, LANES), lambda s: (0, s, 0))
-    fresh = sums is None
+    flat = pl.BlockSpec((size, channels), lambda s, _: (s, 0))
+    half = pl.BlockSpec((blocks, size, LANES), lambda s, _: (0, s, 0))
+    natural = natural_block(rows, steps, channels)
     wspec = full(up_first.shape)
     seq, _, height, _ = mixed[0].shape
     part, parts = place
-    extra = [] if fresh else [(sums, wspec, 2)]
-    if buffer is not None:
-        extra.append((buffer, pl.BlockSpec(memory_space=pl.ANY), 0))
-    return pl.pallas_call(
-        functools.partial(input_kernel, fresh),
-        grid=(steps,),
-        in_specs=[natural, natural, arriving(mixed, size), flat, half, half, wspec] + [e[1] for e in extra],
-        out_specs=[
-            pl.BlockSpec((size // height, None, height, channels), lambda s: (s, part, 0, 0)),
+    return offset_call(
+        input_kernel,
+        (chunk, part),
+        steps,
+        [natural, natural, arriving(mixed, size), flat, half, half, wspec, wspec, pl.BlockSpec(memory_space=pl.ANY)],
+        [
+            pl.BlockSpec((size // height, None, height, channels), lambda s, at: (s, at[1], 0, 0)),
             flat,
             wspec,
         ],
-        out_shape=[
+        [
             in_hbm((seq, parts, height, channels)),
             jax.ShapeDtypeStruct((steps * size, channels), BF),
             jax.ShapeDtypeStruct(up_first.shape, F32),
         ],
-        input_output_aliases={7 + i: e[2] for i, e in enumerate(extra)},
-        compiler_params=params(0),
-        name="inputs",
-    )(x3, g3, mixed[0], hidden, grad_own, grad_recv, up_first, *[e[0] for e in extra])
+        {7: 2, 8: 0},
+        [pltpu.VMEM((blocks, size, 2 * LANES), BF)],
+    )(x3, g3, mixed[0], hidden, grad_own, grad_recv, up_first, sums, buffer)
 
 
 def output_kernel(fresh, *refs):
@@ -482,21 +505,25 @@
     if not fresh:
         sds_in = refs[0]
         refs = refs[2:]
-    o_ref, sds = refs
+    o_ref, sds, perms = refs
 
     @pl.when(pl.program_id(0) == 0)
     def _():
         sds[...] = jnp.zeros(sds.shape, F32) if fresh else sds_in[...]
 
-    rows, cols, channels = g_ref.shape
+    rows, cols, _ = g_ref.shape
     size = rows * cols
     width = w_ref.shape[2]
-    g3 = g_ref[...].reshape(size, channels)
     for h, perm in enumerate(gather_load(do, dr)):
-        part = slice(h * width, (h + 1) * width)
+        perms[h] = perm
+
+    @pl.loop(0, w_ref.shape[0])
+    def _(h):
+        part = pl.ds(pl.multiple_of(h * width, width), width)
+        perm = perms[h]
         value = h_ref[:, part].astype(F32) + dot(perm, w_ref[h])
         o_ref[:, :, part] = value.astype(BF).reshape(rows, cols, width)
-        sds[h] += dot_tn(perm, g3[:, part])
+        sds[h] += dot_tn(perm, g_ref[:, :, part].reshape(size, width))
 
 
 def output_stage(chunk, g3, hidden, down_own, down_recv, down_second, sums, output):
@@ -504,24 +531,20 @@
     size = rows * rows
     steps = length // CHUNKS // rows
     blocks = down_second.shape[0]
-    natural = pl.BlockSpec((rows, rows, channels), lambda s: (0, chunk * steps + s, 0))
-    flat = pl.BlockSpec((size, channels), lambda s: (s, 0))
-    part = pl.BlockSpec((blocks, size, LANES), lambda s: (0, s, 0))
+    flat = pl.BlockSpec((size, channels), lambda s, _: (s, 0))
+    part = pl.BlockSpec((blocks, size, LANES), lambda s, _: (0, s, 0))
+    natural = natural_block(rows, steps, channels)
     fresh = sums is None
     wspec = full(down_second.shape)
-    return pl.pallas_call(
+    return offset_call(
         functools.partial(output_kernel, fresh),
-        grid=(steps,),
-        in_specs=[natural, flat, part, part, wspec]
-        + ([] if fresh else [wspec, pl.BlockSpec(memory_space=pl.ANY)]),
-        out_specs=[natural, wspec],
-        out_shape=[
-            jax.ShapeDtypeStruct(g3.shape, BF),
-            jax.ShapeDtypeStruct(down_second.shape, F32),
-        ],
-        input_output_aliases={} if fresh else {5: 1, 6: 0},
-        compiler_params=params(0),
-        name="outputs",
+        (chunk,),
+        steps,
+        [natural, flat, part, part, wspec] + ([] if fresh else [wspec, pl.BlockSpec(memory_space=pl.ANY)]),
+        [natural, wspec],
+        [jax.ShapeDtypeStruct(g3.shape, BF), jax.ShapeDtypeStruct(down_second.shape, F32)],
+        {} if fresh else {5: 1, 6: 0},
+        [pltpu.VMEM((blocks, size, 2 * LANES), BF)],
     )(g3, hidden, down_own, down_recv, down_second, *(() if fresh else (sums, output)))
 
 
@@ -567,6 +590,120 @@
     )(mix_first, tw_cols, *[f for f, _ in fields], *bases)
 
 
+def group_matrix(mine, width, blocks):
+    stride = width // NBLK
+    out = lax.broadcasted_iota(jnp.int32, (width, width), 0)
+    inp = lax.broadcasted_iota(jnp.int32, (width, width), 1)
+    k = inp % NBLK
+    half = k // blocks
+    half = half + mine - 2 * half * mine
+    target = half * LANES + (k % blocks) * stride + inp // NBLK
+    return jnp.where(out == target, 1.0, 0.0).astype(BF)
+
+
+def copy_halves(mine, source, targets):
+    for own in range(2):
+
+        @pl.when(mine == own)
+        def _():
+            for get, put, kind in zip(source, targets, [t[0].dtype for t in targets]):
+                value = get()
+                low, high = value[..., :LANES], value[..., LANES:]
+                ref, index = put
+                ref[(*index, slice(0, LANES))] = (high if own else low).astype(kind)
+                ref[(*index, slice(LANES, 2 * LANES))] = (low if own else high).astype(kind)
+
+
+def prepare_kernel(mine_ref, uf, us, df, ds, uf_out, us_out, df_out, ds_out, *sums):
+    for ref in sums:
+        ref[...] = jnp.zeros(ref.shape, F32)
+    mine = mine_ref[0]
+    matrix = group_matrix(mine, ds.shape[1], NBLK // 2)
+    copy_halves(mine, (lambda: uf[0], lambda: df[0]), ((uf_out, (0, slice(None))), (df_out, (0, slice(None)))))
+    us_out[0] = dot(matrix, us[0]).astype(BF)
+    ds_out[0] = dot(matrix, ds[0]).astype(BF)
+
+
+def by_block(array):
+    return pl.BlockSpec((1,) + array.shape[1:], lambda g, *_: (g, 0, 0))
+
+
+def prepare_stage(mine, weights):
+    specs = [by_block(w) for w in weights]
+    return pl.pallas_call(
+        prepare_kernel,
+        grid_spec=pltpu.PrefetchScalarGridSpec(
+            num_scalar_prefetch=1,
+            grid=(weights[0].shape[0],),
+            in_specs=specs,
+            out_specs=specs + specs[:3],
+        ),
+        out_shape=[jax.ShapeDtypeStruct(w.shape, BF) for w in weights]
+        + [jax.ShapeDtypeStruct(w.shape, F32) for w in weights[:3]],
+        compiler_params=params(0),
+        name="prepare",
+    )(mine, *weights)
+
+
+def collect_kernel(scale, sus, sdf, suf, sds, out):
+    width = suf.shape[1]
+    row = 0
+    pieces = [sus[0, :, low : low + width] for low in range(0, sus.shape[2], width)]
+    pieces += [sdf[0], suf[0], sds[0]]
+    for piece in pieces:
+        out[0, row : row + piece.shape[0], :] = (piece * scale).astype(BF)
+        row += piece.shape[0]
+
+
+def collect_stage(scale, sums):
+    blocks, width = sums[2].shape[:2]
+    height = sum(v.shape[1] * v.shape[2] for v in sums) // width
+    return pl.pallas_call(
+        functools.partial(collect_kernel, scale),
+        grid=(blocks,),
+        in_specs=[by_block(v) for v in sums],
+        out_specs=pl.BlockSpec((1, height, width), lambda g: (g, 0, 0)),
+        out_shape=jax.ShapeDtypeStruct((blocks, height, width), BF),
+        compiler_params=params(0),
+        name="collect",
+    )(*sums)
+
+
+def finish_kernel(mine_ref, whole, uf, us, df, ds):
+    mine = mine_ref[0]
+    width = ds.shape[1]
+    matrix = group_matrix(mine, width, NBLK // 2)
+    row = us.shape[2] // width * width
+
+    @pl.loop(0, us.shape[2] // width)
+    def _(n):
+        here = pl.ds(pl.multiple_of(n * width, width), width)
+        us[0, :, here] = dot_tn(matrix, whole[0, here, :])
+
+    tall = df.shape[1]
+    down, up = whole.at[0, row : row + tall, :], whole.at[0, row + tall : row + tall + width, :]
+    copy_halves(
+        mine,
+        (lambda: down[...], lambda: up[...]),
+        ((df, (0, slice(None))), (uf, (0, slice(None)))),
+    )
+    row += tall + width
+    ds[0] = dot_tn(matrix, whole[0, row : row + width, :])
+
+
+def finish_stage(mine, whole, weights):
+    specs = [by_block(w) for w in weights]
+    return pl.pallas_call(
+        finish_kernel,
+        grid_spec=pltpu.PrefetchScalarGridSpec(
+            num_scalar_prefetch=1, grid=(whole.shape[0],), in_specs=[by_block(whole)], out_specs=specs
+        ),
+        out_shape=[jax.ShapeDtypeStruct(w.shape, F32) for w in weights],
+        compiler_params=params(0),
+        name="finish",
+    )(mine, whole)
+
+
 def exchange(field):
     return lax.all_to_all(field, "seq", split_axis=0, concat_axis=0, tiled=True)
 
@@ -576,17 +713,21 @@
 
 
 PLAN = (
-    (((1, 0),), (("first", 1), ("back", 0), ("back", 1), ("back", 2), ("back", 3))),
+    (((1, 0),), (("first", 1), ("prepare", 0), ("back", 0))),
     (((1, 1),), (("second", 0),)),
     (((2, 0), (1, 2)), (("second", 1),)),
     (((2, 1), (1, 3)), (("hidden", 0), ("second", 2), ("middle", 0), ("inputs", 0))),
     (((2, 2), (3, 0)), (("hidden", 1), ("second", 3), ("middle", 1), ("outputs", 0), ("inputs", 1))),
     (((2, 3), (3, 1)), (("hidden", 2), ("fourth", 0), ("middle", 2), ("outputs", 1), ("inputs", 2))),
     (((3, 2), (4, 0)), (("hidden", 3), ("fourth", 1), ("middle", 3), ("outputs", 2), ("inputs", 3))),
-    (((3, 3), (4, 1)), (("fourth", 2), ("outputs", 3))),
+    (((3, 3), (4, 1)), (("fourth", 2), ("outputs", 3), ("collect", 0))),
     (((4, 2),), (("fourth", 3),)),
-    (((4, 3),), ()),
+    (((4, 3),), (("finish", 0),)),
 )
+
+
+def tie(value, others):
+    return lax.optimization_barrier((value, others))[0]
 
 
 def chunked_shards(
@@ -603,26 +744,12 @@
 ):
     local_rows, channels = activations.shape
     rows, length = twiddle.shape
-    blocks, width = up_first.shape[0], up_first.shape[1]
-    stride = width // NBLK
-    mine = lax.axis_index("fsdp")
-
-    def own_first(values, axis):
-        return jnp.where(mine == 0, values, jnp.roll(values, LANES, axis))
-
-    def group_rows(weight):
-        shaped = weight.reshape(blocks, stride, NBLK, weight.shape[2])
-        return own_first(jnp.transpose(shaped, (0, 2, 1, 3)).reshape(weight.shape), 1)
-
-    def ungroup_rows(weight):
-        shaped = own_first(weight, 1).reshape(blocks, NBLK, stride, weight.shape[2])
-        return jnp.transpose(shaped, (0, 2, 1, 3)).reshape(weight.shape)
+    mine = lax.axis_index("fsdp").astype(jnp.int32).reshape(1)
+    weights = (up_first, up_second, down_first, down_second)
 
     x3 = activations.reshape(rows, length, channels)
     g3 = grad_out.reshape(rows, length, channels)
     w2, w2t = mix_second, mix_second.T
-    ups_first, downs_first = own_first(up_first, 2), own_first(down_first, 2)
-    ups_second, downs_second = group_rows(up_second), group_rows(down_second)
     tw_cols = jnp.transpose(twiddle.reshape(rows, length // rows, rows), (0, 2, 1)).reshape(
         rows * rows, length // rows
     )
@@ -632,7 +759,8 @@
         for part, key in enumerate(travels):
             place[key] = (slot, part, len(travels))
     buffers, arrived, kept = {}, {}, {}
-    sums, sum_first, sum_last, output = None, None, None, None
+    halves = [list(range(seq // 2)), list(range(seq // 2, seq))]
+    sum_last, output = None, None
 
     def spot(key):
         slot, part, parts = place[key]
@@ -643,15 +771,8 @@
         for m, sent in zip(chunks, results):
             buffers[place[1, m][0]] = sent
 
-    def reduced(values):
-        return lax.psum_scatter(
-            (values * (1.0 / length)).astype(BF), "seq", scatter_dimension=0, tiled=True
-        )
-
-    def gathered(values):
-        return lax.all_gather(values, "seq", axis=0, tiled=True)
-
     first((0,))
+    ups_first, ups_second, downs_first, downs_second, sum_first, *sums = prepare_stage(mine, weights)
     for slot, (travels, tasks) in enumerate(PLAN):
         done = exchange(buffers[slot])
         for part, key in enumerate(travels):
@@ -660,8 +781,8 @@
             if name == "first":
                 first(tuple(range(1, CHUNKS)))
             elif name == "back":
-                own, send = back_stage(n, g3, downs_second)
-                kept["back", n] = (own, partner(send))
+                own, send = back_stage(g3, downs_second)
+                back = (own, partner(send))
             elif name == "second":
                 buffers[place[2, n][0]] = second_stage(w2t, arrived[1, n], *spot((2, n)), rows)
             elif name == "hidden":
@@ -670,7 +791,7 @@
                 kept["up", n] = (own, partner(send))
             elif name == "middle":
                 down_own, down_send, grad_own, grad_send, *sums = middle_stage(
-                    *kept["up", n], *kept["back", n], ups_second, downs_first, sums
+                    n, *kept["up", n], *back, ups_second, downs_first, sums
                 )
                 kept["grad", n] = (grad_own, partner(grad_send))
                 kept["down", n] = (down_own, partner(down_send))
@@ -690,22 +811,23 @@
                 output, sum_last = output_stage(
                     n, g3, kept["hidden", n], *kept["down", n], downs_second, sum_last, output
                 )
-            else:
+            elif name == "fourth":
                 buffers[place[4, n][0]] = second_stage(w2, arrived[3, n], *spot((4, n)), rows)
 
-    parts = (
-        reduced(sums[0].reshape(-1, sums[0].shape[2])),
-        reduced(sums[1].reshape(-1, width)),
-        reduced(jnp.concatenate([sum_first, sum_last], axis=0).reshape(-1, width)),
-    )
-    one, two, rest = (gathered(v) for v in parts)
-    rest = rest.astype(F32).reshape(-1, width, width)
-    grads = (
-        own_first(rest[:blocks], 2),
-        ungroup_rows(one.astype(F32).reshape(up_second.shape)),
-        own_first(two.astype(F32).reshape(down_first.shape), 2),
-        ungroup_rows(rest[blocks:]),
-    )
+    collected = collect_stage(1.0 / length, (*sums, sum_first, sum_last))
+    part = lax.psum_scatter(
+        collected.reshape(-1, collected.shape[2]),
+        "seq",
+        scatter_dimension=0,
+        axis_index_groups=halves,
+        tiled=True,
+    )
+    other = lax.ppermute(part, "seq", [(d, (d + seq // 2) % seq) for d in range(seq)])
+    other = tie(other, buffers[place[4, CHUNKS - 1][0]])
+    part = (part.astype(F32) + other.astype(F32)).astype(BF)
+    whole = lax.all_gather(part, "seq", axis=0, axis_index_groups=halves, tiled=True)
+    grads = finish_stage(mine, whole.reshape(collected.shape), weights)
+    tw_cols = tie(tw_cols, grads)
     fields = [arrived[4, n] for n in range(CHUNKS)]
     bases = [kept["base", n] for n in range(CHUNKS)]
     grad_inputs = last_stage(rows, length, mix_first, tw_cols, fields, bases)

time: 1170 us -> 1150 us (0.983)
  waiting for transfers between devices: 728 us -> 581 us
  Pallas kernels: 272 us -> 351 us
  blocking collectives: 0 us -> 62.2 us
  other arithmetic: 24.4 us -> 1 us
  starting transfers between devices: 100 us -> 115 us
    all_gather x3 -> x1, waiting for transfers between devices: 119 us -> 0.01 us  [chunked_shards(): lax.all_gather(part, 'seq', axis=0, axis_index_groups=halves, tiled=True)]
    reduce_scatter x3 -> x1, waiting for transfers between devices: 216 us -> 102 us  [chunked_shards(): lax.psum_scatter(collected.reshape(-1, collected.shape[2]), 'seq', scatte...]
    all_to_all x10 -> x9, waiting for transfers between devices: 142 us -> 233 us  [exchange(): return lax.all_to_all(field, 'seq', split_axis=0, concat_axis=0, tiled=True)]
    pallas_call x20, Pallas kernels: 210 us -> 281 us  [the longest x4 113 us: middle_stage(): pl.pallas_call(functools.partial(middle_kernel, cols), grid=(blocks, step...]
    all_to_all x0 -> x1, blocking collectives: none -> 62.2 us  [exchange(): return lax.all_to_all(field, 'seq', split_axis=0, concat_axis=0, tiled=True)]
    ppermute x16 -> x13, waiting for transfers between devices: 251 us -> 225 us  [partner(): return lax.ppermute(values, 'fsdp', [(0, 1), (1, 0)])]
    ppermute x0 -> x1, waiting for transfers between devices: none -> 21.1 us  [chunked_shards(): lax.ppermute(part, 'seq', [(d, (d + seq // 2) % seq) for d in range(seq)])]
    all_to_all x10 -> x9, starting transfers between devices: 80.8 us -> 89.5 us  [exchange(): return lax.all_to_all(field, 'seq', split_axis=0, concat_axis=0, tiled=True)]
  transfers between devices with their start and end apart: 32 -> 25, of which waited for: 24 -> 17; matrix products, arithmetic and copies ran while one was open for 3% -> 0% of each run, Pallas kernels for 22% -> 28%
where the time goes in v3:
time: 1150 us; the launch traced here: 1140 us
  waiting for transfers between devices  581 us (51%)
  Pallas kernels  351 us (31%)
  starting transfers between devices  115 us (10%)
  blocking collectives  62.2 us (5%)
  local copies, waits for them, and re-layouts  17.3 us (2%)
  between operations  14.3 us (1%)
    all_to_all x9, waiting for transfers between devices, exchange(): return lax.all_to_all(field, 'seq', split_axis=0, concat_axis=0, tiled=True)  233 us
    ppermute x13, waiting for transfers between devices, partner(): return lax.ppermute(values, 'fsdp', [(0, 1), (1, 0)])  225 us
    pallas_call x4, Pallas kernels, middle_stage(): pl.pallas_call(functools.partial(middle_kernel, cols), grid=(blocks, step...  113 us
    reduce_scatter x1, waiting for transfers between devices, chunked_shards(): lax.psum_scatter(collected.reshape(-1, collected.shape[2]), 'seq', scatte...  102 us
    all_to_all x9, starting transfers between devices, exchange(): return lax.all_to_all(field, 'seq', split_axis=0, concat_axis=0, tiled=True)  89.5 us
    all_to_all x1, blocking collectives, exchange(): return lax.all_to_all(field, 'seq', split_axis=0, concat_axis=0, tiled=True)  62.2 us
    pallas_call x4, Pallas kernels, input_stage(): offset_call(input_kernel, (chunk, part), steps, [natural, natural, arrivi...  55.6 us
    pallas_call x4, Pallas kernels, hidden_stage(): offset_call(hidden_kernel, (chunk,), steps, [natural_block(rows, steps, c...  38.4 us
  transfers between devices with their start and end apart: 25, of which 17 were waited for; matrix products, arithmetic and copies ran while one was open for 0% of the time, Pallas kernels for 28%

profile of v3, /device:TPU:0, one launch (start us, length us, event | category | flops | bytes accessed | tf_op | source)
XLA Modules:
  0.0 1141.6 jit_solution(9180834100286001638)
XLA Ops:
  22.8 14.9 %first.2 = (bf16[16,1,64,1024]{3,2,1,0:T(8,128)(2,1)}, bf16[16,2,64,1024]{3,2,1,0:T(8,128)(2,1)}, bf16[16,2,64,1024]{3,2,1,0:T(8,128)(2,1)}) custom-call(bf16[16,256,1024]{2,1,0:T(8,128)(2,1)} %bitcast.30, bf16[256,256]{1,0:T(8,128)(2,1)} %w_ref.13, f32[16,256]{1,0:T(8,128)} %tw_ref.3), custom_call_target="tpu_custom_call" | custom-call | tf_op jit(solution)/shard_map/first/pallas_call | solution.py:220
  37.7 26.1 %all-to-all-done.2 = bf16[16,1,64,1024]{3,2,1,0:T(8,128)(2,1)S(1)} async-done(((bf16[16,1,64,1024]{3,2,1,0:T(8,128)(2,1)}), bf16[16,1,64,1024]{3,2,1,0:T(8,128)(2,1)S(1)}, u32[]{:S(2)}, u32[]{:S(2)}) %all-to-all-start.2) | async-done | bytes 2097184 | tf_op jit(solution)/shard_map/all_to_all | solution.py:708
  81.4 35.9 %all-to-all-done = bf16[16,1,64,1024]{3,2,1,0:T(8,128)(2,1)S(1)} async-done(((bf16[16,1,64,1024]{3,2,1,0:T(8,128)(2,1)}), bf16[16,1,64,1024]{3,2,1,0:T(8,128)(2,1)S(1)}, u32[]{:S(2)}, u32[]{:S(2)}) %all-to-all-start) | async-done | bytes 2097184 | tf_op jit(solution)/shard_map/all_to_all | solution.py:708
  134.2 73.2 %all-to-all-done.3.refs_1_.refs_2_ = bf16[16,2,64,1024]{3,2,1,0:T(8,128)(2,1)} async-done(((bf16[16,2,64,1024]{3,2,1,0:T(8,128)(2,1)}), bf16[16,2,64,1024]{3,2,1,0:T(8,128)(2,1)}, u32[]{:S(2)}, u32[]{:S(2)}) %all-to-all-start.3) | async-done | bytes 4194336 | tf_op jit(solution)/shard_map/all_to_all | solution.py:708
  207.4 19.7 %all-to-all-start.1 = ((bf16[16,2,64,1024]{3,2,1,0:T(8,128)(2,1)}), bf16[16,2,64,1024]{3,2,1,0:T(8,128)(2,1)}, u32[]{:S(2)}, u32[]{:S(2)}) async-start(bf16[16,2,64,1024]{3,2,1,0:T(8,128)(2,1)} %bitcast.55), calls=%async_computation.1 | async-start | bytes 8388608 | tf_op jit(solution)/shard_map/all_to_all | solution.py:708
  234.9 16.0 %back.1 = (bf16[4,4096,128]{2,1,0:T(8,128)(2,1)}, bf16[4,4096,128]{2,1,0:T(8,128)(2,1)}) custom-call(bf16[16,256,1024]{2,1,0:T(8,128)(2,1)} %bitcast.39, bf16[4,256,256]{2,1,0:T(8,128)(2,1)} %get-tuple-element.86.w_ref.refs_4_), custom_call_target="tpu_custom_call" | custom-call | tf_op jit(solution)/shard_map/back/pallas_call | solution.py:318
  262.5 82.1 %collective-permute-done.1.refs_3_ = bf16[4,4096,128]{2,1,0:T(8,128)(2,1)S(1)} collective-permute-done((bf16[4,4096,128]{2,1,0:T(8,128)(2,1)}, bf16[4,4096,128]{2,1,0:T(8,128)(2,1)S(1)}, u32[]{:S(2)}, u32[]{:S(2)}) %collective-permute-start.1) | collective-permute-done | bytes 4194336 | tf_op jit(solution)/shard_map/ppermute | solution.py:712
  344.5 21.8 %collective-permute-done.2.refs_1_ = bf16[4,1024,128]{2,1,0:T(8,128)(2,1)S(1)} collective-permute-done((bf16[4,1024,128]{2,1,0:T(8,128)(2,1)}, bf16[4,1024,128]{2,1,0:T(8,128)(2,1)S(1)}, u32[]{:S(2)}, u32[]{:S(2)}) %collective-permute-start.2) | collective-permute-done | bytes 1048608 | tf_op jit(solution)/shard_map/ppermute | solution.py:712
  367.4 28.1 %middle.4 = (bf16[4,1024,128]{2,1,0:T(8,128)(2,1)}, bf16[4,1024,128]{2,1,0:T(8,128)(2,1)}, bf16[4,1024,128]{2,1,0:T(8,128)(2,1)}, bf16[4,1024,128]{2,1,0:T(8,128...) custom-call(bf16[4,1024,128]{2,1,0:T(8,128)(2,1)} %get-tuple-element.92.re, ...), custom_call_target="tpu_custom_call", output_to_operand_aliasing={{4}: (6, {}), {5}: (7, {})} | custom-call | tf_op jit(solution)/shard_map/middle/pallas_call | solution.py:427
  401.5 18.8 %collective-permute-done.4.refs_5_ = bf16[4,1024,128]{2,1,0:T(8,128)(2,1)S(1)} collective-permute-done((bf16[4,1024,128]{2,1,0:T(8,128)(2,1)}, bf16[4,1024,128]{2,1,0:T(8,128)(2,1)S(1)}, u32[]{:S(2)}, u32[]{:S(2)}) %collective-permute-start.4) | collective-permute-done | bytes 1048608 | tf_op jit(solution)/shard_map/ppermute | solution.py:712
  451.9 24.1 %collective-permute-done.refs_1_ = bf16[4,1024,128]{2,1,0:T(8,128)(2,1)S(1)} collective-permute-done((bf16[4,1024,128]{2,1,0:T(8,128)(2,1)}, bf16[4,1024,128]{2,1,0:T(8,128)(2,1)S(1)}, u32[]{:S(2)}, u32[]{:S(2)}) %collective-permute-start) | collective-permute-done | bytes 1048608 | tf_op jit(solution)/shard_map/ppermute | solution.py:712
  476.9 28.3 %middle.5 = (bf16[4,1024,128]{2,1,0:T(8,128)(2,1)}, bf16[4,1024,128]{2,1,0:T(8,128)(2,1)}, bf16[4,1024,128]{2,1,0:T(8,128)(2,1)}, bf16[4,1024,128]{2,1,0:T(8,128...) custom-call(bf16[4,1024,128]{2,1,0:T(8,128)(2,1)} %get-tuple-element.84.re, ...), custom_call_target="tpu_custom_call", output_to_operand_aliasing={{4}: (6, {}), {5}: (7, {})} | custom-call | tf_op jit(solution)/shard_map/middle/pallas_call | solution.py:427
  511.2 19.0 %collective-permute-done.3.refs_5_ = bf16[4,1024,128]{2,1,0:T(8,128)(2,1)S(1)} collective-permute-done((bf16[4,1024,128]{2,1,0:T(8,128)(2,1)}, bf16[4,1024,128]{2,1,0:T(8,128)(2,1)S(1)}, u32[]{:S(2)}, u32[]{:S(2)}) %collective-permute-start.3) | collective-permute-done | bytes 1048608 | tf_op jit(solution)/shard_map/ppermute | solution.py:712
  531.1 13.9 %shard_map.139 = (bf16[16,2,64,1024]{3,2,1,0:T(8,128)(2,1)}, bf16[1024,1024]{1,0:T(8,128)(2,1)}, f32[4,256,256]{2,1,0:T(8,128)}) custom-call(s32[2]{0:T(128)} %broadcast_1__.2._, bf16[16,256,1024]{2,1,0:T(8,128)(2,1)} %bitcast.34, bf16[16,256,1024]{2,1,0:T(8,128)(2,1)} %bitcast.41, ...), custom_call_target="tpu_custom_call", output_to_operand_aliasing={{2}: (8, {}), {0}: (9, {})} | custom-call | tf_op jit(solution)/shard_map/pallas_call | solution.py:482
  561.7 66.4 %all-to-all-done.4.refs_1_.refs_2_ = bf16[16,2,64,1024]{3,2,1,0:T(8,128)(2,1)} async-done(((bf16[16,2,64,1024]{3,2,1,0:T(8,128)(2,1)}), bf16[16,2,64,1024]{3,2,1,0:T(8,128)(2,1)}, u32[]{:S(2)}, u32[]{:S(2)}) %all-to-all-start.4) | async-done | bytes 4194336 | tf_op jit(solution)/shard_map/all_to_all | solution.py:708
  640.3 28.3 %middle.6 = (bf16[4,1024,128]{2,1,0:T(8,128)(2,1)}, bf16[4,1024,128]{2,1,0:T(8,128)(2,1)}, bf16[4,1024,128]{2,1,0:T(8,128)(2,1)}, bf16[4,1024,128]{2,1,0:T(8,128...) custom-call(bf16[4,1024,128]{2,1,0:T(8,128)(2,1)} %get-tuple-element.110.r, ...), custom_call_target="tpu_custom_call", output_to_operand_aliasing={{4}: (6, {}), {5}: (7, {})} | custom-call | tf_op jit(solution)/shard_map/middle/pallas_call | solution.py:427
  670.1 28.3 %middle.7 = (bf16[4,1024,128]{2,1,0:T(8,128)(2,1)}, bf16[4,1024,128]{2,1,0:T(8,128)(2,1)}, bf16[4,1024,128]{2,1,0:T(8,128)(2,1)}, bf16[4,1024,128]{2,1,0:T(8,128...) custom-call(bf16[4,1024,128]{2,1,0:T(8,128)(2,1)} %get-tuple-element.107.r, ...), custom_call_target="tpu_custom_call", output_to_operand_aliasing={{4}: (6, {}), {5}: (7, {})} | custom-call | tf_op jit(solution)/shard_map/middle/pallas_call | solution.py:427
  725.1 13.9 %shard_map.147 = (bf16[16,2,64,1024]{3,2,1,0:T(8,128)(2,1)}, bf16[1024,1024]{1,0:T(8,128)(2,1)}, f32[4,256,256]{2,1,0:T(8,128)}) custom-call(s32[2]{0:T(128)} %constant.5.clone.1._, bf16[16,256,1024]{2,1,0:T(8,128)(2,1)} %bitcast.38, bf16[16,256,1024]{2,1,0:T(8,128)(2,1)} %bitcast.43, ...), custom_call_target="tpu_custom_call", output_to_operand_aliasing={{2}: (8, {}), {0}: (9, {})} | custom-call | tf_op jit(solution)/shard_map/pallas_call | solution.py:482
  739.0 19.3 %all-to-all-start.6 = ((bf16[16,2,64,1024]{3,2,1,0:T(8,128)(2,1)}), bf16[16,2,64,1024]{3,2,1,0:T(8,128)(2,1)}, u32[]{:S(2)}, u32[]{:S(2)}) async-start(bf16[16,2,64,1024]{3,2,1,0:T(8,128)(2,1)} %get-tuple-element.142), calls=%async_computation.7 | async-start | bytes 8388608 | tf_op jit(solution)/shard_map/all_to_all | solution.py:708
  762.7 22.0 %collective-permute-done.10.refs_3_ = bf16[4,1024,128]{2,1,0:T(8,128)(2,1)S(1)} collective-permute-done((bf16[4,1024,128]{2,1,0:T(8,128)(2,1)S(1)}, bf16[4,1024,128]{2,1,0:T(8,128)(2,1)S(1)}, u32[]{:S(2)}, u32[]{:S(2)}) %collective-permute-start.10) | collective-permute-done | bytes 1048608 | tf_op jit(solution)/shard_map/ppermute | solution.py:712
  873.9 101.6 %reduce-scatter.2.cloned.1.call-done = bf16[1280,256]{1,0:T(8,128)(2,1)} async-done(((bf16[10240,256]{1,0:T(8,128)(2,1)}), bf16[1280,256]{1,0:T(8,128)(2,1)}) %reduce-scatter.2.cloned.1.call-update) | async-done | bytes 655376 | tf_op jit(solution)/shard_map/reduce_scatter | solution.py:818
  988.6 21.1 %collective-permute-done.13 = bf16[1280,256]{1,0:T(8,128)(2,1)S(1)} collective-permute-done((bf16[1280,256]{1,0:T(8,128)(2,1)}, bf16[1280,256]{1,0:T(8,128)(2,1)S(1)}, u32[]{:S(2)}, u32[]{:S(2)}) %collective-permute-start.13) | collective-permute-done | bytes 655392 | tf_op jit(solution)/shard_map/ppermute | solution.py:825
  1015.1 62.2 %all_to_all.50.refs_2_ = bf16[16,1,64,1024]{3,2,1,0:T(8,128)(2,1)} all-to-all(bf16[16,1,64,1024]{3,2,1,0:T(8,128)(2,1)} %bitcast.60), channel_id=1, replica_groups=mesh['seq'=16,'fsdp'=2] {'seq'}, dimensions={0} | all-to-all | bytes 4194304 | tf_op jit(solution)/shard_map/all_to_all | solution.py:708
  1090.5 31.5 %all-to-all-done.9.refs_3_ = bf16[16,1,64,1024]{3,2,1,0:T(8,128)(2,1)S(1)} async-done(((bf16[16,1,64,1024]{3,2,1,0:T(8,128)(2,1)}), bf16[16,1,64,1024]{3,2,1,0:T(8,128)(2,1)S(1)}, u32[]{:S(2)}, u32[]{:S(2)}) %all-to-all-start.9) | async-done | bytes 2097184 | tf_op jit(solution)/shard_map/all_to_all | solution.py:708
  (106 shorter events, 311.1 us)
Async XLA Ops:
  15.4 48.4 %all-to-all-start.2 = ((bf16[16,1,64,1024]{3,2,1,0:T(8,128)(2,1)}), bf16[16,1,64,1024]{3,2,1,0:T(8,128)(2,1)S(1)}, u32[]{:S(2)}, u32[]{:S(2)}) async-start(bf16[16,1,64,1024]{3,2,1,0:T(8,128)(2,1)} %first.3), calls=%async_computation.2 | async-start | bytes 4194304 | tf_op jit(solution)/shard_map/all_to_all | solution.py:708
  65.1 52.2 %all-to-all-start = ((bf16[16,1,64,1024]{3,2,1,0:T(8,128)(2,1)}), bf16[16,1,64,1024]{3,2,1,0:T(8,128)(2,1)S(1)}, u32[]{:S(2)}, u32[]{:S(2)}) async-start(bf16[16,1,64,1024]{3,2,1,0:T(8,128)(2,1)} %get-tuple-element.80), calls=%async_computation | async-start | bytes 4194304 | tf_op jit(solution)/shard_map/all_to_all | solution.py:708
  118.6 88.8 %all-to-all-start.3 = ((bf16[16,2,64,1024]{3,2,1,0:T(8,128)(2,1)}), bf16[16,2,64,1024]{3,2,1,0:T(8,128)(2,1)}, u32[]{:S(2)}, u32[]{:S(2)}) async-start(bf16[16,2,64,1024]{3,2,1,0:T(8,128)(2,1)} %bitcast.57), calls=%async_computation.3 | async-start | bytes 8388608 | tf_op jit(solution)/shard_map/all_to_all | solution.py:708
  207.4 227.7 %all-to-all-start.1 = ((bf16[16,2,64,1024]{3,2,1,0:T(8,128)(2,1)}), bf16[16,2,64,1024]{3,2,1,0:T(8,128)(2,1)}, u32[]{:S(2)}, u32[]{:S(2)}) async-start(bf16[16,2,64,1024]{3,2,1,0:T(8,128)(2,1)} %bitcast.55), calls=%async_computation.1 | async-start | bytes 8388608 | tf_op jit(solution)/shard_map/all_to_all | solution.py:708
  250.9 93.7 %collective-permute-start.1 = (bf16[4,4096,128]{2,1,0:T(8,128)(2,1)}, bf16[4,4096,128]{2,1,0:T(8,128)(2,1)S(1)}, u32[]{:S(2)}, u32[]{:S(2)}) collective-permute-start(bf16[4,4096,128]{2,1,0:T(8,128)(2,1)} %get-tuple-element.88), channel_id=1, source_target_pairs={{0,1},{1,0},{2,3},{3,2},{4,5},{5,4},{6,7},{7,6},{8,9},{9,8},{10,11... | collective-permute-start | bytes 12582920 | tf_op jit(solution)/shard_map/ppermute | solution.py:712
  262.0 104.4 %collective-permute-start.2 = (bf16[4,1024,128]{2,1,0:T(8,128)(2,1)}, bf16[4,1024,128]{2,1,0:T(8,128)(2,1)S(1)}, u32[]{:S(2)}, u32[]{:S(2)}) collective-permute-start(bf16[4,1024,128]{2,1,0:T(8,128)(2,1)} %get-tuple-element.93), channel_id=1, source_target_pairs={{0,1},{1,0},{2,3},{3,2},{4,5},{5,4},{6,7},{7,6},{8,9},{9,8},{10,11... | collective-permute-start | bytes 3145736 | tf_op jit(solution)/shard_map/ppermute | solution.py:712
  435.2 109.8 %all-to-all-start.5 = ((bf16[16,2,64,1024]{3,2,1,0:T(8,128)(2,1)}), bf16[16,2,64,1024]{3,2,1,0:T(8,128)(2,1)}, u32[]{:S(2)}, u32[]{:S(2)}) async-start(bf16[16,2,64,1024]{3,2,1,0:T(8,128)(2,1)} %get-tuple-element.109), calls=%async_computation.5 | async-start | bytes 8388608 | tf_op jit(solution)/shard_map/all_to_all | solution.py:708
  450.4 25.6 %collective-permute-start = (bf16[4,1024,128]{2,1,0:T(8,128)(2,1)}, bf16[4,1024,128]{2,1,0:T(8,128)(2,1)S(1)}, u32[]{:S(2)}, u32[]{:S(2)}) collective-permute-start(bf16[4,1024,128]{2,1,0:T(8,128)(2,1)} %get-tuple-element.85), channel_id=1, source_target_pairs={{0,1},{1,0},{2,3},{3,2},{4,5},{5,4},{6,7},{7,6},{8,9},{9,8},{10,11... | collective-permute-start | bytes 3145736 | tf_op jit(solution)/shard_map/ppermute | solution.py:712
  505.2 24.9 %collective-permute-start.3 = (bf16[4,1024,128]{2,1,0:T(8,128)(2,1)}, bf16[4,1024,128]{2,1,0:T(8,128)(2,1)S(1)}, u32[]{:S(2)}, u32[]{:S(2)}) collective-permute-start(bf16[4,1024,128]{2,1,0:T(8,128)(2,1)} %get-tuple-element.99), channel_id=1, source_target_pairs={{0,1},{1,0},{2,3},{3,2},{4,5},{5,4},{6,7},{7,6},{8,9},{9,8},{10,11... | collective-permute-start | bytes 3145736 | tf_op jit(solution)/shard_map/ppermute | solution.py:712
  545.0 83.1 %all-to-all-start.4 = ((bf16[16,2,64,1024]{3,2,1,0:T(8,128)(2,1)}), bf16[16,2,64,1024]{3,2,1,0:T(8,128)(2,1)}, u32[]{:S(2)}, u32[]{:S(2)}) async-start(bf16[16,2,64,1024]{3,2,1,0:T(8,128)(2,1)} %get-tuple-element.105), calls=%async_computation.4 | async-start | bytes 8388608 | tf_op jit(solution)/shard_map/all_to_all | solution.py:708
  560.2 79.0 %collective-permute-start.6 = (bf16[4,1024,128]{2,1,0:T(8,128)(2,1)}, bf16[4,1024,128]{2,1,0:T(8,128)(2,1)S(1)}, u32[]{:S(2)}, u32[]{:S(2)}) collective-permute-start(bf16[4,1024,128]{2,1,0:T(8,128)(2,1)} %get-tuple-element.111), channel_id=1, source_target_pairs={{0,1},{1,0},{2,3},{3,2},{4,5},{5,4},{6,7},{7,6},{8,9},{9,8},{10,11... | collective-permute-start | bytes 3145736 | tf_op jit(solution)/shard_map/ppermute | solution.py:712
  637.7 31.4 %collective-permute-start.5 = (bf16[4,1024,128]{2,1,0:T(8,128)(2,1)}, bf16[4,1024,128]{2,1,0:T(8,128)(2,1)S(1)}, u32[]{:S(2)}, u32[]{:S(2)}) collective-permute-start(bf16[4,1024,128]{2,1,0:T(8,128)(2,1)} %get-tuple-element.108), channel_id=1, source_target_pairs={{0,1},{1,0},{2,3},{3,2},{4,5},{5,4},{6,7},{7,6},{8,9},{9,8},{10,11... | collective-permute-start | bytes 3145736 | tf_op jit(solution)/shard_map/ppermute | solution.py:712
  668.5 40.2 %collective-permute-start.12 = (bf16[4,1024,128]{2,1,0:T(8,128)(2,1)}, bf16[4,1024,128]{2,1,0:T(8,128)(2,1)S(1)}, u32[]{:S(2)}, u32[]{:S(2)}) collective-permute-start(bf16[4,1024,128]{2,1,0:T(8,128)(2,1)} %get-tuple-element.137), channel_id=1, source_target_pairs={{0,1},{1,0},{2,3},{3,2},{4,5},{5,4},{6,7},{7,6},{8,9},{9,8},{10,11... | collective-permute-start | bytes 3145736 | tf_op jit(solution)/shard_map/ppermute | solution.py:712
  698.3 25.7 %collective-permute-start.11 = (bf16[4,1024,128]{2,1,0:T(8,128)(2,1)}, bf16[4,1024,128]{2,1,0:T(8,128)(2,1)S(1)}, u32[]{:S(2)}, u32[]{:S(2)}) collective-permute-start(bf16[4,1024,128]{2,1,0:T(8,128)(2,1)} %get-tuple-element.135), channel_id=1, source_target_pairs={{0,1},{1,0},{2,3},{3,2},{4,5},{5,4},{6,7},{7,6},{8,9},{9,8},{10,11... | collective-permute-start | bytes 3145736 | tf_op jit(solution)/shard_map/ppermute | solution.py:712
  739.0 129.1 %all-to-all-start.6 = ((bf16[16,2,64,1024]{3,2,1,0:T(8,128)(2,1)}), bf16[16,2,64,1024]{3,2,1,0:T(8,128)(2,1)}, u32[]{:S(2)}, u32[]{:S(2)}) async-start(bf16[16,2,64,1024]{3,2,1,0:T(8,128)(2,1)} %get-tuple-element.142), calls=%async_computation.7 | async-start | bytes 8388608 | tf_op jit(solution)/shard_map/all_to_all | solution.py:708
  758.3 217.1 %reduce-scatter.2.cloned.1.call-start = ((), (), s32[]{:S(2)}) async-start(), calls=%async_computation.11 | async-start | bytes 5898240 | tf_op jit(solution)/shard_map/reduce_scatter | solution.py:818
  758.6 26.1 %collective-permute-start.10 = (bf16[4,1024,128]{2,1,0:T(8,128)(2,1)S(1)}, bf16[4,1024,128]{2,1,0:T(8,128)(2,1)S(1)}, u32[]{:S(2)}, u32[]{:S(2)}) collective-permute-start(bf16[4,1024,128]{2,1,0:T(8,128)(2,1)S(1)} %copy-done.19), channel_id=1, source_target_pairs={{0,1},{1,0},{2,3},{3,2},{4,5},{5,4},{6,7},{7,6},{8,9},{9,8},{10,11... | collective-permute-start | bytes 3145736 | tf_op jit(solution)/shard_map/ppermute | solution.py:712
  760.1 47.0 %collective-permute-start.9 = (bf16[4,1024,128]{2,1,0:T(8,128)(2,1)}, bf16[4,1024,128]{2,1,0:T(8,128)(2,1)S(1)}, u32[]{:S(2)}, u32[]{:S(2)}) collective-permute-start(bf16[4,1024,128]{2,1,0:T(8,128)(2,1)} %get-tuple-element.122), channel_id=1, source_target_pairs={{0,1},{1,0},{2,3},{3,2},{4,5},{5,4},{6,7},{7,6},{8,9},{9,8},{10,11... | collective-permute-start | bytes 3145736 | tf_op jit(solution)/shard_map/ppermute | solution.py:712
  760.7 68.9 %collective-permute-start.8 = (bf16[4,1024,128]{2,1,0:T(8,128)(2,1)}, bf16[4,1024,128]{2,1,0:T(8,128)(2,1)S(1)}, u32[]{:S(2)}, u32[]{:S(2)}) collective-permute-start(bf16[4,1024,128]{2,1,0:T(8,128)(2,1)} %get-tuple-element.120), channel_id=1, source_target_pairs={{0,1},{1,0},{2,3},{3,2},{4,5},{5,4},{6,7},{7,6},{8,9},{9,8},{10,11... | collective-permute-start | bytes 3145736 | tf_op jit(solution)/shard_map/ppermute | solution.py:712
  762.2 89.3 %collective-permute-start.7 = (bf16[4,1024,128]{2,1,0:T(8,128)(2,1)}, bf16[4,1024,128]{2,1,0:T(8,128)(2,1)S(1)}, u32[]{:S(2)}, u32[]{:S(2)}) collective-permute-start(bf16[4,1024,128]{2,1,0:T(8,128)(2,1)} %get-tuple-element.117), channel_id=1, source_target_pairs={{0,1},{1,0},{2,3},{3,2},{4,5},{5,4},{6,7},{7,6},{8,9},{9,8},{10,11... | collective-permute-start | bytes 3145736 | tf_op jit(solution)/shard_map/ppermute | solution.py:712
  868.0 142.7 %all-to-all-start.7 = ((bf16[16,2,64,1024]{3,2,1,0:T(8,128)(2,1)}), bf16[16,2,64,1024]{3,2,1,0:T(8,128)(2,1)}, u32[]{:S(2)}, u32[]{:S(2)}) async-start(bf16[16,2,64,1024]{3,2,1,0:T(8,128)(2,1)} %get-tuple-element.149), calls=%async_computation.8 | async-start | bytes 8388608 | tf_op jit(solution)/shard_map/all_to_all | solution.py:708
  873.8 208.1 %all-gather.2.cloned.1.call-start = ((), (), s32[]{:S(2)}) async-start(), calls=%async_computation.12 | async-start | bytes 5898240 | tf_op jit(solution)/shard_map/all_gather | solution.py:828
  975.5 34.3 %collective-permute-start.13 = (bf16[1280,256]{1,0:T(8,128)(2,1)}, bf16[1280,256]{1,0:T(8,128)(2,1)S(1)}, u32[]{:S(2)}, u32[]{:S(2)}) collective-permute-start(bf16[1280,256]{1,0:T(8,128)(2,1)} %reduce-scatter.2.cloned.1.call-done), channel_id=1, source_target_pairs={{0,16},{2,18},{4,20},{6,22},{8,24},{10,26},{12,28},{14,30},{16,0},... | collective-permute-start | bytes 1966088 | tf_op jit(solution)/shard_map/ppermute | solution.py:825
  1077.3 44.6 %all-to-all-start.9 = ((bf16[16,1,64,1024]{3,2,1,0:T(8,128)(2,1)}), bf16[16,1,64,1024]{3,2,1,0:T(8,128)(2,1)S(1)}, u32[]{:S(2)}, u32[]{:S(2)}) async-start(bf16[16,1,64,1024]{3,2,1,0:T(8,128)(2,1)} %bitcast.59), calls=%async_computation.10 | async-start | bytes 4194304 | tf_op jit(solution)/shard_map/all_to_all | solution.py:708
  (21 other events, 220.8 us)
Sparse Core Ops, SparseCore 0:
  868.1 107.2 reduce-scatter.1
  1010.9 64.8 all-gather.1

commit v4 on v3

--- a/solution.py
+++ b/solution.py
@@ -204,13 +204,11 @@
     for n, out in enumerate(outs):
         _, _, height, cols = out.shape
         count = size // height
-
-        @pl.loop(0, span // rows)
-        def _(group, n=n, out=out):
-            start = pl.multiple_of(n * span + group * rows, rows)
-            piece = scratch[:, pl.ds(start, rows), :].reshape(size, cols)
+        for group in range(span // rows):
+            start = n * span + group * rows
+            piece = scratch[:, start : start + rows, :].reshape(size, cols)
             value = dot(swap, piece).astype(BF)
-            out[pl.ds(group * count, count), 0] = value.reshape(count, height, cols)
+            out[group * count : (group + 1) * count, 0] = value.reshape(count, height, cols)
 
 
 def first_stage(chunks, places, seq, x3, mix_first, twiddle, cols=256):
@@ -326,22 +324,15 @@
     )(g3, down_second)
 
 
-def hidden_kernel(x_ref, m_ref, w_ref, h_ref, own_ref, send_ref, mids):
-    rows, cols, _ = x_ref.shape
-    size = rows * cols
+def hidden_kernel(x_ref, m_ref, w_ref, h_ref, own_ref, send_ref):
+    rows, cols, channels = x_ref.shape
+    mixed = dot(swap_rows(rows), m_ref[...].reshape(rows * cols, channels))
+    inputs = x_ref[...].reshape(rows * cols, channels).astype(F32)
+    hidden = (inputs + jax.nn.sigmoid(inputs) * mixed).astype(BF)
+    h_ref[...] = hidden
     blocks, width = w_ref.shape[0], w_ref.shape[1]
-    swap = swap_rows(rows)
-
-    @pl.loop(0, blocks)
-    def _(k):
-        part = pl.ds(pl.multiple_of(k * width, width), width)
-        mixed = dot(swap, m_ref[:, :, part].reshape(size, width))
-        inputs = x_ref[:, :, part].reshape(size, width).astype(F32)
-        hidden = (inputs + jax.nn.sigmoid(inputs) * mixed).astype(BF)
-        h_ref[:, part] = hidden
-        mids[k] = dot(hidden, w_ref[k])
-
-    spread_store([mids[k] for k in range(blocks)], own_ref, send_ref)
+    values = [dot(hidden[:, k * width : (k + 1) * width], w_ref[k]) for k in range(blocks)]
+    spread_store(values, own_ref, send_ref)
 
 
 def arriving(field, size):
@@ -367,13 +358,12 @@
             jax.ShapeDtypeStruct((blocks, steps * size, LANES), BF),
             in_hbm((blocks, steps * size, LANES)),
         ],
-        scratch=[pltpu.VMEM((blocks, size, 2 * LANES), F32)],
     )(x3, mixed[0], up_first)
 
 
 def middle_kernel(cols, *refs):
     uo, ur, bo, br, us, df, sus_in, sdf_in = refs[:8]
-    down_own, down_send, grad_own, grad_send, sus, sdf, down_sum, grad_sum = refs[8:]
+    down_own, down_send, grad_own, grad_send, sus, sdf = refs[8:]
     start = pl.program_id(1) == 0
 
     @pl.when(start)
@@ -384,32 +374,24 @@
     up = jnp.concatenate([uo[0], ur[0]], axis=1)
     back = jnp.concatenate([bo[0], br[0]], axis=1)
     hidden_units = us.shape[2]
-    down_sum[...] = jnp.zeros(down_sum.shape, F32)
-    grad_sum[...] = jnp.zeros(grad_sum.shape, F32)
-
-    @pl.loop(0, hidden_units // (2 * cols))
-    def _(pair):
-        down, grad = None, None
-        for side in range(2):
-            part = pl.ds(pl.multiple_of((2 * pair + side) * cols, cols), cols)
-            z = dot(up, us[0, :, part])
-            z2 = z * z
-            h = 0.5 + 0.5 * jnp.tanh(z * (root_two_pi + (root_two_pi * cubic_term) * z2))
-            act = (z * h).astype(BF)
-            slope = h + (h - h * h) * (
-                z * (2.0 * root_two_pi + (6.0 * root_two_pi * cubic_term) * z2)
-            )
-            pre = (dot_nt(back, df[0, part, :]) * slope).astype(BF)
-            step = dot(act, df[0, part, :])
-            down = step if down is None else down + step
-            step = dot_nt(pre, us[0, :, part])
-            grad = step if grad is None else grad + step
-            sdf[0, part, :] += dot_tn(act, back)
-            sus[0, :, part] += dot_tn(up, pre)
-        down_sum[...] += down
-        grad_sum[...] += grad
-
-    down, grad = down_sum[...], grad_sum[...]
+    down = None
+    grad = None
+    for low in range(0, hidden_units, cols):
+        part = slice(low, low + cols)
+        z = dot(up, us[0, :, part])
+        z2 = z * z
+        h = 0.5 + 0.5 * jnp.tanh(z * (root_two_pi + (root_two_pi * cubic_term) * z2))
+        act = (z * h).astype(BF)
+        slope = h + (h - h * h) * (
+            z * (2.0 * root_two_pi + (6.0 * root_two_pi * cubic_term) * z2)
+        )
+        pre = (dot_nt(back, df[0, part, :]) * slope).astype(BF)
+        step = dot(act, df[0, part, :])
+        down = step if down is None else down + step
+        step = dot_nt(pre, us[0, :, part])
+        grad = step if grad is None else grad + step
+        sdf[0, part, :] += dot_tn(act, back)
+        sus[0, :, part] += dot_tn(up, pre)
     down_own[0] = down[:, :LANES].astype(BF)
     down_send[0] = down[:, LANES:].astype(BF)
     grad_own[0] = grad[:, :LANES].astype(BF)
@@ -431,7 +413,6 @@
         out_specs=[part] * 4 + [us_spec, df_spec],
         out_shape=[shape] * 4
         + [jax.ShapeDtypeStruct(up_second.shape, F32), jax.ShapeDtypeStruct(down_first.shape, F32)],
-        scratch_shapes=[pltpu.VMEM((tile, 2 * LANES), F32)] * 2,
         input_output_aliases={6: 4, 7: 5},
         compiler_params=params(0, 0),
         name="middle",
@@ -440,28 +421,24 @@
 
 def input_kernel(*refs):
     x_ref, g_ref, m_ref, h_ref, go, gr, w_ref, suf_in = refs[:8]
-    send_ref, base_ref, suf, mids = refs[-4:]
+    send_ref, base_ref, suf = refs[-3:]
 
     @pl.when(pl.program_id(0) == 0)
     def _():
         suf[...] = suf_in[...]
 
-    rows, cols, _ = x_ref.shape
+    rows, cols, channels = x_ref.shape
     size = rows * cols
     swap = swap_rows(rows)
     width = w_ref.shape[1]
-    for k, mid in enumerate(gather_load(go, gr)):
-        mids[k] = mid
-
-    @pl.loop(0, w_ref.shape[0])
-    def _(k):
-        part = pl.ds(pl.multiple_of(k * width, width), width)
-        mid = mids[k]
+    mids = gather_load(go, gr)
+    x3, g3 = x_ref[...].reshape(size, channels), g_ref[...].reshape(size, channels)
+    for k, mid in enumerate(mids):
+        part = slice(k * width, (k + 1) * width)
         inner = dot_nt(mid, w_ref[k])
         suf[k] += dot_tn(h_ref[:, part], mid)
-        grad = g_ref[:, :, part].reshape(size, width).astype(F32) + inner
-        grad = grad.astype(BF).astype(F32)
-        gating = jax.nn.sigmoid(x_ref[:, :, part].reshape(size, width).astype(F32))
+        grad = (g3[:, part].astype(F32) + inner).astype(BF).astype(F32)
+        gating = jax.nn.sigmoid(x3[:, part].astype(F32))
         mixed = dot(swap, m_ref[:, :, part].reshape(size, width))
         send = dot(swap, (grad * gating).astype(BF)).astype(BF)
         send_ref[:, :, part] = send.reshape(send_ref.shape[0], send_ref.shape[1], width)
@@ -495,7 +472,6 @@
             jax.ShapeDtypeStruct(up_first.shape, F32),
         ],
         {7: 2, 8: 0},
-        [pltpu.VMEM((blocks, size, 2 * LANES), BF)],
     )(x3, g3, mixed[0], hidden, grad_own, grad_recv, up_first, sums, buffer)
 
 
@@ -645,21 +621,19 @@
     )(mine, *weights)
 
 
-def collect_kernel(scale, sus, sdf, suf, sds, out):
-    width = suf.shape[1]
-    row = 0
-    pieces = [sus[0, :, low : low + width] for low in range(0, sus.shape[2], width)]
-    pieces += [sdf[0], suf[0], sds[0]]
-    for piece in pieces:
-        out[0, row : row + piece.shape[0], :] = (piece * scale).astype(BF)
-        row += piece.shape[0]
-
-
-def collect_stage(scale, sums):
-    blocks, width = sums[2].shape[:2]
+def collect_kernel(scale, width, *refs):
+    out, row = refs[-1], 0
+    for ref in refs[:-1]:
+        for low in range(0, ref.shape[2], width):
+            out[0, row : row + ref.shape[1], :] = (ref[0, :, low : low + width] * scale).astype(BF)
+            row += ref.shape[1]
+
+
+def collect_stage(scale, width, sums):
+    blocks = sums[0].shape[0]
     height = sum(v.shape[1] * v.shape[2] for v in sums) // width
     return pl.pallas_call(
-        functools.partial(collect_kernel, scale),
+        functools.partial(collect_kernel, scale, width),
         grid=(blocks,),
         in_specs=[by_block(v) for v in sums],
         out_specs=pl.BlockSpec((1, height, width), lambda g: (g, 0, 0)),
@@ -669,39 +643,35 @@
     )(*sums)
 
 
-def finish_kernel(mine_ref, whole, uf, us, df, ds):
+def finish_kernel(mine_ref, large, small, uf, us, df, ds):
     mine = mine_ref[0]
     width = ds.shape[1]
     matrix = group_matrix(mine, width, NBLK // 2)
-    row = us.shape[2] // width * width
-
-    @pl.loop(0, us.shape[2] // width)
-    def _(n):
-        here = pl.ds(pl.multiple_of(n * width, width), width)
-        us[0, :, here] = dot_tn(matrix, whole[0, here, :])
-
-    tall = df.shape[1]
-    down, up = whole.at[0, row : row + tall, :], whole.at[0, row + tall : row + tall + width, :]
+    for low in range(0, us.shape[2], width):
+        us[0, :, low : low + width] = dot_tn(matrix, large[0, low : low + width, :])
+    row = us.shape[2]
     copy_halves(
         mine,
-        (lambda: down[...], lambda: up[...]),
+        (lambda: large[0, row : row + df.shape[1], :], lambda: small[0, :width, :]),
         ((df, (0, slice(None))), (uf, (0, slice(None)))),
     )
-    row += tall + width
-    ds[0] = dot_tn(matrix, whole[0, row : row + width, :])
-
-
-def finish_stage(mine, whole, weights):
+    ds[0] = dot_tn(matrix, small[0, width : 2 * width, :])
+
+
+def finish_stage(mine, wholes, weights):
     specs = [by_block(w) for w in weights]
     return pl.pallas_call(
         finish_kernel,
         grid_spec=pltpu.PrefetchScalarGridSpec(
-            num_scalar_prefetch=1, grid=(whole.shape[0],), in_specs=[by_block(whole)], out_specs=specs
+            num_scalar_prefetch=1,
+            grid=(wholes[0].shape[0],),
+            in_specs=[by_block(v) for v in wholes],
+            out_specs=specs,
         ),
         out_shape=[jax.ShapeDtypeStruct(w.shape, F32) for w in weights],
         compiler_params=params(0),
         name="finish",
-    )(mine, whole)
+    )(mine, *wholes)
 
 
 def exchange(field):
@@ -719,8 +689,8 @@
     (((2, 1), (1, 3)), (("hidden", 0), ("second", 2), ("middle", 0), ("inputs", 0))),
     (((2, 2), (3, 0)), (("hidden", 1), ("second", 3), ("middle", 1), ("outputs", 0), ("inputs", 1))),
     (((2, 3), (3, 1)), (("hidden", 2), ("fourth", 0), ("middle", 2), ("outputs", 1), ("inputs", 2))),
-    (((3, 2), (4, 0)), (("hidden", 3), ("fourth", 1), ("middle", 3), ("outputs", 2), ("inputs", 3))),
-    (((3, 3), (4, 1)), (("fourth", 2), ("outputs", 3), ("collect", 0))),
+    (((3, 2), (4, 0)), (("hidden", 3), ("fourth", 1), ("middle", 3), ("collect", 0), ("outputs", 2), ("inputs", 3))),
+    (((3, 3), (4, 1)), (("fourth", 2), ("outputs", 3), ("collect", 1))),
     (((4, 2),), (("fourth", 3),)),
     (((4, 3),), (("finish", 0),)),
 )
@@ -814,19 +784,20 @@
             elif name == "fourth":
                 buffers[place[4, n][0]] = second_stage(w2, arrived[3, n], *spot((4, n)), rows)
 
-    collected = collect_stage(1.0 / length, (*sums, sum_first, sum_last))
-    part = lax.psum_scatter(
-        collected.reshape(-1, collected.shape[2]),
-        "seq",
-        scatter_dimension=0,
-        axis_index_groups=halves,
-        tiled=True,
-    )
-    other = lax.ppermute(part, "seq", [(d, (d + seq // 2) % seq) for d in range(seq)])
-    other = tie(other, buffers[place[4, CHUNKS - 1][0]])
-    part = (part.astype(F32) + other.astype(F32)).astype(BF)
-    whole = lax.all_gather(part, "seq", axis=0, axis_index_groups=halves, tiled=True)
-    grads = finish_stage(mine, whole.reshape(collected.shape), weights)
+    width = up_first.shape[1]
+    after = (buffers[place[4, CHUNKS - 1][0]], arrived[4, CHUNKS - 2][0])
+    wholes = []
+    for n, values in enumerate((sums, (sum_first, sum_last))):
+        collected = collect_stage(1.0 / length, width, values)
+        part = lax.psum_scatter(
+            collected.reshape(-1, width), "seq", scatter_dimension=0, axis_index_groups=halves, tiled=True
+        )
+        other = lax.ppermute(part, "seq", [(d, (d + seq // 2) % seq) for d in range(seq)])
+        other = tie(other, after[n])
+        part = (part.astype(F32) + other.astype(F32)).astype(BF)
+        whole = lax.all_gather(part, "seq", axis=0, axis_index_groups=halves, tiled=True)
+        wholes.append(whole.reshape(collected.shape))
+    grads = finish_stage(mine, wholes, weights)
     tw_cols = tie(tw_cols, grads)
     fields = [arrived[4, n] for n in range(CHUNKS)]
     bases = [kept["base", n] for n in range(CHUNKS)]

time: 1150 us -> 1070 us (0.930)
  blocking collectives: 62.2 us -> 0 us
  Pallas kernels: 351 us -> 300 us
  waiting for transfers between devices: 581 us -> 626 us
    reduce_scatter x1 -> x2, waiting for transfers between devices: 102 us -> 0.04 us  [chunked_shards(): lax.psum_scatter(collected.reshape(-1, width), 'seq', scatter_dimension=0...]
    ppermute x1 -> x2, waiting for transfers between devices: 21.1 us -> 118 us  [chunked_shards(): lax.ppermute(part, 'seq', [(d, (d + seq // 2) % seq) for d in range(seq)])]
    all_to_all x1 -> x0, blocking collectives: 62.2 us -> none  [exchange(): return lax.all_to_all(field, 'seq', split_axis=0, concat_axis=0, tiled=True)]
    all_gather x1 -> x2, waiting for transfers between devices: 0.01 us -> 54.4 us  [chunked_shards(): lax.all_gather(part, 'seq', axis=0, axis_index_groups=halves, tiled=True)]
    all_to_all x9 -> x10, waiting for transfers between devices: 233 us -> 179 us  [exchange(): return lax.all_to_all(field, 'seq', split_axis=0, concat_axis=0, tiled=True)]
    ppermute x13, waiting for transfers between devices: 225 us -> 275 us  [partner(): return lax.ppermute(values, 'fsdp', [(0, 1), (1, 0)])]
    pallas_call x4, Pallas kernels: 113 us -> 97.5 us  [middle_stage(): pl.pallas_call(functools.partial(middle_kernel, cols), grid=(blocks, step...]
    pallas_call x4, Pallas kernels: 55.6 us -> 41 us  [input_stage(): offset_call(input_kernel, (chunk, part), steps, [natural, natural, arrivi...]
  transfers between devices with their start and end apart: 25 -> 29, of which waited for: 17 -> 19; matrix products, arithmetic and copies ran while one was open for 0% -> 0% of each run, Pallas kernels for 28% -> 26%
where the time goes in v4:
time: 1070 us
  waiting for transfers between devices  626 us (59%)
  Pallas kernels  300 us (28%)
  starting transfers between devices  106 us (10%)
  local copies, waits for them, and re-layouts  18.6 us (2%)
  between operations  14 us (1%)
    ppermute x13, waiting for transfers between devices, partner(): return lax.ppermute(values, 'fsdp', [(0, 1), (1, 0)])  275 us
    all_to_all x10, waiting for transfers between devices, exchange(): return lax.all_to_all(field, 'seq', split_axis=0, concat_axis=0, tiled=True)  179 us
    ppermute x2, waiting for transfers between devices, chunked_shards(): lax.ppermute(part, 'seq', [(d, (d + seq // 2) % seq) for d in range(seq)])  118 us
    pallas_call x4, Pallas kernels, middle_stage(): pl.pallas_call(functools.partial(middle_kernel, cols), grid=(blocks, step...  97.5 us
    all_to_all x10, starting transfers between devices, exchange(): return lax.all_to_all(field, 'seq', split_axis=0, concat_axis=0, tiled=True)  86.7 us
    all_gather x2, waiting for transfers between devices, chunked_shards(): lax.all_gather(part, 'seq', axis=0, axis_index_groups=halves, tiled=True)  54.4 us
    pallas_call x4, Pallas kernels, input_stage(): offset_call(input_kernel, (chunk, part), steps, [natural, natural, arrivi...  41 us
    pallas_call x4, Pallas kernels, output_stage(): offset_call(functools.partial(output_kernel, fresh), (chunk,), steps, [na...  35.6 us
  transfers between devices with their start and end apart: 29, of which 19 were waited for; matrix products, arithmetic and copies ran while one was open for 0% of the time, Pallas kernels for 26%

profile of v4, /device:TPU:0, one launch (start us, length us, event | category | flops | bytes accessed | tf_op | source)
XLA Modules:
  0.0 1067.9 jit_solution(4360194990504691088)
XLA Ops:
  29.6 32.6 %all-to-all-done.2 = bf16[16,1,64,1024]{3,2,1,0:T(8,128)(2,1)S(1)} async-done(((bf16[16,1,64,1024]{3,2,1,0:T(8,128)(2,1)}), bf16[16,1,64,1024]{3,2,1,0:T(8,128)(2,1)S(1)}, u32[]{:S(2)}, u32[]{:S(2)}) %all-to-all-start.2) | async-done | bytes 2097184 | tf_op jit(solution)/shard_map/all_to_all | solution.py:678
  79.9 35.9 %all-to-all-done = bf16[16,1,64,1024]{3,2,1,0:T(8,128)(2,1)S(1)} async-done(((bf16[16,1,64,1024]{3,2,1,0:T(8,128)(2,1)}), bf16[16,1,64,1024]{3,2,1,0:T(8,128)(2,1)S(1)}, u32[]{:S(2)}, u32[]{:S(2)}) %all-to-all-start) | async-done | bytes 2097184 | tf_op jit(solution)/shard_map/all_to_all | solution.py:678
  132.7 73.2 %all-to-all-done.3.refs_1_.refs_2_ = bf16[16,2,64,1024]{3,2,1,0:T(8,128)(2,1)} async-done(((bf16[16,2,64,1024]{3,2,1,0:T(8,128)(2,1)}), bf16[16,2,64,1024]{3,2,1,0:T(8,128)(2,1)}, u32[]{:S(2)}, u32[]{:S(2)}) %all-to-all-start.3) | async-done | bytes 4194336 | tf_op jit(solution)/shard_map/all_to_all | solution.py:678
  205.9 19.7 %all-to-all-start.1 = ((bf16[16,2,64,1024]{3,2,1,0:T(8,128)(2,1)}), bf16[16,2,64,1024]{3,2,1,0:T(8,128)(2,1)}, u32[]{:S(2)}, u32[]{:S(2)}) async-start(bf16[16,2,64,1024]{3,2,1,0:T(8,128)(2,1)} %bitcast.57), calls=%async_computation.1 | async-start | bytes 8388608 | tf_op jit(solution)/shard_map/all_to_all | solution.py:678
  233.4 16.0 %back.1 = (bf16[4,4096,128]{2,1,0:T(8,128)(2,1)}, bf16[4,4096,128]{2,1,0:T(8,128)(2,1)}) custom-call(bf16[16,256,1024]{2,1,0:T(8,128)(2,1)} %bitcast.41, bf16[4,256,256]{2,1,0:T(8,128)(2,1)} %get-tuple-element.87.w_ref.refs_4_), custom_call_target="tpu_custom_call" | custom-call | tf_op jit(solution)/shard_map/back/pallas_call | solution.py:316
  257.4 85.7 %collective-permute-done.1.refs_3_ = bf16[4,4096,128]{2,1,0:T(8,128)(2,1)S(1)} collective-permute-done((bf16[4,4096,128]{2,1,0:T(8,128)(2,1)}, bf16[4,4096,128]{2,1,0:T(8,128)(2,1)S(1)}, u32[]{:S(2)}, u32[]{:S(2)}) %collective-permute-start.1) | collective-permute-done | bytes 4194336 | tf_op jit(solution)/shard_map/ppermute | solution.py:682
  343.0 21.8 %collective-permute-done.2.refs_1_ = bf16[4,1024,128]{2,1,0:T(8,128)(2,1)S(1)} collective-permute-done((bf16[4,1024,128]{2,1,0:T(8,128)(2,1)}, bf16[4,1024,128]{2,1,0:T(8,128)(2,1)S(1)}, u32[]{:S(2)}, u32[]{:S(2)}) %collective-permute-start.2) | collective-permute-done | bytes 1048608 | tf_op jit(solution)/shard_map/ppermute | solution.py:682
  365.9 24.2 %middle.4 = (bf16[4,1024,128]{2,1,0:T(8,128)(2,1)}, bf16[4,1024,128]{2,1,0:T(8,128)(2,1)}, bf16[4,1024,128]{2,1,0:T(8,128)(2,1)}, bf16[4,1024,128]{2,1,0:T(8,128...) custom-call(bf16[4,1024,128]{2,1,0:T(8,128)(2,1)} %get-tuple-element.93.re, ...), custom_call_target="tpu_custom_call", output_to_operand_aliasing={{4}: (6, {}), {5}: (7, {})} | custom-call | tf_op jit(solution)/shard_map/middle/pallas_call | solution.py:409
  396.1 18.8 %collective-permute-done.4.refs_5_ = bf16[4,1024,128]{2,1,0:T(8,128)(2,1)S(1)} collective-permute-done((bf16[4,1024,128]{2,1,0:T(8,128)(2,1)}, bf16[4,1024,128]{2,1,0:T(8,128)(2,1)S(1)}, u32[]{:S(2)}, u32[]{:S(2)}) %collective-permute-start.4) | collective-permute-done | bytes 1048608 | tf_op jit(solution)/shard_map/ppermute | solution.py:682
  439.3 24.1 %collective-permute-done.refs_1_ = bf16[4,1024,128]{2,1,0:T(8,128)(2,1)S(1)} collective-permute-done((bf16[4,1024,128]{2,1,0:T(8,128)(2,1)}, bf16[4,1024,128]{2,1,0:T(8,128)(2,1)S(1)}, u32[]{:S(2)}, u32[]{:S(2)}) %collective-permute-start) | collective-permute-done | bytes 1048608 | tf_op jit(solution)/shard_map/ppermute | solution.py:682
  464.3 24.4 %middle.5 = (bf16[4,1024,128]{2,1,0:T(8,128)(2,1)}, bf16[4,1024,128]{2,1,0:T(8,128)(2,1)}, bf16[4,1024,128]{2,1,0:T(8,128)(2,1)}, bf16[4,1024,128]{2,1,0:T(8,128...) custom-call(bf16[4,1024,128]{2,1,0:T(8,128)(2,1)} %get-tuple-element.85.re, ...), custom_call_target="tpu_custom_call", output_to_operand_aliasing={{4}: (6, {}), {5}: (7, {})} | custom-call | tf_op jit(solution)/shard_map/middle/pallas_call | solution.py:409
  494.7 19.0 %collective-permute-done.3.refs_5_ = bf16[4,1024,128]{2,1,0:T(8,128)(2,1)S(1)} collective-permute-done((bf16[4,1024,128]{2,1,0:T(8,128)(2,1)}, bf16[4,1024,128]{2,1,0:T(8,128)(2,1)S(1)}, u32[]{:S(2)}, u32[]{:S(2)}) %collective-permute-start.3) | collective-permute-done | bytes 1048608 | tf_op jit(solution)/shard_map/ppermute | solution.py:682
  538.0 24.1 %collective-permute-done.6.refs_1_ = bf16[4,1024,128]{2,1,0:T(8,128)(2,1)S(1)} collective-permute-done((bf16[4,1024,128]{2,1,0:T(8,128)(2,1)}, bf16[4,1024,128]{2,1,0:T(8,128)(2,1)S(1)}, u32[]{:S(2)}, u32[]{:S(2)}) %collective-permute-start.6) | collective-permute-done | bytes 1048608 | tf_op jit(solution)/shard_map/ppermute | solution.py:682
  563.1 24.4 %middle.6 = (bf16[4,1024,128]{2,1,0:T(8,128)(2,1)}, bf16[4,1024,128]{2,1,0:T(8,128)(2,1)}, bf16[4,1024,128]{2,1,0:T(8,128)(2,1)}, bf16[4,1024,128]{2,1,0:T(8,128...) custom-call(bf16[4,1024,128]{2,1,0:T(8,128)(2,1)} %get-tuple-element.111.r, ...), custom_call_target="tpu_custom_call", output_to_operand_aliasing={{4}: (6, {}), {5}: (7, {})} | custom-call | tf_op jit(solution)/shard_map/middle/pallas_call | solution.py:409
  593.6 18.9 %collective-permute-done.13.refs_5_ = bf16[4,1024,128]{2,1,0:T(8,128)(2,1)S(1)} collective-permute-done((bf16[4,1024,128]{2,1,0:T(8,128)(2,1)}, bf16[4,1024,128]{2,1,0:T(8,128)(2,1)S(1)}, u32[]{:S(2)}, u32[]{:S(2)}) %collective-permute-start.13) | collective-permute-done | bytes 1048608 | tf_op jit(solution)/shard_map/ppermute | solution.py:682
  639.6 22.2 %collective-permute-done.5.refs_1_ = bf16[4,1024,128]{2,1,0:T(8,128)(2,1)S(1)} collective-permute-done((bf16[4,1024,128]{2,1,0:T(8,128)(2,1)}, bf16[4,1024,128]{2,1,0:T(8,128)(2,1)S(1)}, u32[]{:S(2)}, u32[]{:S(2)}) %collective-permute-start.5) | collective-permute-done | bytes 1048608 | tf_op jit(solution)/shard_map/ppermute | solution.py:682
  662.8 24.4 %middle.7 = (bf16[4,1024,128]{2,1,0:T(8,128)(2,1)}, bf16[4,1024,128]{2,1,0:T(8,128)(2,1)}, bf16[4,1024,128]{2,1,0:T(8,128)(2,1)}, bf16[4,1024,128]{2,1,0:T(8,128...) custom-call(bf16[4,1024,128]{2,1,0:T(8,128)(2,1)} %get-tuple-element.108.r, ...), custom_call_target="tpu_custom_call", output_to_operand_aliasing={{4}: (6, {}), {5}: (7, {})} | custom-call | tf_op jit(solution)/shard_map/middle/pallas_call | solution.py:409
  739.1 12.5 %collective-permute-done.7.refs_3_ = bf16[4,1024,128]{2,1,0:T(8,128)(2,1)S(1)} collective-permute-done((bf16[4,1024,128]{2,1,0:T(8,128)(2,1)}, bf16[4,1024,128]{2,1,0:T(8,128)(2,1)S(1)}, u32[]{:S(2)}, u32[]{:S(2)}) %collective-permute-start.7) | collective-permute-done | bytes 1048608 | tf_op jit(solution)/shard_map/ppermute | solution.py:682
  761.6 11.9 %collective-permute-done.12.refs_5_ = bf16[4,1024,128]{2,1,0:T(8,128)(2,1)S(1)} collective-permute-done((bf16[4,1024,128]{2,1,0:T(8,128)(2,1)}, bf16[4,1024,128]{2,1,0:T(8,128)(2,1)S(1)}, u32[]{:S(2)}, u32[]{:S(2)}) %collective-permute-start.12) | collective-permute-done | bytes 1048608 | tf_op jit(solution)/shard_map/ppermute | solution.py:682
  804.6 37.3 %all-to-all-done.8.refs_2_ = bf16[16,1,64,1024]{3,2,1,0:T(8,128)(2,1)S(1)} async-done(((bf16[16,1,64,1024]{3,2,1,0:T(8,128)(2,1)}), bf16[16,1,64,1024]{3,2,1,0:T(8,128)(2,1)S(1)}, u32[]{:S(2)}, u32[]{:S(2)}) %all-to-all-start.8) | async-done | bytes 2097184 | tf_op jit(solution)/shard_map/all_to_all | solution.py:678
  857.4 96.4 %collective-permute-done.14 = bf16[256,256]{1,0:T(8,128)(2,1)S(1)} collective-permute-done((bf16[256,256]{1,0:T(8,128)(2,1)}, bf16[256,256]{1,0:T(8,128)(2,1)S(1)}, u32[]{:S(2)}, u32[]{:S(2)}) %collective-permute-start.14) | collective-permute-done | bytes 131104 | tf_op jit(solution)/shard_map/ppermute | solution.py:795
  960.0 21.2 %collective-permute-done.11 = bf16[1024,256]{1,0:T(8,128)(2,1)S(1)} collective-permute-done((bf16[1024,256]{1,0:T(8,128)(2,1)}, bf16[1024,256]{1,0:T(8,128)(2,1)S(1)}, u32[]{:S(2)}, u32[]{:S(2)}) %collective-permute-start.11) | collective-permute-done | bytes 524320 | tf_op jit(solution)/shard_map/ppermute | solution.py:795
  986.8 54.4 %all-gather.3.cloned.1.call-done = bf16[8192,256]{1,0:T(8,128)(2,1)} async-done(((bf16[1024,256]{1,0:T(8,128)(2,1)}), bf16[8192,256]{1,0:T(8,128)(2,1)}) %all-gather.3.cloned.1.call-update) | async-done | bytes 4194320 | tf_op jit(solution)/shard_map/all_gather | solution.py:798
  1049.9 11.5 %last.1 = bf16[16,256,1024]{2,1,0:T(8,128)(2,1)} custom-call(bf16[256,256]{1,0:T(8,128)(2,1)} %w_ref.13, f32[256,16]{1,0:T(8,128)} %bitcast.72, bf16[16,2,64,1024]{3,2,1,0:T(8,128)(2,1)} %all-to-all-done.7.refs_0_, bf16[16,2,64,1024]{3,2,1,0:T(8,128)(2,1)} %all-to-all-done.6.refs_1_, bf16[16,1,64,1024]{3,2,1,0:T(8,128)(2,1)} %copy-done.1, ...), custom_call_target="tpu_custom_call" | custom-call | tf_op jit(solution)/shard_map/last/pallas_call | solution.py:557
  (117 shorter events, 299.2 us)
Async XLA Ops:
  13.9 48.4 %all-to-all-start.2 = ((bf16[16,1,64,1024]{3,2,1,0:T(8,128)(2,1)}), bf16[16,1,64,1024]{3,2,1,0:T(8,128)(2,1)S(1)}, u32[]{:S(2)}, u32[]{:S(2)}) async-start(bf16[16,1,64,1024]{3,2,1,0:T(8,128)(2,1)} %first.3), calls=%async_computation.2 | async-start | bytes 4194304 | tf_op jit(solution)/shard_map/all_to_all | solution.py:678
  63.6 52.2 %all-to-all-start = ((bf16[16,1,64,1024]{3,2,1,0:T(8,128)(2,1)}), bf16[16,1,64,1024]{3,2,1,0:T(8,128)(2,1)S(1)}, u32[]{:S(2)}, u32[]{:S(2)}) async-start(bf16[16,1,64,1024]{3,2,1,0:T(8,128)(2,1)} %get-tuple-element.81), calls=%async_computation | async-start | bytes 4194304 | tf_op jit(solution)/shard_map/all_to_all | solution.py:678
  117.1 88.8 %all-to-all-start.3 = ((bf16[16,2,64,1024]{3,2,1,0:T(8,128)(2,1)}), bf16[16,2,64,1024]{3,2,1,0:T(8,128)(2,1)}, u32[]{:S(2)}, u32[]{:S(2)}) async-start(bf16[16,2,64,1024]{3,2,1,0:T(8,128)(2,1)} %bitcast.59), calls=%async_computation.3 | async-start | bytes 8388608 | tf_op jit(solution)/shard_map/all_to_all | solution.py:678
  205.9 220.3 %all-to-all-start.1 = ((bf16[16,2,64,1024]{3,2,1,0:T(8,128)(2,1)}), bf16[16,2,64,1024]{3,2,1,0:T(8,128)(2,1)}, u32[]{:S(2)}, u32[]{:S(2)}) async-start(bf16[16,2,64,1024]{3,2,1,0:T(8,128)(2,1)} %bitcast.57), calls=%async_computation.1 | async-start | bytes 8388608 | tf_op jit(solution)/shard_map/all_to_all | solution.py:678
  249.4 93.7 %collective-permute-start.1 = (bf16[4,4096,128]{2,1,0:T(8,128)(2,1)}, bf16[4,4096,128]{2,1,0:T(8,128)(2,1)S(1)}, u32[]{:S(2)}, u32[]{:S(2)}) collective-permute-start(bf16[4,4096,128]{2,1,0:T(8,128)(2,1)} %get-tuple-element.89), channel_id=1, source_target_pairs={{0,1},{1,0},{2,3},{3,2},{4,5},{5,4},{6,7},{7,6},{8,9},{9,8},{10,11... | collective-permute-start | bytes 12582920 | tf_op jit(solution)/shard_map/ppermute | solution.py:682
  256.9 108.0 %collective-permute-start.2 = (bf16[4,1024,128]{2,1,0:T(8,128)(2,1)}, bf16[4,1024,128]{2,1,0:T(8,128)(2,1)S(1)}, u32[]{:S(2)}, u32[]{:S(2)}) collective-permute-start(bf16[4,1024,128]{2,1,0:T(8,128)(2,1)} %get-tuple-element.94), channel_id=1, source_target_pairs={{0,1},{1,0},{2,3},{3,2},{4,5},{5,4},{6,7},{7,6},{8,9},{9,8},{10,11... | collective-permute-start | bytes 3145736 | tf_op jit(solution)/shard_map/ppermute | solution.py:682
  426.2 98.7 %all-to-all-start.5 = ((bf16[16,2,64,1024]{3,2,1,0:T(8,128)(2,1)}), bf16[16,2,64,1024]{3,2,1,0:T(8,128)(2,1)}, u32[]{:S(2)}, u32[]{:S(2)}) async-start(bf16[16,2,64,1024]{3,2,1,0:T(8,128)(2,1)} %get-tuple-element.110), calls=%async_computation.5 | async-start | bytes 8388608 | tf_op jit(solution)/shard_map/all_to_all | solution.py:678
  524.9 98.8 %all-to-all-start.4 = ((bf16[16,2,64,1024]{3,2,1,0:T(8,128)(2,1)}), bf16[16,2,64,1024]{3,2,1,0:T(8,128)(2,1)}, u32[]{:S(2)}, u32[]{:S(2)}) async-start(bf16[16,2,64,1024]{3,2,1,0:T(8,128)(2,1)} %get-tuple-element.106), calls=%async_computation.4 | async-start | bytes 8388608 | tf_op jit(solution)/shard_map/all_to_all | solution.py:678
  623.7 164.7 %all-to-all-start.7 = ((bf16[16,2,64,1024]{3,2,1,0:T(8,128)(2,1)}), bf16[16,2,64,1024]{3,2,1,0:T(8,128)(2,1)}, u32[]{:S(2)}, u32[]{:S(2)}) async-start(bf16[16,2,64,1024]{3,2,1,0:T(8,128)(2,1)} %get-tuple-element.145), calls=%async_computation.9 | async-start | bytes 8388608 | tf_op jit(solution)/shard_map/all_to_all | solution.py:678
  629.3 225.0 %reduce-scatter.5.cloned.1.call-start = ((), (), s32[]{:S(2)}) async-start(), calls=%async_computation.14 | async-start | bytes 1179648 | tf_op jit(solution)/shard_map/reduce_scatter | solution.py:792
  635.5 26.2 %collective-permute-start.5 = (bf16[4,1024,128]{2,1,0:T(8,128)(2,1)}, bf16[4,1024,128]{2,1,0:T(8,128)(2,1)S(1)}, u32[]{:S(2)}, u32[]{:S(2)}) collective-permute-start(bf16[4,1024,128]{2,1,0:T(8,128)(2,1)} %get-tuple-element.109), channel_id=1, source_target_pairs={{0,1},{1,0},{2,3},{3,2},{4,5},{5,4},{6,7},{7,6},{8,9},{9,8},{10,11... | collective-permute-start | bytes 3145736 | tf_op jit(solution)/shard_map/ppermute | solution.py:682
  637.1 52.2 %collective-permute-start.10 = (bf16[4,1024,128]{2,1,0:T(8,128)(2,1)}, bf16[4,1024,128]{2,1,0:T(8,128)(2,1)S(1)}, u32[]{:S(2)}, u32[]{:S(2)}) collective-permute-start(bf16[4,1024,128]{2,1,0:T(8,128)(2,1)} %get-tuple-element.125), channel_id=1, source_target_pairs={{0,1},{1,0},{2,3},{3,2},{4,5},{5,4},{6,7},{7,6},{8,9},{9,8},{10,11... | collective-permute-start | bytes 3145736 | tf_op jit(solution)/shard_map/ppermute | solution.py:682
  637.6 69.2 %collective-permute-start.9 = (bf16[4,1024,128]{2,1,0:T(8,128)(2,1)}, bf16[4,1024,128]{2,1,0:T(8,128)(2,1)S(1)}, u32[]{:S(2)}, u32[]{:S(2)}) collective-permute-start(bf16[4,1024,128]{2,1,0:T(8,128)(2,1)} %get-tuple-element.123), channel_id=1, source_target_pairs={{0,1},{1,0},{2,3},{3,2},{4,5},{5,4},{6,7},{7,6},{8,9},{9,8},{10,11... | collective-permute-start | bytes 3145736 | tf_op jit(solution)/shard_map/ppermute | solution.py:682
  639.1 90.1 %collective-permute-start.8 = (bf16[4,1024,128]{2,1,0:T(8,128)(2,1)}, bf16[4,1024,128]{2,1,0:T(8,128)(2,1)S(1)}, u32[]{:S(2)}, u32[]{:S(2)}) collective-permute-start(bf16[4,1024,128]{2,1,0:T(8,128)(2,1)} %get-tuple-element.121), channel_id=1, source_target_pairs={{0,1},{1,0},{2,3},{3,2},{4,5},{5,4},{6,7},{7,6},{8,9},{9,8},{10,11... | collective-permute-start | bytes 3145736 | tf_op jit(solution)/shard_map/ppermute | solution.py:682
  687.2 64.5 %collective-permute-start.7 = (bf16[4,1024,128]{2,1,0:T(8,128)(2,1)}, bf16[4,1024,128]{2,1,0:T(8,128)(2,1)S(1)}, u32[]{:S(2)}, u32[]{:S(2)}) collective-permute-start(bf16[4,1024,128]{2,1,0:T(8,128)(2,1)} %get-tuple-element.118), channel_id=1, source_target_pairs={{0,1},{1,0},{2,3},{3,2},{4,5},{5,4},{6,7},{7,6},{8,9},{9,8},{10,11... | collective-permute-start | bytes 3145736 | tf_op jit(solution)/shard_map/ppermute | solution.py:682
  688.8 84.8 %collective-permute-start.12 = (bf16[4,1024,128]{2,1,0:T(8,128)(2,1)}, bf16[4,1024,128]{2,1,0:T(8,128)(2,1)S(1)}, u32[]{:S(2)}, u32[]{:S(2)}) collective-permute-start(bf16[4,1024,128]{2,1,0:T(8,128)(2,1)} %get-tuple-element.136), channel_id=1, source_target_pairs={{0,1},{1,0},{2,3},{3,2},{4,5},{5,4},{6,7},{7,6},{8,9},{9,8},{10,11... | collective-permute-start | bytes 3145736 | tf_op jit(solution)/shard_map/ppermute | solution.py:682
  792.9 49.0 %all-to-all-start.8 = ((bf16[16,1,64,1024]{3,2,1,0:T(8,128)(2,1)}), bf16[16,1,64,1024]{3,2,1,0:T(8,128)(2,1)S(1)}, u32[]{:S(2)}, u32[]{:S(2)}) async-start(bf16[16,1,64,1024]{3,2,1,0:T(8,128)(2,1)} %bitcast.62), calls=%async_computation.10 | async-start | bytes 4194304 | tf_op jit(solution)/shard_map/all_to_all | solution.py:678
  798.6 156.9 %reduce-scatter.3.cloned.1.call-start = ((), (), s32[]{:S(2)}) async-start(), calls=%async_computation.12 | async-start | bytes 4718592 | tf_op jit(solution)/shard_map/reduce_scatter | solution.py:792
  843.2 112.4 %all-to-all-start.6 = ((bf16[16,2,64,1024]{3,2,1,0:T(8,128)(2,1)}), bf16[16,2,64,1024]{3,2,1,0:T(8,128)(2,1)}, u32[]{:S(2)}, u32[]{:S(2)}) async-start(bf16[16,2,64,1024]{3,2,1,0:T(8,128)(2,1)} %get-tuple-element.141), calls=%async_computation.7 | async-start | bytes 8388608 | tf_op jit(solution)/shard_map/all_to_all | solution.py:678
  854.2 132.6 %all-gather.5.cloned.1.call-start = ((), (), s32[]{:S(2)}) async-start(), calls=%async_computation.15 | async-start | bytes 1179648 | tf_op jit(solution)/shard_map/all_gather | solution.py:798
  854.3 99.5 %collective-permute-start.14 = (bf16[256,256]{1,0:T(8,128)(2,1)}, bf16[256,256]{1,0:T(8,128)(2,1)S(1)}, u32[]{:S(2)}, u32[]{:S(2)}) collective-permute-start(bf16[256,256]{1,0:T(8,128)(2,1)} %reduce-scatter.5.cloned.1.call-done), channel_id=1, source_target_pairs={{0,16},{2,18},{4,20},{6,22},{8,24},{10,26},{12,28},{14,30},{16,0},... | collective-permute-start | bytes 393224 | tf_op jit(solution)/shard_map/ppermute | solution.py:795
  955.4 85.8 %all-gather.3.cloned.1.call-start = ((), (), s32[]{:S(2)}) async-start(), calls=%async_computation.13 | async-start | bytes 4718592 | tf_op jit(solution)/shard_map/all_gather | solution.py:798
  955.5 25.7 %collective-permute-start.11 = (bf16[1024,256]{1,0:T(8,128)(2,1)}, bf16[1024,256]{1,0:T(8,128)(2,1)S(1)}, u32[]{:S(2)}, u32[]{:S(2)}) collective-permute-start(bf16[1024,256]{1,0:T(8,128)(2,1)} %reduce-scatter.3.cloned.1.call-done), channel_id=1, source_target_pairs={{0,16},{2,18},{4,20},{6,22},{8,24},{10,26},{12,28},{14,30},{16,0},... | collective-permute-start | bytes 1572872 | tf_op jit(solution)/shard_map/ppermute | solution.py:795
  982.1 66.4 %all-to-all-start.9 = ((bf16[16,1,64,1024]{3,2,1,0:T(8,128)(2,1)}), bf16[16,1,64,1024]{3,2,1,0:T(8,128)(2,1)S(1)}, u32[]{:S(2)}, u32[]{:S(2)}) async-start(bf16[16,1,64,1024]{3,2,1,0:T(8,128)(2,1)} %bitcast.61), calls=%async_computation.11 | async-start | bytes 4194304 | tf_op jit(solution)/shard_map/all_to_all | solution.py:678
  (25 other events, 261.6 us)
Sparse Core Ops, SparseCore 0:
  788.5 41.7 reduce-scatter.4
  832.5 89.7 reduce-scatter.2
  955.5 29.9 all-gather.4
  987.6 53.5 all-gather.2

commit v5 on v4

--- a/solution.py
+++ b/solution.py
@@ -8,6 +8,23 @@
 from jax.sharding import PartitionSpec as P
 
 
+FIRST = "first"
+PREPARE = "prepare"
+BACK = "back"
+SECOND = "second"
+HIDDEN = "hidden"
+MIDDLE = "middle"
+INPUTS = "inputs"
+OUTPUTS = "outputs"
+FOURTH = "fourth"
+COLLECT = "collect"
+FINISH = "finish"
+UP = "up"
+GRAD = "grad"
+DOWN = "down"
+SEQ = "seq"
+FSDP = "fsdp"
+BASE = "base"
 NBLK = 8
 LANES = 128
 CHUNKS = 4
@@ -39,13 +56,13 @@
 
 def column_pass(field, factor):
     result = product(
-        "ajc,ai->ijc", lax.all_to_all(field, "seq", split_axis=1, concat_axis=0, tiled=True), factor
+        "ajc,ai->ijc", lax.all_to_all(field, SEQ, split_axis=1, concat_axis=0, tiled=True), factor
     ).astype(jnp.bfloat16)
-    return lax.all_to_all(result, "seq", split_axis=0, concat_axis=1, tiled=True)
+    return lax.all_to_all(result, SEQ, split_axis=0, concat_axis=1, tiled=True)
 
 
 def shuffle_blocks(values):
-    return lax.all_to_all(values, "fsdp", split_axis=2, concat_axis=1, tiled=True)
+    return lax.all_to_all(values, FSDP, split_axis=2, concat_axis=1, tiled=True)
 
 
 def spread_blocks(values):
@@ -120,7 +137,7 @@
     output, grad_hidden, grads = blocks_layer(
         hidden, grad_out, up_first, up_second, down_first, down_second
     )
-    totals = lax.psum((grads[0], grads[1], grads[2], grads[3]), "seq")
+    totals = lax.psum((grads[0], grads[1], grads[2], grads[3]), SEQ)
     grad_float = grad_hidden.astype(jnp.float32)
     grad_mixed = (grad_float * gating).astype(jnp.bfloat16)
     back_rows = column_pass(grad_mixed.reshape(block_rows, length, local_channels), mix_second.T)
@@ -229,7 +246,6 @@
         out_shape=[in_hbm((seq, parts, height, channels)) for _, parts in places],
         scratch_shapes=[pltpu.VMEM((rows, span * len(chunks), cols), BF)],
         compiler_params=params(0),
-        name="first",
     )(x3, mix_first, twiddle)
 
 
@@ -260,7 +276,6 @@
         out_shape=in_hbm((seq, parts, own, rows, channels)),
         input_output_aliases={} if buffer is None else {2: 0},
         compiler_params=params(0),
-        name="second",
     )(weight, five, *(() if buffer is None else (buffer.reshape(seq, parts, own, rows, channels),)))
     return out.reshape(seq, parts, height, channels)
 
@@ -320,7 +335,6 @@
         out_specs=[spec, spec],
         out_shape=[shape, shape],
         compiler_params=params(0),
-        name="back",
     )(g3, down_second)
 
 
@@ -415,7 +429,6 @@
         + [jax.ShapeDtypeStruct(up_second.shape, F32), jax.ShapeDtypeStruct(down_first.shape, F32)],
         input_output_aliases={6: 4, 7: 5},
         compiler_params=params(0, 0),
-        name="middle",
     )(up_own, up_recv, back_own, back_recv, up_second, down_first, *sums)
 
 
@@ -617,7 +630,6 @@
         out_shape=[jax.ShapeDtypeStruct(w.shape, BF) for w in weights]
         + [jax.ShapeDtypeStruct(w.shape, F32) for w in weights[:3]],
         compiler_params=params(0),
-        name="prepare",
     )(mine, *weights)
 
 
@@ -639,7 +651,6 @@
         out_specs=pl.BlockSpec((1, height, width), lambda g: (g, 0, 0)),
         out_shape=jax.ShapeDtypeStruct((blocks, height, width), BF),
         compiler_params=params(0),
-        name="collect",
     )(*sums)
 
 
@@ -670,29 +681,28 @@
         ),
         out_shape=[jax.ShapeDtypeStruct(w.shape, F32) for w in weights],
         compiler_params=params(0),
-        name="finish",
     )(mine, *wholes)
 
 
 def exchange(field):
-    return lax.all_to_all(field, "seq", split_axis=0, concat_axis=0, tiled=True)
+    return lax.all_to_all(field, SEQ, split_axis=0, concat_axis=0, tiled=True)
 
 
 def partner(values):
-    return lax.ppermute(values, "fsdp", [(0, 1), (1, 0)])
+    return lax.ppermute(values, FSDP, [(0, 1), (1, 0)])
 
 
 PLAN = (
-    (((1, 0),), (("first", 1), ("prepare", 0), ("back", 0))),
-    (((1, 1),), (("second", 0),)),
-    (((2, 0), (1, 2)), (("second", 1),)),
-    (((2, 1), (1, 3)), (("hidden", 0), ("second", 2), ("middle", 0), ("inputs", 0))),
-    (((2, 2), (3, 0)), (("hidden", 1), ("second", 3), ("middle", 1), ("outputs", 0), ("inputs", 1))),
-    (((2, 3), (3, 1)), (("hidden", 2), ("fourth", 0), ("middle", 2), ("outputs", 1), ("inputs", 2))),
-    (((3, 2), (4, 0)), (("hidden", 3), ("fourth", 1), ("middle", 3), ("collect", 0), ("outputs", 2), ("inputs", 3))),
-    (((3, 3), (4, 1)), (("fourth", 2), ("outputs", 3), ("collect", 1))),
-    (((4, 2),), (("fourth", 3),)),
-    (((4, 3),), (("finish", 0),)),
+    (((1, 0),), ((FIRST, 1), (PREPARE, 0), (BACK, 0))),
+    (((1, 1),), ((SECOND, 0),)),
+    (((2, 0), (1, 2)), ((SECOND, 1),)),
+    (((2, 1), (1, 3)), ((HIDDEN, 0), (SECOND, 2), (MIDDLE, 0), (INPUTS, 0))),
+    (((2, 2), (3, 0)), ((HIDDEN, 1), (SECOND, 3), (MIDDLE, 1), (OUTPUTS, 0), (INPUTS, 1))),
+    (((2, 3), (3, 1)), ((HIDDEN, 2), (FOURTH, 0), (MIDDLE, 2), (OUTPUTS, 1), (INPUTS, 2))),
+    (((3, 2), (4, 0)), ((HIDDEN, 3), (FOURTH, 1), (MIDDLE, 3), (COLLECT, 0), (OUTPUTS, 2), (INPUTS, 3))),
+    (((3, 3), (4, 1)), ((FOURTH, 2), (OUTPUTS, 3), (COLLECT, 1))),
+    (((4, 2),), ((FOURTH, 3),)),
+    (((4, 3),), ((FINISH, 0),)),
 )
 
 
@@ -714,7 +724,7 @@
 ):
     local_rows, channels = activations.shape
     rows, length = twiddle.shape
-    mine = lax.axis_index("fsdp").astype(jnp.int32).reshape(1)
+    mine = lax.axis_index(FSDP).astype(jnp.int32).reshape(1)
     weights = (up_first, up_second, down_first, down_second)
 
     x3 = activations.reshape(rows, length, channels)
@@ -748,40 +758,38 @@
         for part, key in enumerate(travels):
             arrived[key] = (done, part)
         for name, n in tasks:
-            if name == "first":
+            if name == FIRST:
                 first(tuple(range(1, CHUNKS)))
-            elif name == "back":
+            elif name == BACK:
                 own, send = back_stage(g3, downs_second)
                 back = (own, partner(send))
-            elif name == "second":
+            elif name == SECOND:
                 buffers[place[2, n][0]] = second_stage(w2t, arrived[1, n], *spot((2, n)), rows)
-            elif name == "hidden":
+            elif name == HIDDEN:
                 hidden, own, send = hidden_stage(n, x3, arrived[2, n], ups_first)
-                kept["hidden", n] = hidden
-                kept["up", n] = (own, partner(send))
-            elif name == "middle":
+                kept[HIDDEN, n] = hidden
+                kept[UP, n] = (own, partner(send))
+            elif name == MIDDLE:
                 down_own, down_send, grad_own, grad_send, *sums = middle_stage(
-                    n, *kept["up", n], *back, ups_second, downs_first, sums
+                    n, *kept[UP, n], *back, ups_second, downs_first, sums
                 )
-                kept["grad", n] = (grad_own, partner(grad_send))
-                kept["down", n] = (down_own, partner(down_send))
-            elif name == "inputs":
-                buffers[place[3, n][0]], kept["base", n], sum_first = input_stage(
+                kept[GRAD, n] = (grad_own, partner(grad_send))
+                kept[DOWN, n] = (down_own, partner(down_send))
+            elif name == INPUTS:
+                buffers[place[3, n][0]], kept[BASE, n], sum_first = input_stage(
                     n,
                     x3,
                     g3,
                     arrived[2, n],
-                    kept["hidden", n],
-                    *kept["grad", n],
+                    kept[HIDDEN, n],
+                    *kept[GRAD, n],
                     ups_first,
                     sum_first,
                     *spot((3, n)),
                 )
-            elif name == "outputs":
-                output, sum_last = output_stage(
-                    n, g3, kept["hidden", n], *kept["down", n], downs_second, sum_last, output
-                )
-            elif name == "fourth":
+            elif name == OUTPUTS:
+                output, sum_last = output_stage(n, g3, kept[HIDDEN, n], *kept[DOWN, n], downs_second, sum_last, output)
+            elif name == FOURTH:
                 buffers[place[4, n][0]] = second_stage(w2, arrived[3, n], *spot((4, n)), rows)
 
     width = up_first.shape[1]
@@ -790,17 +798,17 @@
     for n, values in enumerate((sums, (sum_first, sum_last))):
         collected = collect_stage(1.0 / length, width, values)
         part = lax.psum_scatter(
-            collected.reshape(-1, width), "seq", scatter_dimension=0, axis_index_groups=halves, tiled=True
+            collected.reshape(-1, width), SEQ, scatter_dimension=0, axis_index_groups=halves, tiled=True
         )
-        other = lax.ppermute(part, "seq", [(d, (d + seq // 2) % seq) for d in range(seq)])
+        other = lax.ppermute(part, SEQ, [(d, (d + seq // 2) % seq) for d in range(seq)])
         other = tie(other, after[n])
         part = (part.astype(F32) + other.astype(F32)).astype(BF)
-        whole = lax.all_gather(part, "seq", axis=0, axis_index_groups=halves, tiled=True)
+        whole = lax.all_gather(part, SEQ, axis=0, axis_index_groups=halves, tiled=True)
         wholes.append(whole.reshape(collected.shape))
     grads = finish_stage(mine, wholes, weights)
     tw_cols = tie(tw_cols, grads)
     fields = [arrived[4, n] for n in range(CHUNKS)]
-    bases = [kept["base", n] for n in range(CHUNKS)]
+    bases = [kept[BASE, n] for n in range(CHUNKS)]
     grad_inputs = last_stage(rows, length, mix_first, tw_cols, fields, bases)
     return (
         output.reshape(local_rows, channels),
@@ -828,22 +836,22 @@
 
 def solution(mesh):
     in_specs = (
-        P("seq", "fsdp"),
+        P(SEQ, FSDP),
         P(),
-        P("seq", None),
+        P(SEQ, None),
         P(),
-        P("fsdp", None, None),
-        P("fsdp", None, None),
-        P("fsdp", None, None),
-        P("fsdp", None, None),
-        P("seq", "fsdp"),
+        P(FSDP, None, None),
+        P(FSDP, None, None),
+        P(FSDP, None, None),
+        P(FSDP, None, None),
+        P(SEQ, FSDP),
     )
     out_specs = (
-        P("seq", "fsdp"),
-        P("seq", "fsdp"),
-        P("fsdp", None, None),
-        P("fsdp", None, None),
-        P("fsdp", None, None),
-        P("fsdp", None, None),
+        P(SEQ, FSDP),
+        P(SEQ, FSDP),
+        P(FSDP, None, None),
+        P(FSDP, None, None),
+        P(FSDP, None, None),
+        P(FSDP, None, None),
     )
     return jax.shard_map(shards, mesh=mesh, in_specs=in_specs, out_specs=out_specs, check_vma=False)

time: 1070 us -> 1070 us (level)
  no operation moved by 1% of the time
where the time goes in v5:
time: 1070 us
  waiting for transfers between devices  626 us (59%)
  Pallas kernels  300 us (28%)
  starting transfers between devices  106 us (10%)
  local copies, waits for them, and re-layouts  18.6 us (2%)
  between operations  14 us (1%)
    ppermute x13, waiting for transfers between devices, partner(): return lax.ppermute(values, FSDP, [(0, 1), (1, 0)])  275 us
    all_to_all x10, waiting for transfers between devices, exchange(): return lax.all_to_all(field, SEQ, split_axis=0, concat_axis=0, tiled=True)  179 us
    ppermute x2, waiting for transfers between devices, chunked_shards(): lax.ppermute(part, SEQ, [(d, (d + seq // 2) % seq) for d in range(seq)])  118 us
    pallas_call x4, Pallas kernels, middle_stage(): pl.pallas_call(functools.partial(middle_kernel, cols), grid=(blocks, step...  97.5 us
    all_to_all x10, starting transfers between devices, exchange(): return lax.all_to_all(field, SEQ, split_axis=0, concat_axis=0, tiled=True)  86.7 us
    all_gather x2, waiting for transfers between devices, chunked_shards(): lax.all_gather(part, SEQ, axis=0, axis_index_groups=halves, tiled=True)  54.4 us
    pallas_call x4, Pallas kernels, input_stage(): offset_call(input_kernel, (chunk, part), steps, [natural, natural, arrivi...  41 us
    pallas_call x4, Pallas kernels, output_stage(): offset_call(functools.partial(output_kernel, fresh), (chunk,), steps, [na...  35.6 us
  transfers between devices with their start and end apart: 29, of which 19 were waited for; matrix products, arithmetic and copies ran while one was open for 0% of the time, Pallas kernels for 26%

profile of v5, /device:TPU:0, one launch (start us, length us, event | category | flops | bytes accessed | tf_op | source)
XLA Modules:
  0.0 1067.9 jit_solution(4360194990504691088)
XLA Ops:
  29.6 32.6 %all-to-all-done.2 = bf16[16,1,64,1024]{3,2,1,0:T(8,128)(2,1)S(1)} async-done(((bf16[16,1,64,1024]{3,2,1,0:T(8,128)(2,1)}), bf16[16,1,64,1024]{3,2,1,0:T(8,128)(2,1)S(1)}, u32[]{:S(2)}, u32[]{:S(2)}) %all-to-all-start.2) | async-done | bytes 2097184 | tf_op jit(solution)/shard_map/all_to_all | solution.py:688
  79.9 35.9 %all-to-all-done = bf16[16,1,64,1024]{3,2,1,0:T(8,128)(2,1)S(1)} async-done(((bf16[16,1,64,1024]{3,2,1,0:T(8,128)(2,1)}), bf16[16,1,64,1024]{3,2,1,0:T(8,128)(2,1)S(1)}, u32[]{:S(2)}, u32[]{:S(2)}) %all-to-all-start) | async-done | bytes 2097184 | tf_op jit(solution)/shard_map/all_to_all | solution.py:688
  132.7 73.2 %all-to-all-done.3.refs_1_.refs_2_ = bf16[16,2,64,1024]{3,2,1,0:T(8,128)(2,1)} async-done(((bf16[16,2,64,1024]{3,2,1,0:T(8,128)(2,1)}), bf16[16,2,64,1024]{3,2,1,0:T(8,128)(2,1)}, u32[]{:S(2)}, u32[]{:S(2)}) %all-to-all-start.3) | async-done | bytes 4194336 | tf_op jit(solution)/shard_map/all_to_all | solution.py:688
  205.9 19.7 %all-to-all-start.1 = ((bf16[16,2,64,1024]{3,2,1,0:T(8,128)(2,1)}), bf16[16,2,64,1024]{3,2,1,0:T(8,128)(2,1)}, u32[]{:S(2)}, u32[]{:S(2)}) async-start(bf16[16,2,64,1024]{3,2,1,0:T(8,128)(2,1)} %bitcast.57), calls=%async_computation.1 | async-start | bytes 8388608 | tf_op jit(solution)/shard_map/all_to_all | solution.py:688
  233.4 16.0 %shard_map.140 = (bf16[4,4096,128]{2,1,0:T(8,128)(2,1)}, bf16[4,4096,128]{2,1,0:T(8,128)(2,1)}) custom-call(bf16[16,256,1024]{2,1,0:T(8,128)(2,1)} %bitcast.41, bf16[4,256,256]{2,1,0:T(8,128)(2,1)} %get-tuple-element.87.w_ref.refs_4_), custom_call_target="tpu_custom_call" | custom-call | tf_op jit(solution)/shard_map/pallas_call | solution.py:331
  257.4 85.7 %collective-permute-done.1.refs_3_ = bf16[4,4096,128]{2,1,0:T(8,128)(2,1)S(1)} collective-permute-done((bf16[4,4096,128]{2,1,0:T(8,128)(2,1)}, bf16[4,4096,128]{2,1,0:T(8,128)(2,1)S(1)}, u32[]{:S(2)}, u32[]{:S(2)}) %collective-permute-start.1) | collective-permute-done | bytes 4194336 | tf_op jit(solution)/shard_map/ppermute | solution.py:692
  343.0 21.8 %collective-permute-done.2.refs_1_ = bf16[4,1024,128]{2,1,0:T(8,128)(2,1)S(1)} collective-permute-done((bf16[4,1024,128]{2,1,0:T(8,128)(2,1)}, bf16[4,1024,128]{2,1,0:T(8,128)(2,1)S(1)}, u32[]{:S(2)}, u32[]{:S(2)}) %collective-permute-start.2) | collective-permute-done | bytes 1048608 | tf_op jit(solution)/shard_map/ppermute | solution.py:692
  365.9 24.2 %shard_map.144 = (bf16[4,1024,128]{2,1,0:T(8,128)(2,1)}, bf16[4,1024,128]{2,1,0:T(8,128)(2,1)}, bf16[4,1024,128]{2,1,0:T(8,128)(2,1)}, bf16[4,1024,128]{2,1,0:T(...) custom-call(bf16[4,1024,128]{2,1,0:T(8,128)(2,1)} %get-tuple-element., ...), custom_call_target="tpu_custom_call", output_to_operand_aliasing={{4}: (6, {}), {5}: (7, {})} | custom-call | tf_op jit(solution)/shard_map/pallas_call | solution.py:423
  396.1 18.8 %collective-permute-done.4.refs_5_ = bf16[4,1024,128]{2,1,0:T(8,128)(2,1)S(1)} collective-permute-done((bf16[4,1024,128]{2,1,0:T(8,128)(2,1)}, bf16[4,1024,128]{2,1,0:T(8,128)(2,1)S(1)}, u32[]{:S(2)}, u32[]{:S(2)}) %collective-permute-start.4) | collective-permute-done | bytes 1048608 | tf_op jit(solution)/shard_map/ppermute | solution.py:692
  439.3 24.1 %collective-permute-done.refs_1_ = bf16[4,1024,128]{2,1,0:T(8,128)(2,1)S(1)} collective-permute-done((bf16[4,1024,128]{2,1,0:T(8,128)(2,1)}, bf16[4,1024,128]{2,1,0:T(8,128)(2,1)S(1)}, u32[]{:S(2)}, u32[]{:S(2)}) %collective-permute-start) | collective-permute-done | bytes 1048608 | tf_op jit(solution)/shard_map/ppermute | solution.py:692
  464.3 24.4 %shard_map.145 = (bf16[4,1024,128]{2,1,0:T(8,128)(2,1)}, bf16[4,1024,128]{2,1,0:T(8,128)(2,1)}, bf16[4,1024,128]{2,1,0:T(8,128)(2,1)}, bf16[4,1024,128]{2,1,0:T(...) custom-call(bf16[4,1024,128]{2,1,0:T(8,128)(2,1)} %get-tuple-element., ...), custom_call_target="tpu_custom_call", output_to_operand_aliasing={{4}: (6, {}), {5}: (7, {})} | custom-call | tf_op jit(solution)/shard_map/pallas_call | solution.py:423
  494.7 19.0 %collective-permute-done.3.refs_5_ = bf16[4,1024,128]{2,1,0:T(8,128)(2,1)S(1)} collective-permute-done((bf16[4,1024,128]{2,1,0:T(8,128)(2,1)}, bf16[4,1024,128]{2,1,0:T(8,128)(2,1)S(1)}, u32[]{:S(2)}, u32[]{:S(2)}) %collective-permute-start.3) | collective-permute-done | bytes 1048608 | tf_op jit(solution)/shard_map/ppermute | solution.py:692
  538.0 24.1 %collective-permute-done.6.refs_1_ = bf16[4,1024,128]{2,1,0:T(8,128)(2,1)S(1)} collective-permute-done((bf16[4,1024,128]{2,1,0:T(8,128)(2,1)}, bf16[4,1024,128]{2,1,0:T(8,128)(2,1)S(1)}, u32[]{:S(2)}, u32[]{:S(2)}) %collective-permute-start.6) | collective-permute-done | bytes 1048608 | tf_op jit(solution)/shard_map/ppermute | solution.py:692
  563.1 24.4 %shard_map.152 = (bf16[4,1024,128]{2,1,0:T(8,128)(2,1)}, bf16[4,1024,128]{2,1,0:T(8,128)(2,1)}, bf16[4,1024,128]{2,1,0:T(8,128)(2,1)}, bf16[4,1024,128]{2,1,0:T(...) custom-call(bf16[4,1024,128]{2,1,0:T(8,128)(2,1)} %get-tuple-element., ...), custom_call_target="tpu_custom_call", output_to_operand_aliasing={{4}: (6, {}), {5}: (7, {})} | custom-call | tf_op jit(solution)/shard_map/pallas_call | solution.py:423
  593.6 18.9 %collective-permute-done.13.refs_5_ = bf16[4,1024,128]{2,1,0:T(8,128)(2,1)S(1)} collective-permute-done((bf16[4,1024,128]{2,1,0:T(8,128)(2,1)}, bf16[4,1024,128]{2,1,0:T(8,128)(2,1)S(1)}, u32[]{:S(2)}, u32[]{:S(2)}) %collective-permute-start.13) | collective-permute-done | bytes 1048608 | tf_op jit(solution)/shard_map/ppermute | solution.py:692
  639.6 22.2 %collective-permute-done.5.refs_1_ = bf16[4,1024,128]{2,1,0:T(8,128)(2,1)S(1)} collective-permute-done((bf16[4,1024,128]{2,1,0:T(8,128)(2,1)}, bf16[4,1024,128]{2,1,0:T(8,128)(2,1)S(1)}, u32[]{:S(2)}, u32[]{:S(2)}) %collective-permute-start.5) | collective-permute-done | bytes 1048608 | tf_op jit(solution)/shard_map/ppermute | solution.py:692
  662.8 24.4 %shard_map.153 = (bf16[4,1024,128]{2,1,0:T(8,128)(2,1)}, bf16[4,1024,128]{2,1,0:T(8,128)(2,1)}, bf16[4,1024,128]{2,1,0:T(8,128)(2,1)}, bf16[4,1024,128]{2,1,0:T(...) custom-call(bf16[4,1024,128]{2,1,0:T(8,128)(2,1)} %get-tuple-element., ...), custom_call_target="tpu_custom_call", output_to_operand_aliasing={{4}: (6, {}), {5}: (7, {})} | custom-call | tf_op jit(solution)/shard_map/pallas_call | solution.py:423
  739.1 12.5 %collective-permute-done.7.refs_3_ = bf16[4,1024,128]{2,1,0:T(8,128)(2,1)S(1)} collective-permute-done((bf16[4,1024,128]{2,1,0:T(8,128)(2,1)}, bf16[4,1024,128]{2,1,0:T(8,128)(2,1)S(1)}, u32[]{:S(2)}, u32[]{:S(2)}) %collective-permute-start.7) | collective-permute-done | bytes 1048608 | tf_op jit(solution)/shard_map/ppermute | solution.py:692
  761.6 11.9 %collective-permute-done.12.refs_5_ = bf16[4,1024,128]{2,1,0:T(8,128)(2,1)S(1)} collective-permute-done((bf16[4,1024,128]{2,1,0:T(8,128)(2,1)}, bf16[4,1024,128]{2,1,0:T(8,128)(2,1)S(1)}, u32[]{:S(2)}, u32[]{:S(2)}) %collective-permute-start.12) | collective-permute-done | bytes 1048608 | tf_op jit(solution)/shard_map/ppermute | solution.py:692
  804.6 37.3 %all-to-all-done.8.refs_2_ = bf16[16,1,64,1024]{3,2,1,0:T(8,128)(2,1)S(1)} async-done(((bf16[16,1,64,1024]{3,2,1,0:T(8,128)(2,1)}), bf16[16,1,64,1024]{3,2,1,0:T(8,128)(2,1)S(1)}, u32[]{:S(2)}, u32[]{:S(2)}) %all-to-all-start.8) | async-done | bytes 2097184 | tf_op jit(solution)/shard_map/all_to_all | solution.py:688
  857.4 96.4 %collective-permute-done.14 = bf16[256,256]{1,0:T(8,128)(2,1)S(1)} collective-permute-done((bf16[256,256]{1,0:T(8,128)(2,1)}, bf16[256,256]{1,0:T(8,128)(2,1)S(1)}, u32[]{:S(2)}, u32[]{:S(2)}) %collective-permute-start.14) | collective-permute-done | bytes 131104 | tf_op jit(solution)/shard_map/ppermute | solution.py:803
  960.0 21.2 %collective-permute-done.11 = bf16[1024,256]{1,0:T(8,128)(2,1)S(1)} collective-permute-done((bf16[1024,256]{1,0:T(8,128)(2,1)}, bf16[1024,256]{1,0:T(8,128)(2,1)S(1)}, u32[]{:S(2)}, u32[]{:S(2)}) %collective-permute-start.11) | collective-permute-done | bytes 524320 | tf_op jit(solution)/shard_map/ppermute | solution.py:803
  986.8 54.4 %all-gather.3.cloned.1.call-done = bf16[8192,256]{1,0:T(8,128)(2,1)} async-done(((bf16[1024,256]{1,0:T(8,128)(2,1)}), bf16[8192,256]{1,0:T(8,128)(2,1)}) %all-gather.3.cloned.1.call-update) | async-done | bytes 4194320 | tf_op jit(solution)/shard_map/all_gather | solution.py:806
  1049.9 11.5 %last.1 = bf16[16,256,1024]{2,1,0:T(8,128)(2,1)} custom-call(bf16[256,256]{1,0:T(8,128)(2,1)} %w_ref.13, f32[256,16]{1,0:T(8,128)} %bitcast.72, bf16[16,2,64,1024]{3,2,1,0:T(8,128)(2,1)} %all-to-all-done.7.refs_0_, bf16[16,2,64,1024]{3,2,1,0:T(8,128)(2,1)} %all-to-all-done.6.refs_1_, bf16[16,1,64,1024]{3,2,1,0:T(8,128)(2,1)} %copy-done.1, ...), custom_call_target="tpu_custom_call" | custom-call | tf_op jit(solution)/shard_map/last/pallas_call | solution.py:570
  (117 shorter events, 299.2 us)
Async XLA Ops:
  13.9 48.4 %all-to-all-start.2 = ((bf16[16,1,64,1024]{3,2,1,0:T(8,128)(2,1)}), bf16[16,1,64,1024]{3,2,1,0:T(8,128)(2,1)S(1)}, u32[]{:S(2)}, u32[]{:S(2)}) async-start(bf16[16,1,64,1024]{3,2,1,0:T(8,128)(2,1)} %shard_map.141), calls=%async_computation.2 | async-start | bytes 4194304 | tf_op jit(solution)/shard_map/all_to_all | solution.py:688
  63.6 52.2 %all-to-all-start = ((bf16[16,1,64,1024]{3,2,1,0:T(8,128)(2,1)}), bf16[16,1,64,1024]{3,2,1,0:T(8,128)(2,1)S(1)}, u32[]{:S(2)}, u32[]{:S(2)}) async-start(bf16[16,1,64,1024]{3,2,1,0:T(8,128)(2,1)} %get-tuple-element.81), calls=%async_computation | async-start | bytes 4194304 | tf_op jit(solution)/shard_map/all_to_all | solution.py:688
  117.1 88.8 %all-to-all-start.3 = ((bf16[16,2,64,1024]{3,2,1,0:T(8,128)(2,1)}), bf16[16,2,64,1024]{3,2,1,0:T(8,128)(2,1)}, u32[]{:S(2)}, u32[]{:S(2)}) async-start(bf16[16,2,64,1024]{3,2,1,0:T(8,128)(2,1)} %bitcast.59), calls=%async_computation.3 | async-start | bytes 8388608 | tf_op jit(solution)/shard_map/all_to_all | solution.py:688
  205.9 220.3 %all-to-all-start.1 = ((bf16[16,2,64,1024]{3,2,1,0:T(8,128)(2,1)}), bf16[16,2,64,1024]{3,2,1,0:T(8,128)(2,1)}, u32[]{:S(2)}, u32[]{:S(2)}) async-start(bf16[16,2,64,1024]{3,2,1,0:T(8,128)(2,1)} %bitcast.57), calls=%async_computation.1 | async-start | bytes 8388608 | tf_op jit(solution)/shard_map/all_to_all | solution.py:688
  249.4 93.7 %collective-permute-start.1 = (bf16[4,4096,128]{2,1,0:T(8,128)(2,1)}, bf16[4,4096,128]{2,1,0:T(8,128)(2,1)S(1)}, u32[]{:S(2)}, u32[]{:S(2)}) collective-permute-start(bf16[4,4096,128]{2,1,0:T(8,128)(2,1)} %get-tuple-element.89), channel_id=1, source_target_pairs={{0,1},{1,0},{2,3},{3,2},{4,5},{5,4},{6,7},{7,6},{8,9},{9,8},{10,11... | collective-permute-start | bytes 12582920 | tf_op jit(solution)/shard_map/ppermute | solution.py:692
  256.9 108.0 %collective-permute-start.2 = (bf16[4,1024,128]{2,1,0:T(8,128)(2,1)}, bf16[4,1024,128]{2,1,0:T(8,128)(2,1)S(1)}, u32[]{:S(2)}, u32[]{:S(2)}) collective-permute-start(bf16[4,1024,128]{2,1,0:T(8,128)(2,1)} %get-tuple-element.94), channel_id=1, source_target_pairs={{0,1},{1,0},{2,3},{3,2},{4,5},{5,4},{6,7},{7,6},{8,9},{9,8},{10,11... | collective-permute-start | bytes 3145736 | tf_op jit(solution)/shard_map/ppermute | solution.py:692
  426.2 98.7 %all-to-all-start.5 = ((bf16[16,2,64,1024]{3,2,1,0:T(8,128)(2,1)}), bf16[16,2,64,1024]{3,2,1,0:T(8,128)(2,1)}, u32[]{:S(2)}, u32[]{:S(2)}) async-start(bf16[16,2,64,1024]{3,2,1,0:T(8,128)(2,1)} %get-tuple-element.110), calls=%async_computation.5 | async-start | bytes 8388608 | tf_op jit(solution)/shard_map/all_to_all | solution.py:688
  524.9 98.8 %all-to-all-start.4 = ((bf16[16,2,64,1024]{3,2,1,0:T(8,128)(2,1)}), bf16[16,2,64,1024]{3,2,1,0:T(8,128)(2,1)}, u32[]{:S(2)}, u32[]{:S(2)}) async-start(bf16[16,2,64,1024]{3,2,1,0:T(8,128)(2,1)} %get-tuple-element.106), calls=%async_computation.4 | async-start | bytes 8388608 | tf_op jit(solution)/shard_map/all_to_all | solution.py:688
  623.7 164.7 %all-to-all-start.7 = ((bf16[16,2,64,1024]{3,2,1,0:T(8,128)(2,1)}), bf16[16,2,64,1024]{3,2,1,0:T(8,128)(2,1)}, u32[]{:S(2)}, u32[]{:S(2)}) async-start(bf16[16,2,64,1024]{3,2,1,0:T(8,128)(2,1)} %get-tuple-element.145), calls=%async_computation.9 | async-start | bytes 8388608 | tf_op jit(solution)/shard_map/all_to_all | solution.py:688
  629.3 225.0 %reduce-scatter.5.cloned.1.call-start = ((), (), s32[]{:S(2)}) async-start(), calls=%async_computation.14 | async-start | bytes 1179648 | tf_op jit(solution)/shard_map/reduce_scatter | solution.py:800
  635.5 26.2 %collective-permute-start.5 = (bf16[4,1024,128]{2,1,0:T(8,128)(2,1)}, bf16[4,1024,128]{2,1,0:T(8,128)(2,1)S(1)}, u32[]{:S(2)}, u32[]{:S(2)}) collective-permute-start(bf16[4,1024,128]{2,1,0:T(8,128)(2,1)} %get-tuple-element.109), channel_id=1, source_target_pairs={{0,1},{1,0},{2,3},{3,2},{4,5},{5,4},{6,7},{7,6},{8,9},{9,8},{10,11... | collective-permute-start | bytes 3145736 | tf_op jit(solution)/shard_map/ppermute | solution.py:692
  637.1 52.2 %collective-permute-start.10 = (bf16[4,1024,128]{2,1,0:T(8,128)(2,1)}, bf16[4,1024,128]{2,1,0:T(8,128)(2,1)S(1)}, u32[]{:S(2)}, u32[]{:S(2)}) collective-permute-start(bf16[4,1024,128]{2,1,0:T(8,128)(2,1)} %get-tuple-element.125), channel_id=1, source_target_pairs={{0,1},{1,0},{2,3},{3,2},{4,5},{5,4},{6,7},{7,6},{8,9},{9,8},{10,11... | collective-permute-start | bytes 3145736 | tf_op jit(solution)/shard_map/ppermute | solution.py:692
  637.6 69.2 %collective-permute-start.9 = (bf16[4,1024,128]{2,1,0:T(8,128)(2,1)}, bf16[4,1024,128]{2,1,0:T(8,128)(2,1)S(1)}, u32[]{:S(2)}, u32[]{:S(2)}) collective-permute-start(bf16[4,1024,128]{2,1,0:T(8,128)(2,1)} %get-tuple-element.123), channel_id=1, source_target_pairs={{0,1},{1,0},{2,3},{3,2},{4,5},{5,4},{6,7},{7,6},{8,9},{9,8},{10,11... | collective-permute-start | bytes 3145736 | tf_op jit(solution)/shard_map/ppermute | solution.py:692
  639.1 90.1 %collective-permute-start.8 = (bf16[4,1024,128]{2,1,0:T(8,128)(2,1)}, bf16[4,1024,128]{2,1,0:T(8,128)(2,1)S(1)}, u32[]{:S(2)}, u32[]{:S(2)}) collective-permute-start(bf16[4,1024,128]{2,1,0:T(8,128)(2,1)} %get-tuple-element.121), channel_id=1, source_target_pairs={{0,1},{1,0},{2,3},{3,2},{4,5},{5,4},{6,7},{7,6},{8,9},{9,8},{10,11... | collective-permute-start | bytes 3145736 | tf_op jit(solution)/shard_map/ppermute | solution.py:692
  687.2 64.5 %collective-permute-start.7 = (bf16[4,1024,128]{2,1,0:T(8,128)(2,1)}, bf16[4,1024,128]{2,1,0:T(8,128)(2,1)S(1)}, u32[]{:S(2)}, u32[]{:S(2)}) collective-permute-start(bf16[4,1024,128]{2,1,0:T(8,128)(2,1)} %get-tuple-element.118), channel_id=1, source_target_pairs={{0,1},{1,0},{2,3},{3,2},{4,5},{5,4},{6,7},{7,6},{8,9},{9,8},{10,11... | collective-permute-start | bytes 3145736 | tf_op jit(solution)/shard_map/ppermute | solution.py:692
  688.8 84.8 %collective-permute-start.12 = (bf16[4,1024,128]{2,1,0:T(8,128)(2,1)}, bf16[4,1024,128]{2,1,0:T(8,128)(2,1)S(1)}, u32[]{:S(2)}, u32[]{:S(2)}) collective-permute-start(bf16[4,1024,128]{2,1,0:T(8,128)(2,1)} %get-tuple-element.136), channel_id=1, source_target_pairs={{0,1},{1,0},{2,3},{3,2},{4,5},{5,4},{6,7},{7,6},{8,9},{9,8},{10,11... | collective-permute-start | bytes 3145736 | tf_op jit(solution)/shard_map/ppermute | solution.py:692
  792.9 49.0 %all-to-all-start.8 = ((bf16[16,1,64,1024]{3,2,1,0:T(8,128)(2,1)}), bf16[16,1,64,1024]{3,2,1,0:T(8,128)(2,1)S(1)}, u32[]{:S(2)}, u32[]{:S(2)}) async-start(bf16[16,1,64,1024]{3,2,1,0:T(8,128)(2,1)} %bitcast.62), calls=%async_computation.10 | async-start | bytes 4194304 | tf_op jit(solution)/shard_map/all_to_all | solution.py:688
  798.6 156.9 %reduce-scatter.3.cloned.1.call-start = ((), (), s32[]{:S(2)}) async-start(), calls=%async_computation.12 | async-start | bytes 4718592 | tf_op jit(solution)/shard_map/reduce_scatter | solution.py:800
  843.2 112.4 %all-to-all-start.6 = ((bf16[16,2,64,1024]{3,2,1,0:T(8,128)(2,1)}), bf16[16,2,64,1024]{3,2,1,0:T(8,128)(2,1)}, u32[]{:S(2)}, u32[]{:S(2)}) async-start(bf16[16,2,64,1024]{3,2,1,0:T(8,128)(2,1)} %get-tuple-element.141), calls=%async_computation.7 | async-start | bytes 8388608 | tf_op jit(solution)/shard_map/all_to_all | solution.py:688
  854.2 132.6 %all-gather.5.cloned.1.call-start = ((), (), s32[]{:S(2)}) async-start(), calls=%async_computation.15 | async-start | bytes 1179648 | tf_op jit(solution)/shard_map/all_gather | solution.py:806
  854.3 99.5 %collective-permute-start.14 = (bf16[256,256]{1,0:T(8,128)(2,1)}, bf16[256,256]{1,0:T(8,128)(2,1)S(1)}, u32[]{:S(2)}, u32[]{:S(2)}) collective-permute-start(bf16[256,256]{1,0:T(8,128)(2,1)} %reduce-scatter.5.cloned.1.call-done), channel_id=1, source_target_pairs={{0,16},{2,18},{4,20},{6,22},{8,24},{10,26},{12,28},{14,30},{16,0},... | collective-permute-start | bytes 393224 | tf_op jit(solution)/shard_map/ppermute | solution.py:803
  955.4 85.8 %all-gather.3.cloned.1.call-start = ((), (), s32[]{:S(2)}) async-start(), calls=%async_computation.13 | async-start | bytes 4718592 | tf_op jit(solution)/shard_map/all_gather | solution.py:806
  955.5 25.7 %collective-permute-start.11 = (bf16[1024,256]{1,0:T(8,128)(2,1)}, bf16[1024,256]{1,0:T(8,128)(2,1)S(1)}, u32[]{:S(2)}, u32[]{:S(2)}) collective-permute-start(bf16[1024,256]{1,0:T(8,128)(2,1)} %reduce-scatter.3.cloned.1.call-done), channel_id=1, source_target_pairs={{0,16},{2,18},{4,20},{6,22},{8,24},{10,26},{12,28},{14,30},{16,0},... | collective-permute-start | bytes 1572872 | tf_op jit(solution)/shard_map/ppermute | solution.py:803
  982.1 66.4 %all-to-all-start.9 = ((bf16[16,1,64,1024]{3,2,1,0:T(8,128)(2,1)}), bf16[16,1,64,1024]{3,2,1,0:T(8,128)(2,1)S(1)}, u32[]{:S(2)}, u32[]{:S(2)}) async-start(bf16[16,1,64,1024]{3,2,1,0:T(8,128)(2,1)} %bitcast.61), calls=%async_computation.11 | async-start | bytes 4194304 | tf_op jit(solution)/shard_map/all_to_all | solution.py:688
  (25 other events, 261.6 us)
Sparse Core Ops, SparseCore 0:
  788.5 41.7 reduce-scatter.4
  832.5 89.7 reduce-scatter.2
  955.5 29.9 all-gather.4
  987.6 53.5 all-gather.2
